TPU v7x, 32 devices: a whole 2x2x4 slice. The times are simulated.
32 devices in a mesh: wide: 8 (over z, y), narrow: 4 (over x, core).
Axes of the slice: x: 2, y: 2, z: 4, core: 2. Of those that a mesh axis runs over, the one named last changes fastest.
Arguments:
- inputs: bfloat16 [16384, 1024], P(('wide', 'narrow')), may hold values from -6 to 6
- segment_ids: int32 [16384], P(('wide', 'narrow')), may hold values from -1 to 7, as said below
- cotangent: bfloat16 [16384, 1024], P(('wide', 'narrow')), may hold values from -6 to 6
- ln1_gain: bfloat16 [1024], P(('wide', 'narrow')), may hold values from 0.5 to 1.5
- ln1_shift: bfloat16 [1024], P(('wide', 'narrow')), may hold values from -3 to 3
- w_qkv: bfloat16 [1024, 3072], P(('wide', 'narrow')), may hold values from -0.1875 to 0.1875
- query_bias: bfloat16 [1024], P(('wide', 'narrow')), may hold values from -3 to 3
- value_bias: bfloat16 [1024], P(('wide', 'narrow')), may hold values from -3 to 3
- w_out: bfloat16 [1024, 1024], P(('wide', 'narrow')), may hold values from -1.5 to 1.5
- out_bias: bfloat16 [1024], P(('wide', 'narrow')), may hold values from -3 to 3
- ln2_gain: bfloat16 [1024], P(('wide', 'narrow')), may hold values from 0.5 to 1.5
- ln2_shift: bfloat16 [1024], P(('wide', 'narrow')), may hold values from -3 to 3
- w_in: bfloat16 [1024, 4096], P(('wide', 'narrow')), may hold values from -0.1875 to 0.1875
- in_bias: bfloat16 [4096], P(('wide', 'narrow')), may hold values from -3 to 3
- w_down: bfloat16 [4096, 1024], P(('wide', 'narrow')), may hold values from -0.125 to 0.125
- down_bias: bfloat16 [1024], P(('wide', 'narrow')), may hold values from -3 to 3
Outputs:
- layer_out: float32 [16384, 1024], P(('wide', 'narrow'))
- grad_input: float32 [16384, 1024], P(('wide', 'narrow'))
- grad_ln1_gain: float32 [1024], P(('wide', 'narrow'))
- grad_ln1_shift: float32 [1024], P(('wide', 'narrow'))
- grad_w_qkv: float32 [1024, 3072], P(('wide', 'narrow'))
- grad_query_bias: float32 [1024], P(('wide', 'narrow'))
- grad_value_bias: float32 [1024], P(('wide', 'narrow'))
- grad_w_out: float32 [1024, 1024], P(('wide', 'narrow'))
- grad_out_bias: float32 [1024], P(('wide', 'narrow'))
- grad_ln2_gain: float32 [1024], P(('wide', 'narrow'))
- grad_ln2_shift: float32 [1024], P(('wide', 'narrow'))
- grad_w_in: float32 [1024, 4096], P(('wide', 'narrow'))
- grad_in_bias: float32 [4096], P(('wide', 'narrow'))
- grad_w_down: float32 [4096, 1024], P(('wide', 'narrow'))
- grad_down_bias: float32 [1024], P(('wide', 'narrow'))
Inputs may be any that keep to these rules, and one draw needn't show every extreme that they name: `segment_ids`: within each sequence of 512 slots the live slots come first, with ids 0 to 7 that start at 0 and never fall, every id present; the last 1 to 64 slots are padding with id -1.
All inputs are finite; a program needn't handle non-finite values.
Results may differ from a plain program's by a relative error of at most 0.012.
Values may be sent and summed in bfloat16 or wider, within the bound.
A program may use at most 192 MiB of HBM per device.

v0:
```python
import jax
import jax.numpy as jnp
from jax import lax
from jax.sharding import PartitionSpec as P

HD = 64


EPS = 1e-05
ROOT_HALF = 0.7071067811865476
INV_ROOT_TAU = 0.3989422804014327
NEG_FILL = -1000000000.0


def normalize(values, gain, shift):
    average = jnp.mean(values, -1, keepdims=True)
    centred = values - average
    inverse = lax.rsqrt(jnp.mean(centred * centred, -1, keepdims=True) + EPS)
    normed = centred * inverse
    return (normed * gain + shift, normed, inverse)


def normalize_back(grad_norm, normed, inverse, gain):
    scaled = grad_norm * gain
    return inverse * (
        scaled
        - jnp.mean(scaled, -1, keepdims=True)
        - normed * jnp.mean(scaled * normed, -1, keepdims=True)
    )


def gelu_value(pre_act):
    return 0.5 * pre_act * (1.0 + lax.erf(pre_act * ROOT_HALF))


def gelu_slope(pre_act):
    return (
        0.5 * (1.0 + lax.erf(pre_act * ROOT_HALF))
        + pre_act * jnp.exp(-0.5 * pre_act * pre_act) * INV_ROOT_TAU
    )


def gather_forward(shards):
    return (
        lax.all_gather(shards[0], ("wide", "narrow"), axis=0, tiled=True),
        lax.all_gather(shards[1], ("wide", "narrow"), axis=0, tiled=True),
        lax.all_gather(shards[2], ("wide", "narrow"), axis=0, tiled=True),
        lax.all_gather(shards[3], ("wide", "narrow"), axis=0, tiled=True),
        lax.all_gather(shards[4], ("wide", "narrow"), axis=0, tiled=True),
        lax.all_gather(shards[5], ("wide", "narrow"), axis=0, tiled=True),
        lax.all_gather(shards[6], ("wide", "narrow"), axis=0, tiled=True),
        lax.all_gather(shards[7], ("wide", "narrow"), axis=0, tiled=True),
        lax.all_gather(shards[8], ("wide", "narrow"), axis=0, tiled=True),
        lax.all_gather(shards[9], ("wide", "narrow"), axis=0, tiled=True),
        lax.all_gather(shards[10], ("wide", "narrow"), axis=0, tiled=True),
        lax.all_gather(shards[11], ("wide", "narrow"), axis=0, tiled=True),
        lax.all_gather(shards[12], ("wide", "narrow"), axis=0, tiled=True),
    )


def gather_backward(shards):
    return (
        lax.all_gather(shards[0], ("wide", "narrow"), axis=0, tiled=True),
        lax.all_gather(shards[1], ("wide", "narrow"), axis=0, tiled=True),
        lax.all_gather(shards[2], ("wide", "narrow"), axis=0, tiled=True),
        lax.all_gather(shards[3], ("wide", "narrow"), axis=0, tiled=True),
        lax.all_gather(shards[4], ("wide", "narrow"), axis=0, tiled=True),
        lax.all_gather(shards[5], ("wide", "narrow"), axis=0, tiled=True),
        lax.all_gather(shards[6], ("wide", "narrow"), axis=0, tiled=True),
        lax.all_gather(shards[7], ("wide", "narrow"), axis=0, tiled=True),
        lax.all_gather(shards[8], ("wide", "narrow"), axis=0, tiled=True),
        lax.all_gather(shards[9], ("wide", "narrow"), axis=0, tiled=True),
        lax.all_gather(shards[10], ("wide", "narrow"), axis=0, tiled=True),
        lax.all_gather(shards[11], ("wide", "narrow"), axis=0, tiled=True),
        lax.all_gather(shards[12], ("wide", "narrow"), axis=0, tiled=True),
    )


def reduce_grads(grads):
    return (
        lax.psum_scatter(grads[0], ("wide", "narrow"), scatter_dimension=0, tiled=True),
        lax.psum_scatter(grads[1], ("wide", "narrow"), scatter_dimension=0, tiled=True),
        lax.psum_scatter(grads[2], ("wide", "narrow"), scatter_dimension=0, tiled=True),
        lax.psum_scatter(grads[3], ("wide", "narrow"), scatter_dimension=0, tiled=True),
        lax.psum_scatter(grads[4], ("wide", "narrow"), scatter_dimension=0, tiled=True),
        lax.psum_scatter(grads[5], ("wide", "narrow"), scatter_dimension=0, tiled=True),
        lax.psum_scatter(grads[6], ("wide", "narrow"), scatter_dimension=0, tiled=True),
        lax.psum_scatter(grads[7], ("wide", "narrow"), scatter_dimension=0, tiled=True),
        lax.psum_scatter(grads[8], ("wide", "narrow"), scatter_dimension=0, tiled=True),
        lax.psum_scatter(grads[9], ("wide", "narrow"), scatter_dimension=0, tiled=True),
        lax.psum_scatter(grads[10], ("wide", "narrow"), scatter_dimension=0, tiled=True),
        lax.psum_scatter(grads[11], ("wide", "narrow"), scatter_dimension=0, tiled=True),
        lax.psum_scatter(grads[12], ("wide", "narrow"), scatter_dimension=0, tiled=True),
    )


def head_block(triple_b, offset, group_width, d_model):
    length = triple_b.shape[0]
    queries = triple_b[:, offset : offset + group_width].reshape(length, group_width // HD, HD)
    key_rows = triple_b[:, d_model + offset : d_model + offset + group_width].reshape(
        length, group_width // HD, HD
    )
    values = triple_b[:, 2 * d_model + offset : 2 * d_model + offset + group_width].reshape(
        length, group_width // HD, HD
    )
    return (queries, key_rows, values)


def block_scores(queries, key_rows, allowed):
    scores = jnp.einsum(
        "qhd,khd->hqk", queries, key_rows, preferred_element_type=jnp.float32
    ) * HD ** (-0.5)
    return jnp.where(allowed[None], scores, NEG_FILL)


def attend(triple_b, allowed, d_model):
    length = triple_b.shape[0]
    group_width = 4 * HD
    pieces = []
    log_totals = []
    for offset in range(0, d_model, group_width):
        queries, key_rows, values = head_block(triple_b, offset, group_width, d_model)
        scores = block_scores(queries, key_rows, allowed)
        highest = jnp.max(scores, -1, keepdims=True)
        exponent = jnp.exp(scores - highest)
        row_total = jnp.sum(exponent, -1, keepdims=True)
        probs_low = (exponent / row_total).astype(jnp.bfloat16)
        mixed = jnp.einsum("hqk,khd->qhd", probs_low, values, preferred_element_type=jnp.float32)
        pieces.append(mixed.reshape(length, group_width))
        log_totals.append(highest + jnp.log(row_total))
    return (jnp.concatenate(pieces, 1), log_totals)


def attend_back(triple_b, grad_att_b, allowed, log_totals, d_model):
    length = triple_b.shape[0]
    group_width = 4 * HD
    query_parts = []
    key_parts = []
    value_parts = []
    for index, offset in enumerate(range(0, d_model, group_width)):
        queries, key_rows, values = head_block(triple_b, offset, group_width, d_model)
        scores = block_scores(queries, key_rows, allowed)
        attn_probs = jnp.exp(scores - log_totals[index])
        probs_low = attn_probs.astype(jnp.bfloat16)
        grad_heads = grad_att_b[:, offset : offset + group_width].reshape(
            length, group_width // HD, HD
        )
        grad_probs = jnp.einsum(
            "qhd,khd->hqk", grad_heads, values, preferred_element_type=jnp.float32
        )
        inner_sum = jnp.sum(attn_probs * grad_probs, -1, keepdims=True)
        grad_scores = (attn_probs * (grad_probs - inner_sum)).astype(jnp.bfloat16)
        grad_query = jnp.einsum(
            "hqk,khd->qhd", grad_scores, key_rows, preferred_element_type=jnp.float32
        ) * HD ** (-0.5)
        grad_key = jnp.einsum(
            "hqk,qhd->khd", grad_scores, queries, preferred_element_type=jnp.float32
        ) * HD ** (-0.5)
        grad_value = jnp.einsum(
            "hqk,qhd->khd", probs_low, grad_heads, preferred_element_type=jnp.float32
        )
        query_parts.append(grad_query.reshape(length, group_width))
        key_parts.append(grad_key.reshape(length, group_width))
        value_parts.append(grad_value.reshape(length, group_width))
    return jnp.concatenate(query_parts + key_parts + value_parts, 1).astype(jnp.bfloat16)


def local(
    inputs,
    segment_ids,
    cotangent,
    ln1_gain,
    ln1_shift,
    w_qkv,
    query_bias,
    value_bias,
    w_out,
    out_bias,
    ln2_gain,
    ln2_shift,
    w_in,
    in_bias,
    w_down,
    down_bias,
):
    shards = (
        ln1_gain,
        ln1_shift,
        w_qkv,
        query_bias,
        value_bias,
        w_out,
        out_bias,
        ln2_gain,
        ln2_shift,
        w_in,
        in_bias,
        w_down,
        down_bias,
    )
    fwd_weights = gather_forward(shards)
    (
        gain_one,
        shift_one,
        qkv_full,
        qbias_full,
        vbias_full,
        outw_full,
        outb_full,
        gain_two,
        shift_two,
        inw_full,
        inb_full,
        downw_full,
        downb_full,
    ) = fwd_weights
    d_model = inputs.shape[1]
    length = inputs.shape[0]
    tokens = inputs.astype(jnp.float32)
    position = jnp.arange(length, dtype=jnp.int32)
    allowed = (segment_ids[:, None] == segment_ids[None, :]) & (segment_ids[:, None] >= 0) | (
        position[:, None] == position[None, :]
    )
    normed_out, normed_one, inverse_one = normalize(
        tokens, gain_one.astype(jnp.float32), shift_one.astype(jnp.float32)
    )
    norm_one = normed_out.astype(jnp.bfloat16)
    shifts = jnp.concatenate(
        [
            qbias_full.astype(jnp.float32),
            jnp.zeros((d_model,), jnp.float32),
            vbias_full.astype(jnp.float32),
        ]
    )
    triple_b = (jnp.dot(norm_one, qkv_full, preferred_element_type=jnp.float32) + shifts).astype(
        jnp.bfloat16
    )
    attended_f, log_totals = attend(triple_b, allowed, d_model)
    attended = attended_f.astype(jnp.bfloat16)
    middle = (
        tokens
        + jnp.dot(attended, outw_full, preferred_element_type=jnp.float32)
        + outb_full.astype(jnp.float32)
    )
    normed_out_two, normed_two, inverse_two = normalize(
        middle, gain_two.astype(jnp.float32), shift_two.astype(jnp.float32)
    )
    norm_two = normed_out_two.astype(jnp.bfloat16)
    pre_act = jnp.dot(norm_two, inw_full, preferred_element_type=jnp.float32) + inb_full.astype(
        jnp.float32
    )
    hidden = gelu_value(pre_act).astype(jnp.bfloat16)
    layer_out = (
        middle
        + jnp.dot(hidden, downw_full, preferred_element_type=jnp.float32)
        + downb_full.astype(jnp.float32)
    )
    back_weights = gather_backward(shards)
    (
        gain_one_b,
        shift_one_b,
        qkv_back,
        qbias_back,
        vbias_back,
        outw_back,
        outb_back,
        gain_two_b,
        shift_two_b,
        inw_back,
        inb_back,
        downw_back,
        downb_back,
    ) = back_weights
    grad_top = cotangent.astype(jnp.float32)
    grad_w_down = jnp.einsum("sf,sd->fd", hidden, cotangent, preferred_element_type=jnp.float32)
    grad_down_bias = jnp.sum(grad_top, 0)
    grad_hidden = jnp.einsum("sd,fd->sf", cotangent, downw_back, preferred_element_type=jnp.float32)
    grad_pre = (grad_hidden * gelu_slope(pre_act)).astype(jnp.bfloat16)
    grad_w_in = jnp.einsum("sd,sf->df", norm_two, grad_pre, preferred_element_type=jnp.float32)
    grad_in_bias = jnp.sum(grad_pre.astype(jnp.float32), 0)
    grad_norm_two = jnp.einsum("sf,df->sd", grad_pre, inw_back, preferred_element_type=jnp.float32)
    grad_ln2_gain = jnp.sum(grad_norm_two * normed_two, 0)
    grad_ln2_shift = jnp.sum(grad_norm_two, 0)
    grad_middle = grad_top + normalize_back(
        grad_norm_two, normed_two, inverse_two, gain_two_b.astype(jnp.float32)
    )
    grad_mixed = grad_middle.astype(jnp.bfloat16)
    grad_w_out = jnp.einsum("sd,se->de", attended, grad_mixed, preferred_element_type=jnp.float32)
    grad_out_bias = jnp.sum(grad_mixed.astype(jnp.float32), 0)
    grad_attended = jnp.einsum(
        "se,de->sd", grad_mixed, outw_back, preferred_element_type=jnp.float32
    ).astype(jnp.bfloat16)
    grad_triple = attend_back(triple_b, grad_attended, allowed, log_totals, d_model)
    grad_w_qkv = jnp.einsum("sd,st->dt", norm_one, grad_triple, preferred_element_type=jnp.float32)
    grad_query_bias = jnp.sum(grad_triple[:, :d_model].astype(jnp.float32), 0)
    grad_value_bias = jnp.sum(grad_triple[:, 2 * d_model :].astype(jnp.float32), 0)
    grad_norm_one = jnp.einsum(
        "st,dt->sd", grad_triple, qkv_back, preferred_element_type=jnp.float32
    )
    grad_ln1_gain = jnp.sum(grad_norm_one * normed_one, 0)
    grad_ln1_shift = jnp.sum(grad_norm_one, 0)
    grad_input = grad_middle + normalize_back(
        grad_norm_one, normed_one, inverse_one, gain_one_b.astype(jnp.float32)
    )
    owned = reduce_grads(
        (
            grad_ln1_gain,
            grad_ln1_shift,
            grad_w_qkv,
            grad_query_bias,
            grad_value_bias,
            grad_w_out,
            grad_out_bias,
            grad_ln2_gain,
            grad_ln2_shift,
            grad_w_in,
            grad_in_bias,
            grad_w_down,
            grad_down_bias,
        )
    )
    return (
        layer_out,
        grad_input,
        owned[0],
        owned[1],
        owned[2],
        owned[3],
        owned[4],
        owned[5],
        owned[6],
        owned[7],
        owned[8],
        owned[9],
        owned[10],
        owned[11],
        owned[12],
    )


def solution(mesh):
    return jax.shard_map(
        local,
        mesh=mesh,
        in_specs=(
            P(("wide", "narrow"), None),
            P(("wide", "narrow")),
            P(("wide", "narrow"), None),
            P(("wide", "narrow")),
            P(("wide", "narrow")),
            P(("wide", "narrow"), None),
            P(("wide", "narrow")),
            P(("wide", "narrow")),
            P(("wide", "narrow"), None),
            P(("wide", "narrow")),
            P(("wide", "narrow")),
            P(("wide", "narrow")),
            P(("wide", "narrow"), None),
            P(("wide", "narrow")),
            P(("wide", "narrow"), None),
            P(("wide", "narrow")),
        ),
        out_specs=(
            P(("wide", "narrow"), None),
            P(("wide", "narrow"), None),
            P(("wide", "narrow")),
            P(("wide", "narrow")),
            P(("wide", "narrow"), None),
            P(("wide", "narrow")),
            P(("wide", "narrow")),
            P(("wide", "narrow"), None),
            P(("wide", "narrow")),
            P(("wide", "narrow")),
            P(("wide", "narrow")),
            P(("wide", "narrow"), None),
            P(("wide", "narrow")),
            P(("wide", "narrow"), None),
            P(("wide", "narrow")),
        ),
        check_vma=False,
    )
```

profile of v0, /device:TPU:0, one launch (start us, length us, event | category | flops | bytes accessed | tf_op | source)
XLA Modules:
  0.0 1002.9 jit_solution(12122718759421481779)
XLA Ops:
  16.7 42.4 %all-reduce.18 = (bf16[1024]{0:T(1024)(128)(2,1)S(1)}, bf16[1024]{0:T(1024)(128)(2,1)S(1)}, bf16[1024]{0:T(1024)(128)(2,1)S(1)}, bf16[1024]{0:T(1024)(128)(2,1)S...) all-reduce(bf16[1024]{0:T(1024)(128)(2,1)S(1)} %dynamic-update-slic, ...), channel_id=1, replica_groups=mesh['wide'=8,'narrow'=4] {'wide','narrow'}, use_global_device_ids=true, to_apply=%add.4 | all-reduce | flops 8192 | bytes 32768
  59.2 41.1 %all-gather = bf16[32,1,128]{2,1,0:T(2,128)(2,1)S(1)} all-gather(bf16[1,1,128]{2,1,0:T(2,128)(2,1)} %bitcast.176), channel_id=1, replica_groups=mesh['wide'=8,'narrow'=4] {'wide','narrow'}, dimensions={0}, use_global_device_ids=true | all-gather | bytes 8448 | tf_op jit(solution)/shard_map/all_gather | solution.py:55
  101.8 1.6 fusion.27
  105.2 6.9 add_convert_fusion
  121.2 1.9 copy.111
  129.8 1.6 fusion.68
  136.0 5.2 all-gather.8.cloned.1.call-done
  141.2 3.3 fusion.86
  144.9 75.5 %all-gather.10.cloned.1.call-done = bf16[1024,4096]{1,0:T(8,128)(2,1)} async-done(((bf16[32,4096]{1,0:T(8,128)(2,1)}), bf16[1024,4096]{1,0:T(8,128)(2,1)}) %all-gather.10.cloned.1.call-update) | async-done | bytes 8388624 | tf_op jit(solution)/shard_map/all_gather | solution.py:54
  220.4 11.0 %multiply_convert_fusion = (bf16[512,4096]{1,0:T(8,128)(2,1)}, f32[512,4096]{1,0:T(8,128)}) fusion(f32[4096]{0:T(1024)S(1)} %bitcast.174, bf16[1024,4096]{1,0:T(8,128)(2,1)} %all-gather.10.cloned.1.call-done, f32[512,1024]{1,0:T(8,128)S(1)} %get-tuple-element.68, f32[1024]{0:T(1024)S(1)} %convert_element_type.119, f32[1024]{0:T(1024)S(1)} %convert_element_type.118, ...), kind=kOutput, calls=%fused_computation.8 | convolution fusion | flops 4310171648 | bytes 23097344 | tf_op jit(solution)/shard_map/dot_general | solution.py:249
  231.4 67.8 %all-gather.12.cloned.1.call-done = bf16[4096,1024]{1,0:T(8,128)(2,1)} async-done(((bf16[128,1024]{1,0:T(8,128)(2,1)}), bf16[4096,1024]{1,0:T(8,128)(2,1)}) %all-gather.12.cloned.1.call-update) | async-done | bytes 8388624 | tf_op jit(solution)/shard_map/all_gather | solution.py:56
  299.2 11.1 %convert_reduce_fusion = (f32[4096]{0:T(1024)S(1)}, bf16[512,4096]{1,0:T(8,128)(2,1)S(1)}) fusion(f32[512,4096]{1,0:T(8,128)} %get-tuple-element.70, f32[4096]{0:T(1024)S(1)} %bitcast.175, bf16[512,1024]{1,0:T(8,128)(2,1)} %param.18, bf16[4096,1024]{1,0:T(8,128)(2,1)} %all-gather.12.cloned.1.call-done), kind=kOutput, calls=%fused_computation.7 | convolution fusion | flops 4322226176 | bytes 22052864 | tf_op jit(solution)/shard_map/sd,fd->sf/dot_general | solution.py:277
  310.3 5.0 multiply_reduce_fusion.4
  317.7 3.3 fusion.70
  321.0 2.9 convolution_convert_fusion
  325.2 3.3 multiply_reduce_fusion.3
  331.0 1.8 copy.133
  332.8 1.8 copy.131
  334.6 1.8 copy.129
  337.4 3.5 multiply_reduce_fusion.2
  358.4 1.7 copy-done.48
  360.1 6.9 fusion.75
  368.5 10.4 %fusion.78 = f32[1024,4096]{1,0:T(8,128)} fusion(bf16[512,4096]{1,0:T(8,128)(2,1)} %copy-done.57, f32[512,1024]{1,0:T(8,128)S(1)} %copy-done.11, f32[1024]{0:T(1024)S(1)} %convert_element_type.119, f32[1024]{0:T(1024)S(1)} %convert_element_type.118, f32[512]{0:T(512)S(1)} %add_rsqrt_fusion, f32[512]{0:T(512)S(1)} %broadcast_multiply_fusion.4), kind=kOutput, calls=%fused_computation.146 | convolution fusion | flops 4297588736 | bytes 23080960 | tf_op jit(solution)/shard_map/sd,sf->df/dot_general | solution.py:279
  379.0 12.8 %fusion.87 = f32[4096,1024]{1,0:T(8,128)} fusion(bf16[512,4096]{1,0:T(8,128)(2,1)} %get-tuple-element.69, bf16[512,1024]{1,0:T(8,128)(2,1)} %param.18), kind=kOutput, calls=%fused_computation.155 | convolution fusion | flops 4294967296 | bytes 22020096 | tf_op jit(solution)/shard_map/sf,sd->fd/dot_general | solution.py:275
  395.3 9.1 fusion.26
  404.4 40.5 %all-reduce.17 = (f32[1024]{0:T(1024)S(1)}, f32[1024]{0:T(1024)S(1)}, f32[1024]{0:T(1024)S(1)}, f32[1024]{0:T(1024)S(1)}, f32[1024]{0:T(1024)S(1)}, /*index=5*/f...) all-reduce(f32[1024]{0:T(1024)S(1)} %get-tuple-element.17, ...), channel_id=2, replica_groups=mesh['wide'=8,'narrow'=4] {'wide','narrow'}, use_global_device_ids=true, to_apply=%region_21.22.clone | all-reduce | flops 12288 | bytes 98304
  450.2 4.4 fusion.25
  454.5 8.5 add_add_fusion
  463.1 1.9 reduce-scatter.7.cloned.1.call-done
  465.0 158.2 %reduce-scatter.5.cloned.1.call-done = f32[32,3072]{1,0:T(8,128)} async-done(((f32[1024,3072]{1,0:T(8,128)}), f32[32,3072]{1,0:T(8,128)}) %reduce-scatter.5.cloned.1.call-update) | async-done | bytes 393232 | tf_op jit(solution)/shard_map/reduce_scatter | solution.py:83
  623.2 184.9 %reduce-scatter.9.cloned.1.call-done = f32[32,4096]{1,0:T(8,128)} async-done(((f32[1024,4096]{1,0:T(8,128)}), f32[32,4096]{1,0:T(8,128)}) %reduce-scatter.9.cloned.1.call-update) | async-done | bytes 524304 | tf_op jit(solution)/shard_map/reduce_scatter | solution.py:90
  808.2 187.4 %reduce-scatter.11.cloned.1.call-done = f32[128,1024]{1,0:T(8,128)} async-done(((f32[4096,1024]{1,0:T(8,128)}), f32[128,1024]{1,0:T(8,128)}) %reduce-scatter.11.cloned.1.call-update) | async-done | bytes 524304 | tf_op jit(solution)/shard_map/reduce_scatter | solution.py:92
  (241 shorter events, 67.6 us)
Async XLA Ops:
  7.2 98.0 %copy-start.9 = (bf16[512,1024]{1,0:T(8,128)(2,1)S(1)}, bf16[512,1024]{1,0:T(8,128)(2,1)}, u32[]{:S(2)}) copy-start(bf16[512,1024]{1,0:T(8,128)(2,1)} %param.16) | copy-start | bytes 3145732
  7.2 98.0 %all-gather.6.cloned.1.call-start = ((), (), s32[]{:S(2)}) async-start(), calls=%async_computation.4 | async-start | bytes 6488064 | tf_op jit(solution)/shard_map/all_gather | solution.py:47
  7.9 133.2 %all-gather.8.cloned.1.call-start = ((), (), s32[]{:S(2)}) async-start(), calls=%async_computation.5 | async-start | bytes 2162688 | tf_op jit(solution)/shard_map/all_gather | solution.py:50
  8.7 211.7 %all-gather.10.cloned.1.call-start = ((), (), s32[]{:S(2)}) async-start(), calls=%async_computation.6 | async-start | bytes 8650752 | tf_op jit(solution)/shard_map/all_gather | solution.py:54
  9.4 289.8 %all-gather.12.cloned.1.call-start = ((), (), s32[]{:S(2)}) async-start(), calls=%async_computation.7 | async-start | bytes 8650752 | tf_op jit(solution)/shard_map/all_gather | solution.py:56
  10.0 455.0 %reduce-scatter.7.cloned.1.call-start = ((), (), s32[]{:S(2)}) async-start(), calls=%async_computation.9 | async-start | bytes 4325376 | tf_op jit(solution)/shard_map/reduce_scatter | solution.py:86
  113.4 10.6 %copy-start.25 = (bf16[512,256]{0,1:T(8,128)(2,1)}, bf16[512,256]{0,1:T(8,128)(2,1)S(1)}, u32[]{:S(2)}) copy-start(bf16[512,256]{0,1:T(8,128)(2,1)S(1)} %copy.113) | copy-start | bytes 786436
  113.6 14.1 %copy-start.15 = (bf16[512,256]{0,1:T(8,128)(2,1)}, bf16[512,256]{0,1:T(8,128)(2,1)S(1)}, u32[]{:S(2)}) copy-start(bf16[512,256]{0,1:T(8,128)(2,1)S(1)} %copy.125) | copy-start | bytes 786436
  115.8 10.4 %copy-start.21 = (bf16[512,256]{0,1:T(8,128)(2,1)}, bf16[512,256]{0,1:T(8,128)(2,1)S(1)}, u32[]{:S(2)}) copy-start(bf16[512,256]{0,1:T(8,128)(2,1)S(1)} %copy.121) | copy-start | bytes 786436
  117.0 9.2 copy-start.13
  118.0 6.6 copy-start.23
  119.2 5.4 copy-start.17
  121.1 3.4 copy-start.19
  124.0 5.3 copy-start.6
  125.5 5.8 copy-start.4
  127.1 5.8 copy-start.2
  128.6 5.8 copy-start
  144.5 170.9 %copy-start.10 = (f32[512,1024]{1,0:T(8,128)}, f32[512,1024]{1,0:T(8,128)S(1)}, u32[]{:S(2)}) copy-start(f32[512,1024]{1,0:T(8,128)S(1)} %get-tuple-element.68) | copy-start | bytes 6291460
  299.2 11.1 %copy-start.50 = (bf16[1024,4096]{1,0:T(8,128)(2,1)S(1)}, bf16[1024,4096]{1,0:T(8,128)(2,1)}, u32[]{:S(2)}) copy-start(bf16[1024,4096]{1,0:T(8,128)(2,1)} %all-gather.10.cloned.1.call-done) | copy-start | bytes 25165828
  310.3 5.1 copy-start.57
  310.3 5.1 copy-start.40
  315.4 2.3 copy-start.52
  315.4 2.3 copy-start.53
  317.7 3.3 copy-start.51
  324.9 3.6 copy-start.27
  325.0 298.3 %reduce-scatter.5.cloned.1.call-start = ((), (), s32[]{:S(2)}) async-start(), calls=%async_computation.8 | async-start | bytes 12976128 | tf_op jit(solution)/shard_map/reduce_scatter | solution.py:83
  325.2 3.5 copy-start.7
  337.4 3.7 copy-start.5
  344.6 2.3 copy-start.1
  367.0 441.2 %reduce-scatter.9.cloned.1.call-start = ((), (), s32[]{:S(2)}) async-start(), calls=%async_computation.10 | async-start | bytes 17301504 | tf_op jit(solution)/shard_map/reduce_scatter | solution.py:90
  379.0 616.6 %reduce-scatter.11.cloned.1.call-start = ((), (), s32[]{:S(2)}) async-start(), calls=%async_computation.11 | async-start | bytes 17301504 | tf_op jit(solution)/shard_map/reduce_scatter | solution.py:92
  450.2 4.4 copy-start.56
  (34 other events, 52.4 us)
Sparse Core Ops, SparseCore 0:
  10.9 72.4 all-gather.5
  86.2 54.8 all-gather.7
  144.0 76.3 all-gather.9
  223.1 76.0 all-gather.11
  325.1 139.8 reduce-scatter.6
  471.5 151.7 reduce-scatter.4
  626.2 181.9 reduce-scatter.8
  811.1 184.3 reduce-scatter.10
where the time goes:
time: 1010 us; the launch traced here: 1000 us
  waiting for transfers between devices  684 us (68%)
  blocking collectives  124 us (12%)
  matrix products  119 us (12%)
  local copies, waits for them, and re-layouts  40 us (4%)
  other arithmetic  20.4 us (2%)
  between operations  15.6 us (2%)
    reduce_scatter x1, waiting for transfers between devices, reduce_grads(): lax.psum_scatter(grads[11], ('wide', 'narrow'), scatter_dimension=0, tile...  187 us
    reduce_scatter x1, waiting for transfers between devices, reduce_grads(): lax.psum_scatter(grads[9], ('wide', 'narrow'), scatter_dimension=0, tiled...  185 us
    reduce_scatter x1, waiting for transfers between devices, reduce_grads(): lax.psum_scatter(grads[2], ('wide', 'narrow'), scatter_dimension=0, tiled...  158 us
    unnamed x2, blocking collectives  82.8 us
    all_gather x1, waiting for transfers between devices, gather_forward(): lax.all_gather(shards[9], ('wide', 'narrow'), axis=0, tiled=True)  75.5 us
    all_gather x1, waiting for transfers between devices, gather_forward(): lax.all_gather(shards[11], ('wide', 'narrow'), axis=0, tiled=True)  67.8 us
    all_gather x1, blocking collectives, gather_forward(): lax.all_gather(shards[10], ('wide', 'narrow'), axis=0, tiled=True)  41.1 us
    unnamed x152, local copies, waits for them, and re-layouts  22.7 us
  transfers between devices with their start and end apart: 8, of which 7 were waited for; matrix products, arithmetic and copies ran while one was open for 14% of the time, Pallas kernels for 0%

commit v1 on v0

--- a/solution.py
+++ b/solution.py
@@ -1,6 +1,9 @@
 import jax
 import jax.numpy as jnp
 from jax import lax
+from jax.experimental import pallas as pl
+from jax.experimental.pallas import tpu as pltpu
+from jax.sharding import Mesh
 from jax.sharding import PartitionSpec as P
 
 HD = 64
@@ -338,44 +341,559 @@
     )
 
 
+MESH_ID = pl.DeviceIdType.MESH
+ROWS = 32
+
+
+def chip_index(z, y, x):
+    return (z * 2 + y) * 2 + x
+
+
+class Place:
+    def __init__(self):
+        self.z = lax.axis_index("z")
+        self.y = lax.axis_index("y")
+        self.x = lax.axis_index("x")
+        self.c = lax.axis_index("c")
+
+    def chip(self, dz=0, dy=0, dx=0):
+        z = self.z
+        if dz == 2:
+            z = lax.rem(z + 2, 4)
+        elif dz == 1:
+            z = z + 1 - 2 * lax.rem(z, 2)
+        elif dz == 3:
+            z = 3 - z
+        y = 1 - self.y if dy else self.y
+        x = 1 - self.x if dx else self.x
+        return z, y, x
+
+    def index(self, dz=0, dy=0, dx=0):
+        return chip_index(*self.chip(dz, dy, dx))
+
+    def device(self, dz=0, dy=0, dx=0):
+        z, y, x = self.chip(dz, dy, dx)
+        return {"z": z, "y": y, "x": x, "c": self.c}
+
+    def partner(self):
+        return {"z": self.z, "y": self.y, "x": self.x, "c": 1 - self.c}
+
+    def greet(self):
+        barrier = pltpu.get_barrier_semaphore()
+        peers = [self.device(dz=1), self.device(dz=2), self.device(dz=3)]
+        peers += [self.device(dy=1), self.device(dx=1), self.partner()]
+        for peer in peers:
+            pl.semaphore_signal(barrier, inc=1, device_id=peer, device_id_type=MESH_ID)
+        pl.semaphore_wait(barrier, len(peers))
+
+
+Z_AT, X_AT, Y_AT, D_AT = -1, 3, 7, 11
+
+
+class Gather:
+    def __init__(self, place, blocks, sent, came):
+        self.p, self.blocks, self.sent, self.came = place, blocks, sent, came
+        self.out = []
+
+    def copy(self, block, slot, device):
+        return pltpu.make_async_remote_copy(
+            src_ref=self.blocks.at[block],
+            dst_ref=self.blocks.at[block],
+            send_sem=self.sent.at[slot],
+            recv_sem=self.came.at[slot],
+            device_id=device,
+            device_id_type=MESH_ID,
+        )
+
+    def send(self, block, slot, device):
+        copy = self.copy(block, slot, device)
+        copy.start()
+        self.out.append(copy)
+
+    def wait(self, block, slot):
+        self.copy(block, slot, self.p.device(dx=1)).wait_recv()
+
+    def begin(self):
+        own = self.p.index()
+        for dz in (3, 2, 1):
+            self.send(own, Z_AT + dz, self.p.device(dz=dz))
+        self.send(own, X_AT, self.p.device(dx=1))
+        self.send(own, Y_AT, self.p.device(dy=1))
+
+    def along(self, dz):
+        block = self.p.index(dz=dz)
+        self.wait(block, Z_AT + dz)
+        self.send(block, X_AT + dz, self.p.device(dx=1))
+        self.send(block, Y_AT + dz, self.p.device(dy=1))
+
+    def across(self, dz):
+        if dz < 2:
+            block = self.p.index(dz=dz, dx=1)
+            self.wait(block, X_AT + dz)
+            self.send(block, D_AT + dz, self.p.device(dy=1))
+        else:
+            block = self.p.index(dz=dz, dy=1)
+            self.wait(block, Y_AT + dz)
+            self.send(block, D_AT + dz, self.p.device(dx=1))
+
+    def finish(self):
+        for dz in range(4):
+            if dz < 2:
+                self.wait(self.p.index(dz=dz, dy=1), Y_AT + dz)
+            else:
+                self.wait(self.p.index(dz=dz, dx=1), X_AT + dz)
+        for dz in range(4):
+            self.wait(self.p.index(dz=dz, dy=1, dx=1), D_AT + dz)
+
+    def drain(self):
+        for copy in self.out:
+            copy.wait_send()
+
+
+class Scatter:
+    def __init__(self, place, blocks, landed, sent, came):
+        self.p, self.blocks, self.landed = place, blocks, landed
+        self.sent, self.came = sent, came
+        self.out = []
+
+    def copy(self, block, slot, device):
+        return pltpu.make_async_remote_copy(
+            src_ref=self.blocks.at[block],
+            dst_ref=self.landed.at[slot],
+            send_sem=self.sent.at[slot],
+            recv_sem=self.came.at[slot],
+            device_id=device,
+            device_id_type=MESH_ID,
+        )
+
+    def send(self, block, slot, device):
+        copy = self.copy(block, slot, device)
+        copy.start()
+        self.out.append(copy)
+
+    def wait(self, slot):
+        self.copy(0, slot, self.p.device(dx=1)).wait_recv()
+
+    def add(self, block, slots):
+        rows = self.blocks.shape[1]
+        step = 16
+
+        def body(i, carry):
+            at = pl.ds(pl.multiple_of(i * step, step), step)
+            total = self.blocks[block, at, :].astype(jnp.float32)
+            for slot in slots:
+                total = total + self.landed[slot, at, :].astype(jnp.float32)
+            self.blocks[block, at, :] = total.astype(self.blocks.dtype)
+            return carry
+
+        lax.fori_loop(0, rows // step, body, 0)
+
+    def begin(self):
+        for dz in (1, 2, 3, 0):
+            diagonal = self.p.index(dz=dz, dy=1, dx=1)
+            if dz < 2:
+                self.send(diagonal, D_AT + dz, self.p.device(dy=1))
+                self.send(self.p.index(dz=dz, dy=1), Y_AT + dz, self.p.device(dy=1))
+            else:
+                self.send(diagonal, D_AT + dz, self.p.device(dx=1))
+                self.send(self.p.index(dz=dz, dx=1), X_AT + dz, self.p.device(dx=1))
+
+    def across(self, dz):
+        self.wait(D_AT + dz)
+        if dz < 2:
+            block = self.p.index(dz=dz, dx=1)
+            self.add(block, (D_AT + dz,))
+            self.send(block, X_AT + dz, self.p.device(dx=1))
+        else:
+            block = self.p.index(dz=dz, dy=1)
+            self.add(block, (D_AT + dz,))
+            self.send(block, Y_AT + dz, self.p.device(dy=1))
+
+    def along(self, dz):
+        self.wait(X_AT + dz)
+        self.wait(Y_AT + dz)
+        block = self.p.index(dz=dz)
+        if dz:
+            self.add(block, (X_AT + dz, Y_AT + dz))
+            self.send(block, Z_AT + dz, self.p.device(dz=dz))
+
+    def total(self, write):
+        for dz in (1, 2, 3):
+            self.wait(Z_AT + dz)
+        own = self.p.index()
+        rows = self.blocks.shape[1]
+        step = 16
+
+        def body(i, carry):
+            at = pl.ds(pl.multiple_of(i * step, step), step)
+            total = self.blocks[own, at, :].astype(jnp.float32)
+            for slot in (X_AT, Y_AT, Z_AT + 1, Z_AT + 2, Z_AT + 3):
+                total = total + self.landed[slot, at, :].astype(jnp.float32)
+            write(at, total)
+            return carry
+
+        lax.fori_loop(0, rows // step, body, 0)
+
+    def drain(self):
+        for copy in self.out:
+            copy.wait_send()
+
+
+def gather_kernel(
+    wqkv_ref, wout_ref, win_ref, wdown_ref, vec_ref, tok_ref, cot_ref,
+    qkv_o, out_o, in_o, down_o, vec_o, tok_o, cot_o,
+    w_qkv, w_nat, w_out, w_in, w_down, vec, tok, cot,
+    sent, came, pair_sent, pair_came, local,
+):
+    p = Place()
+    own = p.index()
+    c = p.c
+    mine = pl.ds(pl.multiple_of(ROWS * c, ROWS), ROWS)
+    loads = [
+        pltpu.make_async_copy(wqkv_ref.at[c], w_qkv.at[own, mine], local.at[0]),
+        pltpu.make_async_copy(win_ref.at[c], w_in.at[own, mine], local.at[1]),
+        pltpu.make_async_copy(wout_ref, w_nat.at[own], local.at[2]),
+        pltpu.make_async_copy(wdown_ref, w_down.at[own], local.at[3]),
+        pltpu.make_async_copy(vec_ref, vec.at[own], local.at[4]),
+        pltpu.make_async_copy(tok_ref, tok.at[c], local.at[5]),
+        pltpu.make_async_copy(cot_ref, cot.at[c], local.at[6]),
+    ]
+    for load in loads:
+        load.start()
+    p.greet()
+
+    def to_partner(src, dst, slot):
+        return pltpu.make_async_remote_copy(
+            src_ref=src, dst_ref=dst, send_sem=pair_sent.at[slot], recv_sem=pair_came.at[slot],
+            device_id=p.partner(), device_id_type=MESH_ID,
+        )
+
+    pair = [
+        to_partner(wqkv_ref.at[1 - c], w_qkv.at[own, mine], 0),
+        to_partner(win_ref.at[1 - c], w_in.at[own, mine], 1),
+        to_partner(tok_ref, tok.at[c], 2),
+        to_partner(cot_ref, cot.at[c], 3),
+    ]
+    for copy in pair:
+        copy.start()
+    g_qkv, g_out, g_in, g_down, g_vec = (
+        Gather(p, blocks, sent.at[i], came.at[i])
+        for i, blocks in enumerate((w_qkv, w_nat, w_in, w_down, vec))
+    )
+    loads[4].wait()
+    g_vec.begin()
+    loads[0].wait()
+    pair[0].wait_recv()
+    g_qkv.begin()
+    loads[2].wait()
+    g_out.begin()
+    loads[1].wait()
+    pair[1].wait_recv()
+    g_in.begin()
+    loads[3].wait()
+    g_down.begin()
+    for g in (g_vec, g_qkv, g_out, g_in, g_down):
+        for dz in (1, 2, 3):
+            g.along(dz)
+        for dz in (0, 1, 2, 3):
+            g.across(dz)
+    for g in (g_vec, g_qkv, g_out):
+        g.finish()
+    half = to_partner(w_nat.at[pl.ds(8 * (1 - c), 8)], w_out.at[:, mine], 4)
+    half.start()
+    keep = pltpu.make_async_copy(w_nat.at[pl.ds(8 * c, 8)], w_out.at[:, mine], local.at[7])
+    keep.start()
+    for g in (g_in, g_down):
+        g.finish()
+    loads[5].wait()
+    loads[6].wait()
+    pair[2].wait_recv()
+    pair[3].wait_recv()
+    keep.wait()
+    half.wait_recv()
+    stores = [
+        pltpu.make_async_copy(a, b, local.at[8 + i])
+        for i, (a, b) in enumerate(
+            ((w_qkv, qkv_o), (w_out, out_o), (w_in, in_o), (w_down, down_o), (vec, vec_o), (tok, tok_o), (cot, cot_o))
+        )
+    ]
+    for store in stores:
+        store.start()
+    for g in (g_vec, g_qkv, g_out, g_in, g_down):
+        g.drain()
+    for copy in pair:
+        copy.wait_send()
+    half.wait_send()
+    for store in stores:
+        store.wait()
+
+
+def gather_all(wqkv2, w_out, win2, w_down, tile, inputs, cotangent):
+    bf, f32 = jnp.bfloat16, jnp.float32
+    dq, do, di = wqkv2.shape[2], w_out.shape[1], win2.shape[2]
+    shapes = [
+        ((16, 64, dq), bf), ((8, 64, do), bf), ((16, 64, di), bf), ((16,) + w_down.shape, bf),
+        ((16, 16, 128), f32), ((2,) + inputs.shape, bf), ((2,) + cotangent.shape, bf),
+    ]
+    scratch = list(shapes)
+    scratch.insert(1, ((16, 32, do), bf))
+    return pl.pallas_call(
+        gather_kernel,
+        out_shape=[jax.ShapeDtypeStruct(s, d) for s, d in shapes],
+        in_specs=[pl.BlockSpec(memory_space=pl.ANY)] * 7,
+        out_specs=[pl.BlockSpec(memory_space=pl.ANY)] * 7,
+        scratch_shapes=[pltpu.VMEM(s, d) for s, d in scratch]
+        + [
+            pltpu.SemaphoreType.DMA((5, 15)),
+            pltpu.SemaphoreType.DMA((5, 15)),
+            pltpu.SemaphoreType.DMA((5,)),
+            pltpu.SemaphoreType.DMA((5,)),
+            pltpu.SemaphoreType.DMA((15,)),
+        ],
+        compiler_params=pltpu.CompilerParams(
+            collective_id=0, has_side_effects=True, vmem_limit_bytes=60 * 1024 * 1024
+        ),
+        name="weights_gather",
+    )(wqkv2, w_out, win2, w_down, tile, inputs, cotangent)
+
+
+def scatter_kernel(
+    qkv_ref, out_ref, in_ref, down_ref, vec_ref,
+    qkv_o, out_o, in_o, down_o, vec_o,
+    b_qkv, b_out, b_in, b_down, b_vec,
+    l_qkv, l_out, l_in, l_down, l_vec,
+    f_qkv, f_out, f_in, f_down, f_vec, n_vec,
+    sent, came, pair_sent, pair_came, local,
+):
+    p = Place()
+    c = p.c
+    mine = pl.ds(pl.multiple_of(ROWS * c, ROWS), ROWS)
+    theirs = pl.ds(pl.multiple_of(ROWS * (1 - c), ROWS), ROWS)
+    loads = [
+        pltpu.make_async_copy(a, b, local.at[i])
+        for i, (a, b) in enumerate(
+            ((down_ref, b_down), (in_ref, b_in), (out_ref.at[:, mine], b_out.at[pl.ds(8 * c, 8)]), (qkv_ref, b_qkv), (vec_ref, b_vec))
+        )
+    ]
+    for load in loads:
+        load.start()
+    p.greet()
+
+    def to_partner(src, dst, slot):
+        return pltpu.make_async_remote_copy(
+            src_ref=src, dst_ref=dst, send_sem=pair_sent.at[slot], recv_sem=pair_came.at[slot],
+            device_id=p.partner(), device_id_type=MESH_ID,
+        )
+
+    half = to_partner(out_ref.at[:, theirs], b_out.at[pl.ds(8 * c, 8)], 0)
+    half.start()
+    s_down, s_in, s_out, s_qkv, s_vec = (
+        Scatter(p, blocks, landed, sent.at[i], came.at[i])
+        for i, (blocks, landed) in enumerate(
+            ((b_down, l_down), (b_in, l_in), (b_out, l_out), (b_qkv, l_qkv), (b_vec, l_vec))
+        )
+    )
+    for i, s in enumerate((s_down, s_in, s_out, s_qkv, s_vec)):
+        loads[i].wait()
+        if i == 2:
+            half.wait_recv()
+        s.begin()
+
+    def put(ref):
+        def write(at, value):
+            ref[at, :] = value
+
+        return write
+
+    finals = {0: f_down, 1: f_in, 2: f_out, 3: f_qkv, 4: f_vec}
+    every = (s_down, s_in, s_out, s_qkv, s_vec)
+    for s in every:
+        for dz in (1, 2, 3, 0):
+            s.across(dz)
+        for dz in (1, 2, 3, 0):
+            s.along(dz)
+    for i, s in enumerate(every):
+        s.total(put(finals[i]))
+    pair = [
+        to_partner(f_qkv.at[theirs], qkv_o.at[c], 1),
+        to_partner(f_in.at[theirs], in_o.at[c], 2),
+        to_partner(f_vec, n_vec, 3),
+    ]
+    for copy in pair:
+        copy.start()
+    stores = [
+        pltpu.make_async_copy(f_down, down_o, local.at[5]),
+        pltpu.make_async_copy(f_out, out_o, local.at[6]),
+        pltpu.make_async_copy(f_qkv.at[mine], qkv_o.at[c], local.at[7]),
+        pltpu.make_async_copy(f_in.at[mine], in_o.at[c], local.at[8]),
+        pltpu.make_async_copy(f_vec, vec_o.at[0], local.at[9]),
+    ]
+    for store in stores:
+        store.start()
+    pair[2].wait_recv()
+    other = pltpu.make_async_copy(n_vec, vec_o.at[1], local.at[10])
+    other.start()
+    for s in every:
+        s.drain()
+    half.wait_send()
+    pair[0].wait()
+    pair[1].wait()
+    pair[2].wait_send()
+    for store in stores:
+        store.wait()
+    other.wait()
+
+
+def scatter_all(g_qkv, g_out, g_in, g_down, g_vec):
+    bf, f32 = jnp.bfloat16, jnp.float32
+    dq, do, di, dd = g_qkv.shape[2], g_out.shape[2], g_in.shape[2], g_down.shape[2]
+    down = g_down.shape[1]
+    outs = [((2, 32, dq), f32), ((32, do), f32), ((2, 32, di), f32), ((down, dd), f32), ((2, 16, 128), f32)]
+    blocks = [((64, dq), bf), ((32, do), bf), ((64, di), bf), ((down, dd), bf), ((16, 128), f32)]
+    return pl.pallas_call(
+        scatter_kernel,
+        out_shape=[jax.ShapeDtypeStruct(s, d) for s, d in outs],
+        in_specs=[pl.BlockSpec(memory_space=pl.ANY)] * 5,
+        out_specs=[pl.BlockSpec(memory_space=pl.ANY)] * 5,
+        scratch_shapes=[pltpu.VMEM((16,) + s, d) for s, d in blocks]
+        + [pltpu.VMEM((15,) + s, d) for s, d in blocks]
+        + [pltpu.VMEM(s, f32) for s, d in blocks]
+        + [pltpu.VMEM((16, 128), f32)]
+        + [
+            pltpu.SemaphoreType.DMA((5, 15)),
+            pltpu.SemaphoreType.DMA((5, 15)),
+            pltpu.SemaphoreType.DMA((4,)),
+            pltpu.SemaphoreType.DMA((4,)),
+            pltpu.SemaphoreType.DMA((11,)),
+        ],
+        compiler_params=pltpu.CompilerParams(
+            collective_id=1, has_side_effects=True, vmem_limit_bytes=60 * 1024 * 1024
+        ),
+        name="gradients_scatter",
+    )(g_qkv, g_out, g_in, g_down, g_vec)
+
+
+def swap(value):
+    return lax.ppermute(value, "c", [(0, 1), (1, 0)])
+
+
+def local_split(
+    inputs, segment_ids, cotangent, ln1_gain, ln1_shift, w_qkv, query_bias, value_bias, w_out, out_bias,
+    ln2_gain, ln2_shift, w_in, in_bias, w_down, down_bias,
+):
+    f32, bf = jnp.float32, jnp.bfloat16
+    c = lax.axis_index("c")
+    narrow = lax.axis_index("x") * 2 + c
+    wide = lax.axis_index("z") * 2 + lax.axis_index("y")
+    length, d_model = inputs.shape
+    rows = ln1_gain.shape[0]
+    small = jnp.stack(
+        [ln1_gain, ln1_shift, query_bias, value_bias, out_bias, ln2_gain, ln2_shift, down_bias]
+    ).astype(f32)
+    quarter = jnp.arange(4)[None, :, None] == narrow
+    tile = jnp.where(quarter, small[:, None, :], 0.0).reshape(8, 128)
+    tile = jnp.concatenate([tile, in_bias.astype(f32)[None], jnp.zeros((7, 128), f32)])
+    wqkv2 = w_qkv.reshape(rows, 3, 2, d_model // 2).transpose(2, 0, 1, 3).reshape(2, rows, -1)
+    win2 = w_in.reshape(rows, 16, 2, 128).transpose(2, 0, 1, 3).reshape(2, rows, -1)
+    qkv_f, out_f, in_f, down_f, vec_f, tok2, cot2 = gather_all(wqkv2, w_out, win2, w_down, tile, inputs, cotangent)
+    mates = swap(vec_f)
+    vecs = (vec_f + mates)[:, :8].reshape(8, 2, 8, 128).sum(1).transpose(1, 0, 2).reshape(8, d_model)
+    g1, b1, qb, vb, ob, g2, b2, db = [vecs[i] for i in range(8)]
+    inb = vec_f[:, 8].reshape(-1)
+    qkv_m = qkv_f.reshape(d_model, -1)
+    out_m = out_f.reshape(-1, d_model)
+    in_m = in_f.reshape(d_model, -1)
+    down_m = down_f.reshape(-1, d_model)
+    half = d_model // 2
+    cut = lambda v: lax.dynamic_slice(v, (c * half,), (half,))
+    seg2 = jnp.where(c == 0, jnp.stack([segment_ids, swap(segment_ids)]), jnp.stack([swap(segment_ids), segment_ids]))
+    tokens = tok2.astype(f32).reshape(2 * length, d_model)
+    position = jnp.arange(length, dtype=jnp.int32)
+    allowed = ((seg2[:, :, None] == seg2[:, None, :]) & (seg2[:, :, None] >= 0)) | (
+        position[:, None] == position[None, :]
+    )
+    n1, x1, r1 = normalize(tokens, g1, b1)
+    norm_one = n1.astype(bf)
+    shifts = jnp.concatenate([cut(qb), jnp.zeros((half,), f32), cut(vb)])
+    triple = (jnp.dot(norm_one, qkv_m, preferred_element_type=f32) + shifts).astype(bf)
+    t5 = triple.reshape(2, length, 3, half // HD, HD)
+    q, k, v = t5[:, :, 0], t5[:, :, 1], t5[:, :, 2]
+    scores = jnp.einsum("sqhd,skhd->shqk", q, k, preferred_element_type=f32) * HD ** (-0.5)
+    scores = jnp.where(allowed[:, None], scores, NEG_FILL)
+    probs = jax.nn.softmax(scores, axis=-1)
+    probs_low = probs.astype(bf)
+    attended = jnp.einsum("shqk,skhd->sqhd", probs_low, v, preferred_element_type=f32)
+    attended = attended.reshape(2 * length, half).astype(bf)
+    part = jnp.dot(attended, out_m, preferred_element_type=f32)
+    middle = tokens + part + swap(part) + ob
+    n2, x2, r2 = normalize(middle, g2, b2)
+    norm_two = n2.astype(bf)
+    pre_act = jnp.dot(norm_two, in_m, preferred_element_type=f32) + inb
+    hidden = gelu_value(pre_act).astype(bf)
+    cot = cot2.reshape(2 * length, d_model)
+    grad_down = jnp.einsum("sf,sd->fd", hidden, cot, preferred_element_type=f32).astype(bf)
+    outp = jnp.dot(hidden, down_m, preferred_element_type=f32).reshape(2, length, d_model)
+    pick = lambda a, i: lax.dynamic_index_in_dim(a, i, 0, False)
+    layer_out = pick(middle.reshape(2, length, d_model), c) + pick(outp, c) + swap(pick(outp, 1 - c)) + db
+    grad_hidden = jnp.einsum("sd,fd->sf", cot, down_m, preferred_element_type=f32)
+    grad_pre = (grad_hidden * gelu_slope(pre_act)).astype(bf)
+    grad_in = jnp.einsum("sd,sf->df", norm_two, grad_pre, preferred_element_type=f32).astype(bf)
+    grad_in_bias = jnp.sum(grad_pre.astype(f32), 0)
+    gn2 = jnp.einsum("sf,df->sd", grad_pre, in_m, preferred_element_type=f32)
+    gn2 = gn2 + swap(gn2)
+    gm = cot.astype(f32) + normalize_back(gn2, x2, r2, g2)
+    grad_mixed = gm.astype(bf)
+    grad_out = jnp.einsum("sd,se->de", attended, grad_mixed, preferred_element_type=f32).astype(bf)
+    grad_att = jnp.einsum("se,de->sd", grad_mixed, out_m, preferred_element_type=f32).astype(bf)
+    ga = grad_att.reshape(2, length, half // HD, HD)
+    gp = jnp.einsum("sqhd,skhd->shqk", ga, v, preferred_element_type=f32)
+    gs = (probs * (gp - jnp.sum(probs * gp, -1, keepdims=True))).astype(bf)
+    gq = jnp.einsum("shqk,skhd->sqhd", gs, k, preferred_element_type=f32) * HD ** (-0.5)
+    gk = jnp.einsum("shqk,sqhd->skhd", gs, q, preferred_element_type=f32) * HD ** (-0.5)
+    gv = jnp.einsum("shqk,sqhd->skhd", probs_low, ga, preferred_element_type=f32)
+    gt = jnp.stack([gq, gk, gv], 2).reshape(2 * length, 3 * half).astype(bf)
+    grad_qkv = jnp.einsum("sd,st->dt", norm_one, gt, preferred_element_type=f32).astype(bf)
+    gqb = jnp.sum(gt[:, :half].astype(f32), 0)
+    gvb = jnp.sum(gt[:, 2 * half :].astype(f32), 0)
+    gn1 = jnp.einsum("st,dt->sd", gt, qkv_m, preferred_element_type=f32).reshape(2, length, d_model)
+    gn1 = pick(gn1, c) + swap(pick(gn1, 1 - c))
+    own = lambda a: pick(a.reshape(2, length, d_model), c)
+    r1o = pick(r1.reshape(2, length, 1), c)
+    grad_input = own(gm) + normalize_back(gn1, own(x1), r1o, g1)
+    put = lambda v: lax.dynamic_update_slice(jnp.zeros((d_model,), f32), v, (c * half,))
+    sums = jnp.stack(
+        [
+            jnp.sum(gn1 * own(x1), 0), jnp.sum(gn1, 0), put(gqb), put(gvb), jnp.sum(own(grad_mixed).astype(f32), 0),
+            jnp.sum(own(gn2 * x2), 0), jnp.sum(own(gn2), 0), jnp.sum(own(cot).astype(f32), 0),
+        ]
+    )
+    gvec = jnp.repeat(sums.reshape(8, 8, 128).transpose(1, 0, 2), 2, 0)
+    gvec = jnp.concatenate([gvec, grad_in_bias.reshape(16, 1, 128), jnp.zeros((16, 7, 128), f32)], 1)
+    d_qkv, d_out, d_in, d_down, d_vec = scatter_all(
+        grad_qkv.reshape(16, 64, -1), grad_out.reshape(8, 64, -1), grad_in.reshape(16, 64, -1),
+        grad_down.reshape(16, 128, -1), gvec,
+    )
+    d_qkv = d_qkv.reshape(2, rows, 3, half).transpose(1, 2, 0, 3).reshape(rows, -1)
+    d_in = d_in.reshape(2, rows, 16, 128).transpose(1, 2, 0, 3).reshape(rows, -1)
+    eight = (d_vec[0, :8] + d_vec[1, :8]).reshape(8, 4, 32)
+    eight = lax.dynamic_index_in_dim(eight, narrow, 1, False)
+    return (
+        layer_out, grad_input, eight[0], eight[1], d_qkv, eight[2], eight[3], d_out, eight[4],
+        eight[5], eight[6], d_in, d_vec[0, 8], d_down, eight[7],
+    )
+
+
 def solution(mesh):
+    sizes = tuple(mesh.shape.values())
+    step, names = local, (("wide", "narrow"),)
+    if sizes == (8, 4):
+        mesh = Mesh(mesh.devices.reshape(4, 2, 2, 2), ("z", "y", "x", "c"))
+        step, names = local_split, (("z", "y", "x", "c"),)
+    line, plane = P(names[0]), P(names[0], None)
     return jax.shard_map(
-        local,
+        step,
         mesh=mesh,
-        in_specs=(
-            P(("wide", "narrow"), None),
-            P(("wide", "narrow")),
-            P(("wide", "narrow"), None),
-            P(("wide", "narrow")),
-            P(("wide", "narrow")),
-            P(("wide", "narrow"), None),
-            P(("wide", "narrow")),
-            P(("wide", "narrow")),
-            P(("wide", "narrow"), None),
-            P(("wide", "narrow")),
-            P(("wide", "narrow")),
-            P(("wide", "narrow")),
-            P(("wide", "narrow"), None),
-            P(("wide", "narrow")),
-            P(("wide", "narrow"), None),
-            P(("wide", "narrow")),
-        ),
-        out_specs=(
-            P(("wide", "narrow"), None),
-            P(("wide", "narrow"), None),
-            P(("wide", "narrow")),
-            P(("wide", "narrow")),
-            P(("wide", "narrow"), None),
-            P(("wide", "narrow")),
-            P(("wide", "narrow")),
-            P(("wide", "narrow"), None),
-            P(("wide", "narrow")),
-            P(("wide", "narrow")),
-            P(("wide", "narrow")),
-            P(("wide", "narrow"), None),
-            P(("wide", "narrow")),
-            P(("wide", "narrow"), None),
-            P(("wide", "narrow")),
-        ),
+        in_specs=(plane, line, plane, line, line, plane, line, line, plane, line, line, line, plane, line, plane, line),
+        out_specs=(plane, plane, line, line, plane, line, line, plane, line, line, line, plane, line, plane, line),
         check_vma=False,
     )

time: 1010 us -> 516 us (0.51)
  waiting for transfers between devices: 684 us -> 6.82 us
  Pallas kernels: 0 us -> 279 us
  blocking collectives: 124 us -> 0 us
  local copies, waits for them, and re-layouts: 40 us -> 65.6 us
  other arithmetic: 20.4 us -> 43.4 us
  between operations: 15.6 us -> 1.78 us
  matrix products: 119 us -> 108 us
    reduce_scatter x4 -> x0, waiting for transfers between devices: 532 us -> none  [the longest x1 187 us: reduce_grads(): lax.psum_scatter(grads[11], ('wide', 'narrow'), scatter_dimension=0, tile...]
    pallas_call x0 -> x2, Pallas kernels: none -> 279 us  [the longest x1 150 us: scatter_all(): pl.pallas_call(scatter_kernel, out_shape=[jax.ShapeDtypeStruct(s, d) for...]
    all_gather x4 -> x0, waiting for transfers between devices: 149 us -> none  [the longest x1 75.5 us: gather_forward(): lax.all_gather(shards[9], ('wide', 'narrow'), axis=0, tiled=True)]
    unnamed x2 -> x0, blocking collectives: 82.8 us -> none
    all_gather x1 -> x0, blocking collectives: 41.1 us -> none  [gather_forward(): lax.all_gather(shards[10], ('wide', 'narrow'), axis=0, tiled=True)]
    dot_general x36 -> x17, matrix products: 119 us -> 97 us  [the longest x1 13.6 us: local_split(): gp = jnp.einsum('sqhd,skhd->shqk', ga, v, preferred_element_type=f32)]
    reshape x0 -> x12, local copies, waits for them, and re-layouts: none -> 19.1 us  [the longest x1 8.85 us: local_split(): t5 = triple.reshape(2, length, 3, half // HD, HD)]
    sub x0 -> x1, matrix products: none -> 11.3 us  [local_split(): probs = jax.nn.softmax(scores, axis=-1)]
  transfers between devices with their start and end apart: 8 -> 6, of which waited for: 7 -> 1; matrix products, arithmetic and copies ran while one was open for 14% -> 21% of each run, Pallas kernels for 0% -> 26%
where the time goes in v1:
time: 516 us; the launch traced here: 507 us
  Pallas kernels  279 us (54%)
  matrix products  108 us (21%)
  local copies, waits for them, and re-layouts  65.6 us (13%)
  other arithmetic  43.4 us (8%)
  waiting for transfers between devices  6.82 us (1%)
    pallas_call x1, Pallas kernels, scatter_all(): pl.pallas_call(scatter_kernel, out_shape=[jax.ShapeDtypeStruct(s, d) for...  150 us
    pallas_call x1, Pallas kernels, gather_all(): pl.pallas_call(gather_kernel, out_shape=[jax.ShapeDtypeStruct(s, d) for s...  130 us
    unnamed x98, local copies, waits for them, and re-layouts  29.7 us
    dot_general x1, matrix products, local_split(): gp = jnp.einsum('sqhd,skhd->shqk', ga, v, preferred_element_type=f32)  13.6 us
    sub x1, matrix products, local_split(): probs = jax.nn.softmax(scores, axis=-1)  11.3 us
  transfers between devices with their start and end apart: 6, of which 1 were waited for; matrix products, arithmetic and copies ran while one was open for 21% of the time, Pallas kernels for 26%

profile of v1, /device:TPU:0, one launch (start us, length us, event | category | flops | bytes accessed | tf_op | source)
XLA Modules:
  0.0 506.8 jit_solution(1389497532615218710)
XLA Ops:
  8.3 129.6 %weights_gather.1 = (bf16[16,64,1536]{2,1,0:T(8,128)(2,1)}, bf16[8,64,1024]{2,1,0:T(8,128)(2,1)}, bf16[16,64,2048]{2,1,0:T(8,128)(2,1)}, bf16[16,128,1024]{2,1,0...) custom-call(bf16[2,32,1536]{2,1,0:T(8,128)(2,1)} %reshape.511.wqkv_ref, ...), custom_call_target="tpu_custom_call" | custom-call | tf_op jit(solution)/shard_map/weights_gather/pallas_call | solution.py:640
  144.6 2.9 subtract_multiply_fusion.1
  148.9 4.8 add_convert_fusion
  153.7 8.8 %reshape.541 = bf16[2,512,3,8,64]{4,3,2,1,0:T(8,128)(2,1)} reshape(bf16[1024,1536]{1,0:T(8,128)(2,1)} %add_convert_fusion) | data formatting | bytes 6291456 | tf_op jit(solution)/shard_map/reshape | solution.py:819
  162.5 5.7 %fusion.65 = (bf16[2,512,1,8,64]{4,3,2,1,0:T(8,128)(2,1)}, bf16[2,512,1,8,64]{4,3,2,1,0:T(8,128)(2,1)}, bf16[2,512,1,8,64]{4,3,2,1,0:T(8,128)(2,1)}) fusion(bf16[2,512,3,8,64]{4,3,2,1,0:T(8,128)(2,1)} %reshape.541), kind=kLoop, calls=%fused_computation.130 | loop fusion | bytes 6291456 | tf_op jit(solution)/shard_map/slice | solution.py:820
  168.2 3.3 copy.91
  171.6 3.3 copy.90
  174.8 2.5 copy.92
  177.4 11.3 %fusion.67 = (f32[2,8,512]{2,1,0:T(8,128)S(1)}, f32[2,8,512,512]{2,3,1,0:T(8,128)}) fusion(pred[2,512,512]{1,2,0:T(8,128)(4,1)} %and_or_fusion, bf16[2,512,1,8,64]{1,4,3,0,2:T(8,128)(2,1)S(1)} %copy.92, bf16[2,512,1,8,64]{1,4,3,0,2:T(8,128)(2,1)} %copy.91), kind=kOutput, calls=%fused_computation.132 | convolution fusion | flops 553648640 | bytes 19431424 | tf_op jit(solution)/shard_map/sub | solution.py:823
  188.7 7.7 %fusion.32 = bf16[2,512,8,64]{1,3,2,0:T(8,128)(2,1)S(1)} fusion(bf16[2,512,1,8,64]{1,4,3,0,2:T(8,128)(2,1)} %copy.90, f32[2,8,512,512]{2,3,1,0:T(8,128)} %get-tuple-element.78, f32[2,8,512]{2,1,0:T(8,128)S(1)} %get-tuple-element.77), kind=kOutput, calls=%fused_computation.71 | convolution fusion | flops 545783808 | bytes 18907136 | tf_op jit(solution)/shard_map/shqk,skhd->sqhd/dot_general | solution.py:825
  199.5 6.8 %collective-permute-done.2 = f32[1024,1024]{1,0:T(8,128)S(1)} collective-permute-done((f32[1024,1024]{1,0:T(8,128)S(1)}, f32[1024,1024]{1,0:T(8,128)S(1)}, u32[]{:S(2)}, u32[]{:S(2)}) %collective-permute-start.2) | collective-permute-done | bytes 4194336 | tf_op jit(solution)/shard_map/ppermute | solution.py:777
  207.6 3.1 copy-done.35
  210.8 7.5 %multiply_convert_fusion.1 = (bf16[1024,2048]{1,0:T(8,128)(2,1)}, f32[1024,2048]{1,0:T(8,128)S(1)}) fusion(f32[2048]{0:T(1024)S(1)} %bitcast.269, bf16[1024,2048]{1,0:T(8,128)(2,1)S(1)} %bitcast.288, f32[1024,1024]{1,0:T(8,128)S(1)} %get-tuple-element.53, f32[1024]{0:T(1024)S(1)} %bitcast.274, f32[1024]{0:T(1024)S(1)} %bitcast.251, ...), kind=kOutput, calls=%fused_computation.14 | convolution fusion | flops 4312793088 | bytes 20996096 | tf_op jit(solution)/shard_map/dot_general | solution.py:831
  218.3 7.8 %convert_reduce_fusion = (f32[2048]{0:T(1024)S(1)}, bf16[1024,2048]{1,0:T(8,128)(2,1)S(1)}) fusion(f32[1024,2048]{1,0:T(8,128)S(1)} %get-tuple-element.80, f32[2048]{0:T(1024)S(1)} %bitcast.270, bf16[1024,1024]{1,0:T(8,128)(2,1)S(1)} %bitcast.227, bf16[2048,1024]{1,0:T(8,128)(2,1)S(1)} %bitcast.287), kind=kOutput, calls=%fused_computation.13 | convolution fusion | flops 4322228224 | bytes 18890752 | tf_op jit(solution)/shard_map/sd,fd->sf/dot_general | solution.py:838
  226.2 6.2 %fusion.78 = f32[1024,1024]{1,0:T(8,128)} fusion(bf16[1024,2048]{1,0:T(8,128)(2,1)S(1)} %get-tuple-element.84, bf16[1024,2048]{1,0:T(8,128)(2,1)S(1)} %bitcast.289), kind=kOutput, calls=%fused_computation.135 | convolution fusion | flops 4294967296 | bytes 12582912 | tf_op jit(solution)/shard_map/sf,df->sd/dot_general | solution.py:842
  232.9 8.1 %fusion.77 = f32[2,512,1024]{2,1,0:T(8,128)S(1)} fusion(bf16[2,512,2048]{2,1,0:T(8,128)(2,1)} %bitcast.292, bf16[2048,1024,1]{1,0,2:T(8,128)(2,1)} %bitcast.286), kind=kOutput, calls=%fused_computation.134 | convolution fusion | flops 4294967296 | bytes 12582912 | tf_op jit(solution)/shard_map/dot_general | solution.py:835
  242.8 2.6 copy-done.1
  245.5 6.7 %convolution_convert_fusion.2 = bf16[1024,2048]{1,0:T(8,128)(2,1)} fusion(bf16[1024,2048]{1,0:T(8,128)(2,1)S(1)} %copy-done.40, f32[1024,1024]{1,0:T(8,128)S(1)} %copy-done.1, f32[1024]{0:T(1024)S(1)} %bitcast.275, f32[1024]{0:T(1024)S(1)} %bitcast.252, f32[1024]{0:T(1024)S(1)} %add_rsqrt_fusion, f32[1024]{0:T(1024)S(1)} %broadcast_multiply_fusion.2), kind=kOutput, calls=%fused_computation.40 | convolution fusion | flops 4302307328 | bytes 12599296 | tf_op jit(solution)/shard_map/sd,sf->df/dot_general | solution.py:840
  252.1 6.2 %fusion.17 = (f32[1024,1024]{1,0:T(8,128)}, f32[1024,1024]{1,0:T(8,128)S(1)}) fusion(f32[1024,1024]{1,0:T(8,128)S(1)} %copy-done.1, f32[1024]{0:T(1024)S(1)} %add_rsqrt_fusion, f32[1024]{0:T(1024)S(1)} %broadcast_multiply_fusion.2, f32[1024,1024]{1,0:T(8,128)} %fusion.78, f32[1024,1024]{1,0:T(8,128)} %collective-permute-done.4), kind=kLoop, calls=%fused_computation.42 | loop fusion | flops 4194304 | bytes 20979712 | tf_op jit(solution)/shard_map/mul | solution.py:867
  260.2 3.1 fusion.62
  269.5 9.6 %fusion.26 = bf16[2,512,1,8,64]{1,4,3,0,2:T(8,128)(2,1)} fusion(bf16[2,512,8,64]{1,3,2,0:T(8,128)(2,1)S(1)} %copy.71, f32[2,8,512,512]{2,3,1,0:T(8,128)} %get-tuple-element.78, f32[2,8,512]{2,1,0:T(8,128)S(1)} %get-tuple-element.77), kind=kOutput, calls=%fused_computation.67 | convolution fusion | flops 545259520 | bytes 18907136 | tf_op jit(solution)/shard_map/shqk,sqhd->skhd/dot_general | solution.py:853
  279.0 13.6 %multiply_reduce_fusion = (f32[2,8,512]{2,1,0:T(8,128)S(1)}, f32[2,8,512,512]{2,3,1,0:T(8,128)}) fusion(f32[2,8,512,512]{2,3,1,0:T(8,128)} %get-tuple-element.78, f32[2,8,512]{2,1,0:T(8,128)S(1)} %get-tuple-element.77, bf16[2,512,8,64]{1,3,2,0:T(8,128)(2,1)} %copy-done.21, bf16[2,512,1,8,64]{1,4,3,0,2:T(8,128)(2,1)} %copy.90), kind=kOutput, calls=%fused_computation.2 | convolution fusion | flops 549445632 | bytes 35717120 | tf_op jit(solution)/shard_map/sqhd,skhd->shqk/dot_general | solution.py:849
  293.5 8.1 %multiply_convert_fusion = bf16[2,8,512,512]{2,3,1,0:T(8,128)(2,1)S(1)} fusion(f32[2,8,512,512]{2,3,1,0:T(8,128)} %get-tuple-element.82, f32[2,8,512]{2,1,0:T(8,128)S(1)} %get-tuple-element.81, f32[2,8,512,512]{2,3,1,0:T(8,128)S(1)} %bitcast.219, f32[2,8,512]{2,1,0:T(8,128)S(1)} %get-tuple-element.77), kind=kLoop, calls=%fused_computation.1 | loop fusion | flops 16777216 | bytes 42008576 | tf_op jit(solution)/shard_map/convert_element_type | solution.py:850
  301.7 3.9 multiply_bitcast_fusion
  309.3 3.5 fusion.79
  314.4 6.5 %convolution_convert_fusion.1 = bf16[2048,1024]{1,0:T(8,128)(2,1)} fusion(bf16[1024,2048]{1,0:T(8,128)(2,1)S(1)} %copy-done.38, bf16[1024,1024]{1,0:T(8,128)(2,1)S(1)} %bitcast.228), kind=kOutput, calls=%fused_computation.39 | convolution fusion | flops 4297064448 | bytes 10485760 | tf_op jit(solution)/shard_map/sf,sd->fd/dot_general | solution.py:834
  320.9 3.6 fusion.23
  324.5 3.3 copy.78
  333.6 4.9 convolution_convert_fusion
  339.8 2.6 fusion.22
  343.2 149.5 %gradients_scatter.1 = (f32[2,32,1536]{2,1,0:T(8,128)}, f32[32,1024]{1,0:T(8,128)}, f32[2,32,2048]{2,1,0:T(8,128)}, f32[128,1024]{1,0:T(8,128)}, f32[2,16,128]{2,1,0:T(8,128)}) custom-call(bf16[16,64,1536]{2,1,0:T(8,128)(2,1)} %bitcast.234, bf16[8,64,1024]{2,1,0:T(8,128)(2,1)} %bitcast.239, bf16[16,64,2048]{2,1,0:T(8,128)(2,1)} %bitcast.230, ...), custom_call_target="tpu_custom_call" | custom-call | tf_op jit(solution)/shard_map/gradients_scatter/pallas_call | solution.py:753
  500.2 4.1 fusion.21
  (177 shorter events, 53.8 us)
Async XLA Ops:
  0.6 141.8 %collective-permute-start.1 = (s32[512]{0:T(512)}, s32[512]{0:T(512)S(1)}, u32[]{:S(2)}, u32[]{:S(2)}) collective-permute-start(s32[512]{0:T(512)} %param.17), channel_id=1, source_target_pairs={{0,1},{1,0},{2,3},{3,2},{4,5},{5,4},{6,7},{7,6},{8,9},{9,8},{10,11... | collective-permute-start | bytes 6152 | tf_op jit(solution)/shard_map/ppermute | solution.py:777
  6.1 136.3 %copy-start.33 = (s32[512]{0:T(512)S(1)}, s32[512]{0:T(512)}, u32[]{:S(2)}) copy-start(s32[512]{0:T(512)} %param.17) | copy-start | bytes 6148
  137.8 5.9 %copy-start.29 = (f32[16,16,128]{2,1,0:T(8,128)S(1)}, f32[16,16,128]{2,1,0:T(8,128)}, u32[]{:S(2)}) copy-start(f32[16,16,128]{2,1,0:T(8,128)} %get-tuple-element.28) | copy-start | bytes 393220
  137.9 6.7 %copy-start.5 = (bf16[2,512,1024]{2,1,0:T(8,128)(2,1)S(1)}, bf16[2,512,1024]{2,1,0:T(8,128)(2,1)}, u32[]{:S(2)}) copy-start(bf16[2,512,1024]{2,1,0:T(8,128)(2,1)} %get-tuple-element.27) | copy-start | bytes 6291460
  137.9 5.9 %collective-permute-start = (f32[16,16,128]{2,1,0:T(8,128)}, f32[16,16,128]{2,1,0:T(8,128)S(1)}, u32[]{:S(2)}, u32[]{:S(2)}) collective-permute-start(f32[16,16,128]{2,1,0:T(8,128)} %get-tuple-element.28), channel_id=1, source_target_pairs={{0,1},{1,0},{2,3},{3,2},{4,5},{5,4},{6,7},{7,6},{8,9},{9,8},{10,11... | collective-permute-start | bytes 393224 | tf_op jit(solution)/shard_map/ppermute | solution.py:777
  144.6 4.3 copy-start.36
  177.4 11.3 %copy-start.8 = (bf16[2,512,1,8,64]{1,4,3,0,2:T(8,128)(2,1)}, bf16[2,512,1,8,64]{1,4,3,0,2:T(8,128)(2,1)S(1)}, u32[]{:S(2)}) copy-start(bf16[2,512,1,8,64]{1,4,3,0,2:T(8,128)(2,1)S(1)} %copy.92) | copy-start | bytes 3145732
  197.7 9.3 %copy-start.10 = (bf16[64,8,2,512]{3,1,2,0:T(8,128)(2,1)}, bf16[64,8,2,512]{3,1,2,0:T(8,128)(2,1)S(1)}, u32[]{:S(2)}) copy-start(bf16[64,8,2,512]{3,1,2,0:T(8,128)(2,1)S(1)} %copy.93) | copy-start | bytes 3145732
  199.0 7.2 %collective-permute-start.2 = (f32[1024,1024]{1,0:T(8,128)S(1)}, f32[1024,1024]{1,0:T(8,128)S(1)}, u32[]{:S(2)}, u32[]{:S(2)}) collective-permute-start(f32[1024,1024]{1,0:T(8,128)S(1)} %fusion.76), channel_id=1, source_target_pairs={{0,1},{1,0},{2,3},{3,2},{4,5},{5,4},{6,7},{7,6},{8,9},{9,8},{10,11... | collective-permute-start | bytes 12582920 | tf_op jit(solution)/shard_map/ppermute | solution.py:777
  207.0 11.2 %copy-start = (f32[1024,1024]{1,0:T(8,128)}, f32[1024,1024]{1,0:T(8,128)S(1)}, u32[]{:S(2)}) copy-start(f32[1024,1024]{1,0:T(8,128)S(1)} %get-tuple-element.53) | copy-start | bytes 12582916
  210.8 7.5 %copy-start.12 = (bf16[2,512,1024]{2,1,0:T(8,128)(2,1)S(1)}, bf16[2,512,1024]{2,1,0:T(8,128)(2,1)}, u32[]{:S(2)}) copy-start(bf16[2,512,1024]{2,1,0:T(8,128)(2,1)} %get-tuple-element.33) | copy-start | bytes 6291460
  210.8 7.5 %copy-start.34 = (bf16[16,128,1024]{2,1,0:T(8,128)(2,1)S(1)}, bf16[16,128,1024]{2,1,0:T(8,128)(2,1)}, u32[]{:S(2)}) copy-start(bf16[16,128,1024]{2,1,0:T(8,128)(2,1)} %get-tuple-element.32) | copy-start | bytes 12582916
  226.1 6.2 %copy-start.39 = (bf16[1024,2048]{1,0:T(8,128)(2,1)}, bf16[1024,2048]{1,0:T(8,128)(2,1)S(1)}, u32[]{:S(2)}) copy-start(bf16[1024,2048]{1,0:T(8,128)(2,1)S(1)} %get-tuple-element.84) | copy-start | bytes 12582916
  232.4 19.8 %collective-permute-start.4 = (f32[1024,1024]{1,0:T(8,128)}, f32[1024,1024]{1,0:T(8,128)}, u32[]{:S(2)}, u32[]{:S(2)}) collective-permute-start(f32[1024,1024]{1,0:T(8,128)} %fusion.78), channel_id=1, source_target_pairs={{0,1},{1,0},{2,3},{3,2},{4,5},{5,4},{6,7},{7,6},{8,9},{9,8},{10,11... | collective-permute-start | bytes 12582920 | tf_op jit(solution)/shard_map/ppermute | solution.py:777
  232.9 9.9 %copy-start.40 = (bf16[1024,2048]{1,0:T(8,128)(2,1)S(1)}, bf16[1024,2048]{1,0:T(8,128)(2,1)}, u32[]{:S(2)}) copy-start(bf16[1024,2048]{1,0:T(8,128)(2,1)} %copy-done.39) | copy-start | bytes 12582916
  241.0 11.1 %copy-start.16 = (f32[2,512,1024]{2,1,0:T(8,128)}, f32[2,512,1024]{2,1,0:T(8,128)S(1)}, u32[]{:S(2)}) copy-start(f32[2,512,1024]{2,1,0:T(8,128)S(1)} %fusion.77) | copy-start | bytes 12582916
  241.0 4.4 copy-start.1
  242.6 78.2 %collective-permute-start.3 = (f32[512,1024]{1,0:T(8,128)}, f32[512,1024]{1,0:T(8,128)}, u32[]{:S(2)}, u32[]{:S(2)}) collective-permute-start(f32[512,1024]{1,0:T(8,128)} %dynamic-slice_bitcast_fusion.1), channel_id=1, source_target_pairs={{0,1},{1,0},{2,3},{3,2},{4,5},{5,4},{6,7},{7,6},{8,9},{9,8},{10,11... | collective-permute-start | bytes 6291464 | tf_op jit(solution)/shard_map/ppermute | solution.py:777
  260.2 4.4 copy-start.24
  269.5 23.2 %slice-start = ((s8[16777216]{0:T(1024)(128)(4,1)}), s8[4194304]{0:T(1024)(128)(4,1)S(1)}, s32[]{:S(2)}) async-start(s8[16777216]{0:T(1024)(128)(4,1)} %bitcast.218), calls=%async_computation | async-start | bytes 8388608
  269.5 23.2 %slice-start.1 = ((s8[16777216]{0:T(1024)(128)(4,1)}), s8[4194304]{0:T(1024)(128)(4,1)S(1)}, s32[]{:S(2)}) async-start(s8[16777216]{0:T(1024)(128)(4,1)} %bitcast.218), calls=%async_computation.1 | async-start | bytes 8388608
  279.0 13.7 %slice-start.2 = ((s8[16777216]{0:T(1024)(128)(4,1)}), s8[4194304]{0:T(1024)(128)(4,1)S(1)}, s32[]{:S(2)}) async-start(s8[16777216]{0:T(1024)(128)(4,1)} %bitcast.218), calls=%async_computation.2 | async-start | bytes 8388608
  279.0 14.5 %slice-start.3 = ((s8[16777216]{0:T(1024)(128)(4,1)}), s8[4194304]{0:T(1024)(128)(4,1)S(1)}, s32[]{:S(2)}) async-start(s8[16777216]{0:T(1024)(128)(4,1)} %bitcast.218), calls=%async_computation.3 | async-start | bytes 8388608
  313.1 7.8 %copy-start.2 = (f32[1024,1024]{1,0:T(8,128)S(1)}, f32[1024,1024]{1,0:T(8,128)}, u32[]{:S(2)}) copy-start(f32[1024,1024]{1,0:T(8,128)} %copy-done) | copy-start | bytes 12582916
  313.1 7.8 %copy-start.17 = (f32[2,512,1024]{2,1,0:T(8,128)S(1)}, f32[2,512,1024]{2,1,0:T(8,128)}, u32[]{:S(2)}) copy-start(f32[2,512,1024]{2,1,0:T(8,128)} %copy-done.16) | copy-start | bytes 12582916
  313.1 7.8 %copy-start.30 = (f32[1,8,128]{2,0,1:T(1,128)S(1)}, f32[1,8,128]{2,0,1:T(1,128)}, u32[]{:S(2)}) copy-start(f32[1,8,128]{2,0,1:T(1,128)} %get-tuple-element.61) | copy-start | bytes 12292
  313.1 25.4 %collective-permute-start.5 = (f32[512,1024]{1,0:T(8,128)S(1)}, f32[512,1024]{1,0:T(8,128)S(1)}, u32[]{:S(2)}, u32[]{:S(2)}) collective-permute-start(f32[512,1024]{1,0:T(8,128)S(1)} %dynamic-slice_bitcast_fusion), channel_id=1, source_target_pairs={{0,1},{1,0},{2,3},{3,2},{4,5},{5,4},{6,7},{7,6},{8,9},{9,8},{10,11... | collective-permute-start | bytes 6291464 | tf_op jit(solution)/shard_map/ppermute | solution.py:777
  324.5 5.0 copy-start.7
  333.6 6.2 %copy-start.6 = (f32[2,512,1024]{2,1,0:T(8,128)S(1)}, f32[2,512,1024]{2,1,0:T(8,128)}, u32[]{:S(2)}) copy-start(f32[2,512,1024]{2,1,0:T(8,128)} %get-tuple-element.59) | copy-start | bytes 12582916
  333.6 6.2 %copy-start.28 = (f32[1,8,128]{2,0,1:T(1,128)S(1)}, f32[1,8,128]{2,0,1:T(1,128)}, u32[]{:S(2)}) copy-start(f32[1,8,128]{2,0,1:T(1,128)} %copy-done.27) | copy-start | bytes 12292
  500.2 4.7 copy-start.26
  500.2 5.3 %copy-start.25 = (f32[128,1024]{1,0:T(8,128)S(1)}, f32[128,1024]{1,0:T(8,128)}, u32[]{:S(2)}) copy-start(f32[128,1024]{1,0:T(8,128)} %get-tuple-element.117) | copy-start | bytes 1572868
  (19 other events, 40.9 us)

commit v2 on v1

--- a/solution.py
+++ b/solution.py
@@ -1,3 +1,5 @@
+import functools
+
 import jax
 import jax.numpy as jnp
 from jax import lax
@@ -343,10 +345,7 @@
 
 MESH_ID = pl.DeviceIdType.MESH
 ROWS = 32
-
-
-def chip_index(z, y, x):
-    return (z * 2 + y) * 2 + x
+BF, F32 = jnp.bfloat16, jnp.float32
 
 
 class Place:
@@ -369,7 +368,8 @@
         return z, y, x
 
     def index(self, dz=0, dy=0, dx=0):
-        return chip_index(*self.chip(dz, dy, dx))
+        z, y, x = self.chip(dz, dy, dx)
+        return (z * 2 + y) * 2 + x
 
     def device(self, dz=0, dy=0, dx=0):
         z, y, x = self.chip(dz, dy, dx)
@@ -387,274 +387,512 @@
         pl.semaphore_wait(barrier, len(peers))
 
 
+class Pair:
+    def __init__(self, place, sent, came):
+        self.p, self.sent, self.came = place, sent, came
+
+    def copy(self, src, dst, slot):
+        return pltpu.make_async_remote_copy(
+            src_ref=src,
+            dst_ref=dst,
+            send_sem=self.sent.at[slot],
+            recv_sem=self.came.at[slot],
+            device_id=self.p.partner(),
+            device_id_type=MESH_ID,
+        )
+
+
 Z_AT, X_AT, Y_AT, D_AT = -1, 3, 7, 11
 
 
 class Gather:
     def __init__(self, place, blocks, sent, came):
         self.p, self.blocks, self.sent, self.came = place, blocks, sent, came
-        self.out = []
-
-    def copy(self, block, slot, device):
+        self.left = []
+
+    def copy(self, block, slot, to):
+        at = self.p.index(**block)
         return pltpu.make_async_remote_copy(
-            src_ref=self.blocks.at[block],
-            dst_ref=self.blocks.at[block],
+            src_ref=self.blocks.at[at],
+            dst_ref=self.blocks.at[at],
             send_sem=self.sent.at[slot],
             recv_sem=self.came.at[slot],
-            device_id=device,
+            device_id=self.p.device(**to),
             device_id_type=MESH_ID,
         )
 
-    def send(self, block, slot, device):
-        copy = self.copy(block, slot, device)
-        copy.start()
-        self.out.append(copy)
+    def send(self, block, slot, to):
+        self.copy(block, slot, to).start()
+        self.left.append((block, slot, to))
 
     def wait(self, block, slot):
-        self.copy(block, slot, self.p.device(dx=1)).wait_recv()
+        self.copy(block, slot, dict(dx=1)).wait_recv()
 
     def begin(self):
-        own = self.p.index()
         for dz in (3, 2, 1):
-            self.send(own, Z_AT + dz, self.p.device(dz=dz))
-        self.send(own, X_AT, self.p.device(dx=1))
-        self.send(own, Y_AT, self.p.device(dy=1))
+            self.send({}, Z_AT + dz, dict(dz=dz))
+        self.send({}, X_AT, dict(dx=1))
+        self.send({}, Y_AT, dict(dy=1))
 
     def along(self, dz):
-        block = self.p.index(dz=dz)
-        self.wait(block, Z_AT + dz)
-        self.send(block, X_AT + dz, self.p.device(dx=1))
-        self.send(block, Y_AT + dz, self.p.device(dy=1))
+        self.wait(dict(dz=dz), Z_AT + dz)
+        self.send(dict(dz=dz), X_AT + dz, dict(dx=1))
+        self.send(dict(dz=dz), Y_AT + dz, dict(dy=1))
 
     def across(self, dz):
         if dz < 2:
-            block = self.p.index(dz=dz, dx=1)
-            self.wait(block, X_AT + dz)
-            self.send(block, D_AT + dz, self.p.device(dy=1))
+            self.wait(dict(dz=dz, dx=1), X_AT + dz)
+            self.send(dict(dz=dz, dx=1), D_AT + dz, dict(dy=1))
         else:
-            block = self.p.index(dz=dz, dy=1)
-            self.wait(block, Y_AT + dz)
-            self.send(block, D_AT + dz, self.p.device(dx=1))
+            self.wait(dict(dz=dz, dy=1), Y_AT + dz)
+            self.send(dict(dz=dz, dy=1), D_AT + dz, dict(dx=1))
 
     def finish(self):
         for dz in range(4):
             if dz < 2:
-                self.wait(self.p.index(dz=dz, dy=1), Y_AT + dz)
+                self.wait(dict(dz=dz, dy=1), Y_AT + dz)
             else:
-                self.wait(self.p.index(dz=dz, dx=1), X_AT + dz)
+                self.wait(dict(dz=dz, dx=1), X_AT + dz)
         for dz in range(4):
-            self.wait(self.p.index(dz=dz, dy=1, dx=1), D_AT + dz)
+            self.wait(dict(dz=dz, dy=1, dx=1), D_AT + dz)
+
+    def steps(self):
+        for dz in (1, 2, 3):
+            yield functools.partial(self.along, dz)
+        for dz in (0, 1, 2, 3):
+            yield functools.partial(self.across, dz)
 
     def drain(self):
-        for copy in self.out:
-            copy.wait_send()
+        for block, slot, to in self.left:
+            self.copy(block, slot, to).wait_send()
 
 
 class Scatter:
     def __init__(self, place, blocks, landed, sent, came):
         self.p, self.blocks, self.landed = place, blocks, landed
         self.sent, self.came = sent, came
-        self.out = []
-
-    def copy(self, block, slot, device):
+        self.left = []
+
+    def copy(self, block, slot, to):
         return pltpu.make_async_remote_copy(
-            src_ref=self.blocks.at[block],
+            src_ref=self.blocks.at[self.p.index(**block)],
             dst_ref=self.landed.at[slot],
             send_sem=self.sent.at[slot],
             recv_sem=self.came.at[slot],
-            device_id=device,
+            device_id=self.p.device(**to),
             device_id_type=MESH_ID,
         )
 
-    def send(self, block, slot, device):
-        copy = self.copy(block, slot, device)
-        copy.start()
-        self.out.append(copy)
+    def send(self, block, slot, to):
+        self.copy(block, slot, to).start()
+        self.left.append((block, slot, to))
 
     def wait(self, slot):
-        self.copy(0, slot, self.p.device(dx=1)).wait_recv()
-
-    def add(self, block, slots):
+        self.copy({}, slot, dict(dx=1)).wait_recv()
+
+    def add(self, at, slots, write):
         rows = self.blocks.shape[1]
         step = 16
 
         def body(i, carry):
-            at = pl.ds(pl.multiple_of(i * step, step), step)
-            total = self.blocks[block, at, :].astype(jnp.float32)
+            some = pl.ds(pl.multiple_of(i * step, step), step)
+            total = self.blocks[at, some, :].astype(F32)
             for slot in slots:
-                total = total + self.landed[slot, at, :].astype(jnp.float32)
-            self.blocks[block, at, :] = total.astype(self.blocks.dtype)
+                total = total + self.landed[slot, some, :].astype(F32)
+            write(some, total)
             return carry
 
         lax.fori_loop(0, rows // step, body, 0)
+
+    def merge(self, block, slots):
+        at = self.p.index(**block)
+
+        def write(some, total):
+            self.blocks[at, some, :] = total.astype(self.blocks.dtype)
+
+        self.add(at, slots, write)
 
     def begin(self):
         for dz in (1, 2, 3, 0):
-            diagonal = self.p.index(dz=dz, dy=1, dx=1)
             if dz < 2:
-                self.send(diagonal, D_AT + dz, self.p.device(dy=1))
-                self.send(self.p.index(dz=dz, dy=1), Y_AT + dz, self.p.device(dy=1))
+                self.send(dict(dz=dz, dy=1, dx=1), D_AT + dz, dict(dy=1))
+                self.send(dict(dz=dz, dy=1), Y_AT + dz, dict(dy=1))
             else:
-                self.send(diagonal, D_AT + dz, self.p.device(dx=1))
-                self.send(self.p.index(dz=dz, dx=1), X_AT + dz, self.p.device(dx=1))
+                self.send(dict(dz=dz, dy=1, dx=1), D_AT + dz, dict(dx=1))
+                self.send(dict(dz=dz, dx=1), X_AT + dz, dict(dx=1))
 
     def across(self, dz):
         self.wait(D_AT + dz)
         if dz < 2:
-            block = self.p.index(dz=dz, dx=1)
-            self.add(block, (D_AT + dz,))
-            self.send(block, X_AT + dz, self.p.device(dx=1))
+            self.merge(dict(dz=dz, dx=1), (D_AT + dz,))
+            self.send(dict(dz=dz, dx=1), X_AT + dz, dict(dx=1))
         else:
-            block = self.p.index(dz=dz, dy=1)
-            self.add(block, (D_AT + dz,))
-            self.send(block, Y_AT + dz, self.p.device(dy=1))
+            self.merge(dict(dz=dz, dy=1), (D_AT + dz,))
+            self.send(dict(dz=dz, dy=1), Y_AT + dz, dict(dy=1))
 
     def along(self, dz):
         self.wait(X_AT + dz)
         self.wait(Y_AT + dz)
-        block = self.p.index(dz=dz)
         if dz:
-            self.add(block, (X_AT + dz, Y_AT + dz))
-            self.send(block, Z_AT + dz, self.p.device(dz=dz))
+            self.merge(dict(dz=dz), (X_AT + dz, Y_AT + dz))
+            self.send(dict(dz=dz), Z_AT + dz, dict(dz=dz))
 
     def total(self, write):
         for dz in (1, 2, 3):
             self.wait(Z_AT + dz)
-        own = self.p.index()
-        rows = self.blocks.shape[1]
-        step = 16
-
-        def body(i, carry):
-            at = pl.ds(pl.multiple_of(i * step, step), step)
-            total = self.blocks[own, at, :].astype(jnp.float32)
-            for slot in (X_AT, Y_AT, Z_AT + 1, Z_AT + 2, Z_AT + 3):
-                total = total + self.landed[slot, at, :].astype(jnp.float32)
-            write(at, total)
+        self.add(self.p.index(), (X_AT, Y_AT, Z_AT + 1, Z_AT + 2, Z_AT + 3), write)
+
+    def steps(self):
+        for dz in (1, 2, 3, 0):
+            yield functools.partial(self.across, dz)
+        for dz in (1, 2, 3, 0):
+            yield functools.partial(self.along, dz)
+
+    def drain(self):
+        for block, slot, to in self.left:
+            self.copy(block, slot, to).wait_send()
+
+
+class Pump:
+    def __init__(self):
+        self.queue = []
+
+    def add(self, steps):
+        self.queue.extend(steps)
+
+    def take(self, count):
+        now, self.queue = self.queue[:count], self.queue[count:]
+        for step in now:
+            step()
+
+    def loop(self, trips, body, per_trip=0):
+        groups = []
+        for i in range(trips):
+            groups.append(self.queue[:per_trip])
+            self.queue = self.queue[per_trip:]
+
+        def trip(i, carry):
+            body(i)
+            for k, group in enumerate(groups):
+                if group:
+
+                    @pl.when(i == k)
+                    def _(group=group):
+                        for step in group:
+                            step()
+
             return carry
 
-        lax.fori_loop(0, rows // step, body, 0)
-
-    def drain(self):
-        for copy in self.out:
-            copy.wait_send()
-
-
-def gather_kernel(
-    wqkv_ref, wout_ref, win_ref, wdown_ref, vec_ref, tok_ref, cot_ref,
-    qkv_o, out_o, in_o, down_o, vec_o, tok_o, cot_o,
-    w_qkv, w_nat, w_out, w_in, w_down, vec, tok, cot,
+        lax.fori_loop(0, trips, trip, 0)
+
+
+NN = (((1,), (0,)), ((), ()))
+NT = (((1,), (1,)), ((), ()))
+TN = (((0,), (0,)), ((), ()))
+
+
+def mm(a, b, dims=NN):
+    return lax.dot_general(a, b, dims, preferred_element_type=F32)
+
+
+def span(i, size):
+    return pl.ds(pl.multiple_of(i * size, size), size)
+
+
+def stats(v):
+    average = jnp.mean(v, -1, keepdims=True)
+    centred = v - average
+    inverse = lax.rsqrt(jnp.mean(centred * centred, -1, keepdims=True) + EPS)
+    return centred * inverse, inverse
+
+
+def build_mask(mask, seg_col, seg_row):
+    size = mask.shape[1]
+    for s in range(2):
+
+        def body(i, carry, s=s):
+            rows = span(i, 128)
+            col = seg_col[s, rows, :][:, :1]
+            row = seg_row[s, :1, :]
+            here = lax.broadcasted_iota(jnp.int32, (128, size), 0) + i * 128
+            there = lax.broadcasted_iota(jnp.int32, (128, size), 1)
+            fine = ((col == row) & (col >= 0)) | (here == there)
+            mask[s, rows, :] = jnp.where(fine, 0.0, NEG_FILL)
+            return carry
+
+        lax.fori_loop(0, size // 128, body, 0)
+
+
+def build_vectors(vecs, hidden_shift, triple_shift, tiles, c):
+    for w in range(8):
+        vecs[0:8, 128 * w : 128 * (w + 1)] = tiles[2 * w, 0:8, :] + tiles[2 * w + 1, 0:8, :]
+    for j in range(16):
+        hidden_shift[0:1, 128 * j : 128 * (j + 1)] = tiles[j, 8:9, :]
+    half = vecs.shape[1] // 2
+    first = c == 0
+    triple_shift[0:1, 0:half] = jnp.where(first, vecs[2:3, 0:half], vecs[2:3, half:])
+    triple_shift[0:1, half : 2 * half] = jnp.zeros((1, half), F32)
+    triple_shift[0:1, 2 * half :] = jnp.where(first, vecs[3:4, 0:half], vecs[3:4, half:])
+
+
+G1, B1, QB, VB, OB, G2, B2, DB = range(8)
+
+
+def attend_pair(i, triple, mask, attended, lse):
+    length = mask.shape[1]
+    half = attended.shape[1]
+    pairs = half // 128
+    s, pair = i // pairs, lax.rem(i, pairs)
+    rows = span(s, length)
+    q = triple[rows, pl.ds(pl.multiple_of(pair * 128, 128), 128)]
+    k = triple[rows, pl.ds(pl.multiple_of(half + pair * 128, 128), 128)]
+    v = triple[rows, pl.ds(pl.multiple_of(2 * half + pair * 128, 128), 128)]
+    lane = lax.broadcasted_iota(jnp.int32, (length, 128), 1)
+    low = lane < HD
+    outs = []
+    kept = lse[s]
+    for h in range(2):
+        mine = low if h == 0 else ~low
+        scores = mm(jnp.where(mine, q, jnp.zeros_like(q)), k, NT) * HD ** (-0.5) + mask[s]
+        highest = jnp.max(scores, -1, keepdims=True)
+        exponent = jnp.exp(scores - highest)
+        total = jnp.sum(exponent, -1, keepdims=True)
+        probs = (exponent * (1.0 / total)).astype(BF)
+        outs.append(mm(probs, v))
+        kept = jnp.where(lane == pair * 2 + h, highest + jnp.log(total), kept)
+    lse[s] = kept
+    attended[rows, pl.ds(pl.multiple_of(pair * 128, 128), 128)] = jnp.where(low, outs[0], outs[1]).astype(BF)
+
+
+def forward_kernel(
+    wqkv_ref, wout_ref, win_ref, wdown_ref, tile_ref, tok_ref, cot_ref, col_ref, row_ref,
+    qkv_o, out_o, in_o, down_o, vecs_o, norm1_o, triple_o, att_o, lse_o, xhat_o, inv_o, norm2_o, slope_o, cot_o,
+    mask_o, gdown_o, layer_o,
+    w_qkv, w_nat, w_out, w_in, w_down, tiles, tile, tile_in, tok, cot, col, row, mask,
+    vecs, hshift, tshift, norm1, triple, att, lse, mid, part, part_in, last_in, norm2, xhat, inv, hidden, slope, gdown,
     sent, came, pair_sent, pair_came, local,
 ):
     p = Place()
-    own = p.index()
-    c = p.c
+    own, c = p.index(), p.c
+    length = tok.shape[1]
     mine = pl.ds(pl.multiple_of(ROWS * c, ROWS), ROWS)
+    slots = iter(range(local.shape[0]))
+
+    def load(src, dst):
+        copy = pltpu.make_async_copy(src, dst, local.at[next(slots)])
+        copy.start()
+        return copy
+
     loads = [
-        pltpu.make_async_copy(wqkv_ref.at[c], w_qkv.at[own, mine], local.at[0]),
-        pltpu.make_async_copy(win_ref.at[c], w_in.at[own, mine], local.at[1]),
-        pltpu.make_async_copy(wout_ref, w_nat.at[own], local.at[2]),
-        pltpu.make_async_copy(wdown_ref, w_down.at[own], local.at[3]),
-        pltpu.make_async_copy(vec_ref, vec.at[own], local.at[4]),
-        pltpu.make_async_copy(tok_ref, tok.at[c], local.at[5]),
-        pltpu.make_async_copy(cot_ref, cot.at[c], local.at[6]),
+        load(wqkv_ref.at[c], w_qkv.at[own, mine]),
+        load(wout_ref, w_nat.at[own]),
+        load(win_ref.at[c], w_in.at[own, mine]),
+        load(wdown_ref, w_down.at[own]),
+        load(tile_ref, tile),
+        load(tok_ref, tok.at[c]),
+        load(cot_ref, cot.at[c]),
+        load(col_ref, col.at[c]),
+        load(row_ref, row.at[c]),
     ]
-    for load in loads:
-        load.start()
     p.greet()
-
-    def to_partner(src, dst, slot):
-        return pltpu.make_async_remote_copy(
-            src_ref=src, dst_ref=dst, send_sem=pair_sent.at[slot], recv_sem=pair_came.at[slot],
-            device_id=p.partner(), device_id_type=MESH_ID,
-        )
-
-    pair = [
-        to_partner(wqkv_ref.at[1 - c], w_qkv.at[own, mine], 0),
-        to_partner(win_ref.at[1 - c], w_in.at[own, mine], 1),
-        to_partner(tok_ref, tok.at[c], 2),
-        to_partner(cot_ref, cot.at[c], 3),
+    pair = Pair(p, pair_sent, pair_came)
+    swaps = [
+        pair.copy(tile_ref, tile_in, 0),
+        pair.copy(wqkv_ref.at[1 - c], w_qkv.at[own, mine], 1),
+        pair.copy(win_ref.at[1 - c], w_in.at[own, mine], 2),
+        pair.copy(row_ref, row.at[c], 3),
+        pair.copy(col_ref, col.at[c], 4),
+        pair.copy(tok_ref, tok.at[c], 5),
+        pair.copy(cot_ref, cot.at[c], 6),
     ]
-    for copy in pair:
+    for copy in swaps:
         copy.start()
     g_qkv, g_out, g_in, g_down, g_vec = (
         Gather(p, blocks, sent.at[i], came.at[i])
-        for i, blocks in enumerate((w_qkv, w_nat, w_in, w_down, vec))
-    )
+        for i, blocks in enumerate((w_qkv, w_nat, w_in, w_down, tiles))
+    )
+    loads[0].wait()
+    swaps[1].wait_recv()
+    g_qkv.begin()
     loads[4].wait()
+    swaps[0].wait_recv()
+    tiles[own, 0:8, :] = tile[0:8, :] + tile_in[0:8, :]
+    tiles[own, 8:16, :] = tile[8:16, :]
     g_vec.begin()
-    loads[0].wait()
-    pair[0].wait_recv()
-    g_qkv.begin()
+    loads[1].wait()
+    g_out.begin()
     loads[2].wait()
-    g_out.begin()
-    loads[1].wait()
-    pair[1].wait_recv()
+    swaps[2].wait_recv()
     g_in.begin()
     loads[3].wait()
     g_down.begin()
+    pump = Pump()
     for g in (g_vec, g_qkv, g_out, g_in, g_down):
-        for dz in (1, 2, 3):
-            g.along(dz)
-        for dz in (0, 1, 2, 3):
-            g.across(dz)
-    for g in (g_vec, g_qkv, g_out):
-        g.finish()
-    half = to_partner(w_nat.at[pl.ds(8 * (1 - c), 8)], w_out.at[:, mine], 4)
+        pump.add(g.steps())
+    for i in (7, 8, 5):
+        loads[i].wait()
+    for i in (3, 4, 5):
+        swaps[i].wait_recv()
+    build_mask(mask, col, row)
+    pump.take(7)
+    g_vec.finish()
+    build_vectors(vecs, hshift, tshift, tiles, c)
+    tokens = tok.shape[0] * length
+
+    def first_norm(i):
+        rows = span(i, 128)
+        v = tok[i // 4, span(lax.rem(i, 4), 128), :].astype(F32)
+        normed, _ = stats(v)
+        norm1[rows, :] = (normed * vecs[G1 : G1 + 1, :] + vecs[B1 : B1 + 1, :]).astype(BF)
+
+    pump.loop(tokens // 128, first_norm, 0)
+    pump.take(7)
+    g_qkv.finish()
+    stores = [load(w_qkv, qkv_o), load(norm1, norm1_o), load(vecs, vecs_o), load(mask, mask_o)]
+    depth = norm1.shape[1]
+
+    def project(i):
+        cols = span(i, 256)
+        w = w_qkv[:, :, cols].reshape(depth, 256)
+        triple[:, cols] = (mm(norm1[...], w) + tshift[0:1, cols]).astype(BF)
+
+    pump.loop(triple.shape[1] // 256, project, 1)
+    stores.append(load(triple, triple_o))
+    lse[...] = jnp.zeros_like(lse)
+    pump.loop(8, functools.partial(attend_pair, triple=triple, mask=mask, attended=att, lse=lse), 1)
+    stores += [load(att, att_o), load(lse, lse_o)]
+    g_out.finish()
+    half = pair.copy(w_nat.at[pl.ds(8 * (1 - c), 8)], w_out.at[:, mine], 7)
     half.start()
-    keep = pltpu.make_async_copy(w_nat.at[pl.ds(8 * c, 8)], w_out.at[:, mine], local.at[7])
-    keep.start()
-    for g in (g_in, g_down):
-        g.finish()
-    loads[5].wait()
-    loads[6].wait()
-    pair[2].wait_recv()
-    pair[3].wait_recv()
+    keep = load(w_nat.at[pl.ds(8 * c, 8)], w_out.at[:, mine])
     keep.wait()
     half.wait_recv()
-    stores = [
-        pltpu.make_async_copy(a, b, local.at[8 + i])
-        for i, (a, b) in enumerate(
-            ((w_qkv, qkv_o), (w_out, out_o), (w_in, in_o), (w_down, down_o), (vec, vec_o), (tok, tok_o), (cot, cot_o))
-        )
-    ]
-    for store in stores:
-        store.start()
+    stores.append(load(w_out, out_o))
+
+    def send_part(i):
+        rows = span(i, 256)
+        return pair.copy(part.at[rows], part_in.at[rows], 8 + i)
+
+    def mix(i):
+        rows = span(i, 256)
+        own_part = mm(att[rows, :], w_out[...].reshape(att.shape[1], depth))
+        part[rows, :] = own_part.astype(BF)
+        send_part(i).start()
+        v = tok[i // 2, span(lax.rem(i, 2), 256), :].astype(F32)
+        mid[rows, :] = v + own_part + vecs[OB : OB + 1, :]
+
+    pump.loop(4, mix, 0)
+
+    def second_norm(i):
+        send_part(i).wait_recv()
+        rows = span(i, 256)
+        v = mid[rows, :] + part_in[rows, :].astype(F32)
+        mid[rows, :] = v
+        normed, inverse = stats(v)
+        xhat[rows, :] = normed.astype(BF)
+        inv[rows, :] = jnp.broadcast_to(inverse, (256, 128))
+        norm2[rows, :] = (normed * vecs[G2 : G2 + 1, :] + vecs[B2 : B2 + 1, :]).astype(BF)
+
+    pump.loop(4, second_norm, 0)
+    stores += [load(xhat, xhat_o), load(inv, inv_o), load(norm2, norm2_o)]
+    pump.take(max(len(pump.queue) - 7, 0))
+    g_in.finish()
+    stores.append(load(w_in, in_o))
+
+    def expand(i):
+        cols = span(i, 256)
+        w = w_in[:, :, cols].reshape(depth, 256)
+        pre = mm(norm2[...], w) + hshift[0:1, cols]
+        bell = 0.5 * (1.0 + lax.erf(pre * ROOT_HALF))
+        hidden[:, cols] = (pre * bell).astype(BF)
+        slope[:, cols] = (bell + pre * jnp.exp(-0.5 * pre * pre) * INV_ROOT_TAU).astype(BF)
+
+    loads[6].wait()
+    swaps[6].wait_recv()
+    stores.append(load(cot, cot_o))
+    pump.loop(hidden.shape[1] // 256, expand, 1)
+    stores.append(load(slope, slope_o))
+
+    def down_grad(i):
+        cols = span(i, 256)
+        grad = mm(hidden[:, cols], cot[...].reshape(tokens, depth), TN).astype(BF)
+        gdown[pl.ds(pl.multiple_of(2 * i, 2), 2)] = grad.reshape(2, 128, depth)
+
+    pump.loop(hidden.shape[1] // 256, down_grad, 1)
+    stores.append(load(gdown, gdown_o))
+    pump.take(len(pump.queue))
+    g_down.finish()
+    stores.append(load(w_down, down_o))
+    for i in range(4):
+        send_part(i).wait_send()
+    yours, ours = span(1 - c, length), span(c, length)
+    units = hidden.shape[1]
+
+    def theirs(i):
+        cols = span(i, 256)
+        w = w_down[:, :, cols].reshape(units, 256)
+        part[yours, cols] = mm(hidden[yours, :], w).astype(BF)
+
+    lax.fori_loop(0, depth // 256, lambda i, carry: (theirs(i), carry)[1], 0)
+    last = pair.copy(part.at[yours], last_in, 12)
+    last.start()
+
+    def contract(i):
+        cols = span(i, 256)
+        w = w_down[:, :, cols].reshape(units, 256)
+        mid[ours, cols] = mid[ours, cols] + mm(hidden[ours, :], w) + vecs[DB : DB + 1, cols]
+
+    lax.fori_loop(0, depth // 256, lambda i, carry: (contract(i), carry)[1], 0)
+    last.wait_recv()
+    mid[ours, :] = mid[ours, :] + last_in[...].astype(F32)
+    stores.append(load(mid.at[ours], layer_o))
     for g in (g_vec, g_qkv, g_out, g_in, g_down):
         g.drain()
-    for copy in pair:
+    for copy in swaps:
         copy.wait_send()
     half.wait_send()
+    last.wait_send()
     for store in stores:
         store.wait()
 
 
-def gather_all(wqkv2, w_out, win2, w_down, tile, inputs, cotangent):
-    bf, f32 = jnp.bfloat16, jnp.float32
+def forward_all(wqkv2, w_out, win2, w_down, tile, inputs, cotangent, col, row):
     dq, do, di = wqkv2.shape[2], w_out.shape[1], win2.shape[2]
-    shapes = [
-        ((16, 64, dq), bf), ((8, 64, do), bf), ((16, 64, di), bf), ((16,) + w_down.shape, bf),
-        ((16, 16, 128), f32), ((2,) + inputs.shape, bf), ((2,) + cotangent.shape, bf),
+    length, depth = inputs.shape
+    tokens = 2 * length
+    outs = [
+        ((16, 64, dq), BF), ((8, 64, do), BF), ((16, 64, di), BF), ((16,) + w_down.shape, BF),
+        ((8, depth), F32), ((tokens, depth), BF), ((tokens, dq), BF), ((tokens, dq // 3), BF), ((2, length, 128), F32),
+        ((tokens, depth), BF), ((tokens, 128), F32), ((tokens, depth), BF), ((tokens, di), BF), ((2, length, depth), BF),
+        ((2, length, length), F32), ((16,) + w_down.shape, BF), ((length, depth), F32),
     ]
-    scratch = list(shapes)
-    scratch.insert(1, ((16, 32, do), bf))
+    scratch = [
+        ((16, 64, dq), BF), ((16, 32, do), BF), ((8, 64, do), BF), ((16, 64, di), BF), ((16,) + w_down.shape, BF),
+        ((16, 16, 128), F32), ((16, 128), F32), ((16, 128), F32), ((2, length, depth), BF), ((2, length, depth), BF),
+        ((2, length, 128), jnp.int32), ((2, 8, length), jnp.int32), ((2, length, length), F32),
+        ((8, depth), F32), ((8, di), F32), ((8, dq), F32), ((tokens, depth), BF), ((tokens, dq), BF),
+        ((tokens, dq // 3), BF), ((2, length, 128), F32), ((tokens, depth), F32), ((tokens, depth), BF),
+        ((tokens, depth), BF), ((length, depth), BF), ((tokens, depth), BF), ((tokens, depth), BF), ((tokens, 128), F32),
+        ((tokens, di), BF), ((tokens, di), BF), ((16,) + w_down.shape, BF),
+    ]
     return pl.pallas_call(
-        gather_kernel,
-        out_shape=[jax.ShapeDtypeStruct(s, d) for s, d in shapes],
-        in_specs=[pl.BlockSpec(memory_space=pl.ANY)] * 7,
-        out_specs=[pl.BlockSpec(memory_space=pl.ANY)] * 7,
+        forward_kernel,
+        out_shape=[jax.ShapeDtypeStruct(s, d) for s, d in outs],
+        in_specs=[pl.BlockSpec(memory_space=pl.ANY)] * 9,
+        out_specs=[pl.BlockSpec(memory_space=pl.ANY)] * len(outs),
         scratch_shapes=[pltpu.VMEM(s, d) for s, d in scratch]
         + [
             pltpu.SemaphoreType.DMA((5, 15)),
             pltpu.SemaphoreType.DMA((5, 15)),
-            pltpu.SemaphoreType.DMA((5,)),
-            pltpu.SemaphoreType.DMA((5,)),
-            pltpu.SemaphoreType.DMA((15,)),
+            pltpu.SemaphoreType.DMA((13,)),
+            pltpu.SemaphoreType.DMA((13,)),
+            pltpu.SemaphoreType.DMA((32,)),
         ],
         compiler_params=pltpu.CompilerParams(
-            collective_id=0, has_side_effects=True, vmem_limit_bytes=60 * 1024 * 1024
+            collective_id=0, has_side_effects=True, vmem_limit_bytes=67043328
         ),
-        name="weights_gather",
-    )(wqkv2, w_out, win2, w_down, tile, inputs, cotangent)
+        name="forward_gather",
+    )(wqkv2, w_out, win2, w_down, tile, inputs, cotangent, col, row)
 
 
 def scatter_kernel(
@@ -795,48 +1033,29 @@
     tile = jnp.concatenate([tile, in_bias.astype(f32)[None], jnp.zeros((7, 128), f32)])
     wqkv2 = w_qkv.reshape(rows, 3, 2, d_model // 2).transpose(2, 0, 1, 3).reshape(2, rows, -1)
     win2 = w_in.reshape(rows, 16, 2, 128).transpose(2, 0, 1, 3).reshape(2, rows, -1)
-    qkv_f, out_f, in_f, down_f, vec_f, tok2, cot2 = gather_all(wqkv2, w_out, win2, w_down, tile, inputs, cotangent)
-    mates = swap(vec_f)
-    vecs = (vec_f + mates)[:, :8].reshape(8, 2, 8, 128).sum(1).transpose(1, 0, 2).reshape(8, d_model)
-    g1, b1, qb, vb, ob, g2, b2, db = [vecs[i] for i in range(8)]
-    inb = vec_f[:, 8].reshape(-1)
+    col = jnp.broadcast_to(segment_ids[:, None], (length, 128))
+    row = jnp.broadcast_to(segment_ids[None, :], (8, length))
+    half = d_model // 2
+    (
+        qkv_f, out_f, in_f, down_f, vecs, norm_one, triple, attended, lse, x2, r2, norm_two, slope, cot2, mask, grad_down,
+        layer_out,
+    ) = forward_all(wqkv2, w_out, win2, w_down, tile, inputs, cotangent, col, row)
+    g1, g2 = vecs[0], vecs[5]
     qkv_m = qkv_f.reshape(d_model, -1)
     out_m = out_f.reshape(-1, d_model)
     in_m = in_f.reshape(d_model, -1)
     down_m = down_f.reshape(-1, d_model)
-    half = d_model // 2
-    cut = lambda v: lax.dynamic_slice(v, (c * half,), (half,))
-    seg2 = jnp.where(c == 0, jnp.stack([segment_ids, swap(segment_ids)]), jnp.stack([swap(segment_ids), segment_ids]))
-    tokens = tok2.astype(f32).reshape(2 * length, d_model)
-    position = jnp.arange(length, dtype=jnp.int32)
-    allowed = ((seg2[:, :, None] == seg2[:, None, :]) & (seg2[:, :, None] >= 0)) | (
-        position[:, None] == position[None, :]
-    )
-    n1, x1, r1 = normalize(tokens, g1, b1)
-    norm_one = n1.astype(bf)
-    shifts = jnp.concatenate([cut(qb), jnp.zeros((half,), f32), cut(vb)])
-    triple = (jnp.dot(norm_one, qkv_m, preferred_element_type=f32) + shifts).astype(bf)
+    cot = cot2.reshape(2 * length, d_model)
+    pick = lambda a, i: lax.dynamic_index_in_dim(a, i, 0, False)
+    x2 = x2.astype(f32)
+    r2 = r2[:, :1]
     t5 = triple.reshape(2, length, 3, half // HD, HD)
     q, k, v = t5[:, :, 0], t5[:, :, 1], t5[:, :, 2]
-    scores = jnp.einsum("sqhd,skhd->shqk", q, k, preferred_element_type=f32) * HD ** (-0.5)
-    scores = jnp.where(allowed[:, None], scores, NEG_FILL)
-    probs = jax.nn.softmax(scores, axis=-1)
+    scores = jnp.einsum("sqhd,skhd->shqk", q, k, preferred_element_type=f32) * HD ** (-0.5) + mask[:, None]
+    probs = jnp.exp(scores - lse[:, :, : half // HD].transpose(0, 2, 1)[..., None])
     probs_low = probs.astype(bf)
-    attended = jnp.einsum("shqk,skhd->sqhd", probs_low, v, preferred_element_type=f32)
-    attended = attended.reshape(2 * length, half).astype(bf)
-    part = jnp.dot(attended, out_m, preferred_element_type=f32)
-    middle = tokens + part + swap(part) + ob
-    n2, x2, r2 = normalize(middle, g2, b2)
-    norm_two = n2.astype(bf)
-    pre_act = jnp.dot(norm_two, in_m, preferred_element_type=f32) + inb
-    hidden = gelu_value(pre_act).astype(bf)
-    cot = cot2.reshape(2 * length, d_model)
-    grad_down = jnp.einsum("sf,sd->fd", hidden, cot, preferred_element_type=f32).astype(bf)
-    outp = jnp.dot(hidden, down_m, preferred_element_type=f32).reshape(2, length, d_model)
-    pick = lambda a, i: lax.dynamic_index_in_dim(a, i, 0, False)
-    layer_out = pick(middle.reshape(2, length, d_model), c) + pick(outp, c) + swap(pick(outp, 1 - c)) + db
     grad_hidden = jnp.einsum("sd,fd->sf", cot, down_m, preferred_element_type=f32)
-    grad_pre = (grad_hidden * gelu_slope(pre_act)).astype(bf)
+    grad_pre = (grad_hidden * slope.astype(f32)).astype(bf)
     grad_in = jnp.einsum("sd,sf->df", norm_two, grad_pre, preferred_element_type=f32).astype(bf)
     grad_in_bias = jnp.sum(grad_pre.astype(f32), 0)
     gn2 = jnp.einsum("sf,df->sd", grad_pre, in_m, preferred_element_type=f32)
@@ -858,12 +1077,12 @@
     gn1 = jnp.einsum("st,dt->sd", gt, qkv_m, preferred_element_type=f32).reshape(2, length, d_model)
     gn1 = pick(gn1, c) + swap(pick(gn1, 1 - c))
     own = lambda a: pick(a.reshape(2, length, d_model), c)
-    r1o = pick(r1.reshape(2, length, 1), c)
-    grad_input = own(gm) + normalize_back(gn1, own(x1), r1o, g1)
+    _, x1, r1 = normalize(inputs.astype(f32), g1, g1)
+    grad_input = own(gm) + normalize_back(gn1, x1, r1, g1)
     put = lambda v: lax.dynamic_update_slice(jnp.zeros((d_model,), f32), v, (c * half,))
     sums = jnp.stack(
         [
-            jnp.sum(gn1 * own(x1), 0), jnp.sum(gn1, 0), put(gqb), put(gvb), jnp.sum(own(grad_mixed).astype(f32), 0),
+            jnp.sum(gn1 * x1, 0), jnp.sum(gn1, 0), put(gqb), put(gvb), jnp.sum(own(grad_mixed).astype(f32), 0),
             jnp.sum(own(gn2 * x2), 0), jnp.sum(own(gn2), 0), jnp.sum(own(cot).astype(f32), 0),
         ]
     )

time: 516 us -> 485 us (0.940)
  matrix products: 108 us -> 67.1 us
  Pallas kernels: 279 us -> 297 us
  waiting for transfers between devices: 6.82 us -> 0.01 us
  local copies, waits for them, and re-layouts: 65.6 us -> 71.8 us
  other arithmetic: 43.4 us -> 37.7 us
    dot_general x6 -> x1, matrix products: 35.9 us -> 9.78 us  [local_split(): jnp.einsum('sqhd,skhd->shqk', q, k, preferred_element_type=f32)]
    pallas_call x1, Pallas kernels: 130 us -> 144 us  [forward_all(): pl.pallas_call(forward_kernel, out_shape=[jax.ShapeDtypeStruct(s, d) for...]
    sub x1 -> x0, matrix products: 11.3 us -> none  [local_split(): probs = jax.nn.softmax(scores, axis=-1)]
    ppermute x6 -> x2, waiting for transfers between devices: 6.82 us -> 0.01 us  [swap(): return lax.ppermute(value, 'c', [(0, 1), (1, 0)])]
    unnamed x98 -> x64, local copies, waits for them, and re-layouts: 29.7 us -> 24 us
  transfers between devices with their start and end apart: 6 -> 2, of which waited for: 1 -> 0; matrix products, arithmetic and copies ran while one was open for 21% -> 13% of each run, Pallas kernels for 26% -> 0%
where the time goes in v2:
time: 485 us; the launch traced here: 476 us
  Pallas kernels  297 us (61%)
  local copies, waits for them, and re-layouts  71.8 us (15%)
  matrix products  67.1 us (14%)
  other arithmetic  37.7 us (8%)
    pallas_call x1, Pallas kernels, scatter_all(): pl.pallas_call(scatter_kernel, out_shape=[jax.ShapeDtypeStruct(s, d) for...  153 us
    pallas_call x1, Pallas kernels, forward_all(): pl.pallas_call(forward_kernel, out_shape=[jax.ShapeDtypeStruct(s, d) for...  144 us
    unnamed x64, local copies, waits for them, and re-layouts  24 us
    convert_element_type x1, other arithmetic, local_split(): gs = (probs * (gp - jnp.sum(probs * gp, -1, keepdims=True))).astype(bf)  12.3 us
    dot_general x1, matrix products, local_split(): gp = jnp.einsum('sqhd,skhd->shqk', ga, v, preferred_element_type=f32)  11.6 us
    dot_general x1, matrix products, local_split(): jnp.einsum('sqhd,skhd->shqk', q, k, preferred_element_type=f32)  9.78 us
  transfers between devices with their start and end apart: 2, of which 0 were waited for; matrix products, arithmetic and copies ran while one was open for 13% of the time, Pallas kernels for 0%

profile of v2, /device:TPU:0, one launch (start us, length us, event | category | flops | bytes accessed | tf_op | source)
XLA Modules:
  0.0 475.7 jit_solution(14929360753219604350)
XLA Ops:
  10.0 144.4 %forward_gather.1 = (bf16[16,64,1536]{2,1,0:T(8,128)(2,1)}, bf16[8,64,1024]{2,1,0:T(8,128)(2,1)}, bf16[16,64,2048]{2,1,0:T(8,128)(2,1)}, bf16[16,128,1024]{2,1,0...) custom-call(bf16[2,32,1536]{2,1,0:T(8,128)(2,1)} %reshape.262.wqkv_r, ...), custom_call_target="tpu_custom_call" | custom-call | tf_op jit(solution)/shard_map/forward_gather/pallas_call | solution.py:878
  154.5 8.7 %convert_reduce_fusion = (f32[2048]{0:T(1024)S(1)}, bf16[1024,2048]{1,0:T(8,128)(2,1)S(1)}) fusion(bf16[1024,2048]{1,0:T(8,128)(2,1)} %get-tuple-element.41, bf16[1024,1024]{1,0:T(8,128)(2,1)} %bitcast.144, bf16[2048,1024]{1,0:T(8,128)(2,1)} %bitcast.180), kind=kOutput, calls=%fused_computation.4 | convolution fusion | flops 4305451008 | bytes 14688256 | tf_op jit(solution)/shard_map/sd,fd->sf/dot_general | solution.py:1057
  163.3 6.6 %fusion.41 = f32[1024,1024]{1,0:T(8,128)} fusion(bf16[1024,2048]{1,0:T(8,128)(2,1)S(1)} %get-tuple-element.88, bf16[1024,2048]{1,0:T(8,128)(2,1)S(1)} %bitcast.179), kind=kOutput, calls=%fused_computation.92 | convolution fusion | flops 4294967296 | bytes 12582912 | tf_op jit(solution)/shard_map/sf,df->sd/dot_general | solution.py:1061
  170.1 1.9 copy.68
  172.0 8.9 %reshape.287 = bf16[2,512,3,8,64]{4,3,2,1,0:T(8,128)(2,1)} reshape(bf16[1024,1536]{1,0:T(8,128)(2,1)} %get-tuple-element.45) | data formatting | bytes 6291456 | tf_op jit(solution)/shard_map/reshape | solution.py:1052
  180.9 5.7 %fusion.39 = (bf16[2,512,1,8,64]{4,3,2,1,0:T(8,128)(2,1)}, bf16[2,512,1,8,64]{4,3,2,1,0:T(8,128)(2,1)}, bf16[2,512,1,8,64]{4,3,2,1,0:T(8,128)(2,1)}) fusion(bf16[2,512,3,8,64]{4,3,2,1,0:T(8,128)(2,1)} %reshape.287), kind=kLoop, calls=%fused_computation.90 | loop fusion | bytes 6291456 | tf_op jit(solution)/shard_map/slice | solution.py:1053
  186.5 3.3 copy.92
  189.9 3.4 copy.91
  193.3 3.3 copy.90
  198.9 9.8 %fusion.24 = f32[2,8,512,512]{2,3,1,0:T(8,128)} fusion(bf16[2,512,1,8,64]{1,4,3,0,2:T(8,128)(2,1)} %copy.91, bf16[2,512,1,8,64]{1,4,3,0,2:T(8,128)(2,1)} %copy.90), kind=kOutput, calls=%fused_computation.48 | convolution fusion | flops 536870912 | bytes 18874368 | tf_op jit(solution)/shard_map/sqhd,skhd->shqk/dot_general | solution.py:1054
  208.7 6.4 %convolution_convert_fusion.1 = bf16[1024,2048]{1,0:T(8,128)(2,1)} fusion(bf16[1024,1024]{1,0:T(8,128)(2,1)S(1)} %copy-done.24, bf16[1024,2048]{1,0:T(8,128)(2,1)S(1)} %copy-done.27), kind=kOutput, calls=%fused_computation.16 | convolution fusion | flops 4297064448 | bytes 10485760 | tf_op jit(solution)/shard_map/sd,sf->df/dot_general | solution.py:1059
  215.2 7.0 %convert_multiply_fusion = (f32[1024,1024]{1,0:T(8,128)}, f32[1024,1024]{1,0:T(8,128)S(1)}) fusion(bf16[1024,1024]{1,0:T(8,128)(2,1)S(1)} %copy-done.4, f32[1024,1024]{1,0:T(8,128)} %fusion.41, f32[1024,1024]{1,0:T(8,128)} %collective-permute-done), kind=kLoop, calls=%fused_computation.8 | loop fusion | flops 3145728 | bytes 18874368 | tf_op jit(solution)/shard_map/mul | solution.py:1086
  225.3 3.0 fusion.37
  230.9 2.1 reshape.288
  233.0 2.5 copy.72
  235.5 7.9 %fusion.18 = bf16[2,512,1,8,64]{1,4,3,0,2:T(8,128)(2,1)S(1)} fusion(bf16[2,512,8,64]{1,3,2,0:T(8,128)(2,1)S(1)} %copy.72, f32[2,8,512,512]{2,3,1,0:T(8,128)} %fusion.24, f32[2,8,512]{2,1,0:T(8,128)S(1)} %copy.69, f32[2,512,512]{1,2,0:T(8,128)S(1)} %copy.68), kind=kOutput, calls=%fused_computation.42 | convolution fusion | flops 553648128 | bytes 21004288 | tf_op jit(solution)/shard_map/shqk,sqhd->skhd/dot_general | solution.py:1072
  243.4 11.6 %multiply_reduce_fusion = (f32[2,8,512]{2,1,0:T(8,128)S(1)}, f32[2,8,512,512]{2,3,1,0:T(8,128)}) fusion(f32[2,8,512,512]{2,3,1,0:T(8,128)} %fusion.24, f32[2,8,512]{2,1,0:T(8,128)S(1)} %copy.69, f32[2,512,512]{1,2,0:T(8,128)S(1)} %copy.68, bf16[2,512,8,64]{1,3,2,0:T(8,128)(2,1)S(1)} %copy.72, bf16[2,512,1,8,64]{1,4,3,0,2:T(8,128)(2,1)S(1)} %copy-done.11), kind=kOutput, calls=%fused_computation.1 | convolution fusion | flops 557834240 | bytes 37814272 | tf_op jit(solution)/shard_map/sqhd,skhd->shqk/dot_general | solution.py:1068
  255.0 12.3 %multiply_convert_fusion = bf16[2,8,512,512]{2,3,1,0:T(8,128)(2,1)S(1)} fusion(f32[2,8,512,512]{2,3,1,0:T(8,128)} %get-tuple-element.86, f32[2,8,512,512]{2,3,1,0:T(8,128)} %fusion.24, f32[2,8,512]{2,1,0:T(8,128)S(1)} %get-tuple-element.85, f32[2,8,512]{2,1,0:T(8,128)S(1)} %copy.69, f32[2,512,512]{1,2,0:T(8,128)S(1)} %copy.68), kind=kLoop, calls=%fused_computation | loop fusion | flops 25165824 | bytes 44105728 | tf_op jit(solution)/shard_map/convert_element_type | solution.py:1069
  267.3 2.6 multiply_bitcast_fusion
  272.0 1.6 copy-done.22
  273.7 3.5 fusion.42
  277.1 1.9 copy-done.12
  279.1 1.6 dynamic-slice_bitcast_fusion
  282.5 1.6 fusion.17
  284.2 3.3 copy.79
  291.5 2.2 convolution_convert_fusion.2
  293.8 5.0 %convolution_convert_fusion = bf16[1024,1536]{1,0:T(8,128)(2,1)} fusion(bf16[1024,1024]{1,0:T(8,128)(2,1)S(1)} %copy-done.23, bf16[1024,1536]{0,1:T(8,128)(2,1)S(1)} %bitcast.143), kind=kOutput, calls=%fused_computation.15 | convolution fusion | flops 3222798336 | bytes 8388608 | tf_op jit(solution)/shard_map/sd,st->dt/dot_general | solution.py:1074
  298.8 2.7 fusion.16
  302.4 152.7 %gradients_scatter.1 = (f32[2,32,1536]{2,1,0:T(8,128)}, f32[32,1024]{1,0:T(8,128)}, f32[2,32,2048]{2,1,0:T(8,128)}, f32[128,1024]{1,0:T(8,128)}, f32[2,16,128]{2,1,0:T(8,128)}) custom-call(bf16[16,64,1536]{2,1,0:T(8,128)(2,1)} %bitcast.148, bf16[8,64,1024]{2,1,0:T(8,128)(2,1)} %bitcast.146, bf16[16,64,2048]{2,1,0:T(8,128)(2,1)} %bitcast.145, ...), custom_call_target="tpu_custom_call" | custom-call | tf_op jit(solution)/shard_map/gradients_scatter/pallas_call | solution.py:991
  458.2 2.1 reshape.281
  465.1 2.3 reshape.284
  467.3 3.8 fusion.15
  (116 shorter events, 38.5 us)
Async XLA Ops:
  6.6 0.7 copy-start.19
  154.5 8.8 %copy-start.21 = (bf16[16,64,2048]{2,1,0:T(8,128)(2,1)S(1)}, bf16[16,64,2048]{2,1,0:T(8,128)(2,1)}, u32[]{:S(2)}) copy-start(bf16[16,64,2048]{2,1,0:T(8,128)(2,1)} %get-tuple-element.42) | copy-start | bytes 12582916
  163.2 6.6 %copy-start.26 = (bf16[1024,2048]{1,0:T(8,128)(2,1)}, bf16[1024,2048]{1,0:T(8,128)(2,1)S(1)}, u32[]{:S(2)}) copy-start(bf16[1024,2048]{1,0:T(8,128)(2,1)S(1)} %get-tuple-element.88) | copy-start | bytes 12582916
  163.2 6.6 %copy-start.17 = (f32[2,512,128]{2,1,0:T(8,128)S(1)}, f32[2,512,128]{2,1,0:T(8,128)}, u32[]{:S(2)}) copy-start(f32[2,512,128]{2,1,0:T(8,128)} %get-tuple-element.47) | copy-start | bytes 1572868
  169.8 45.3 %collective-permute-start = (f32[1024,1024]{1,0:T(8,128)}, f32[1024,1024]{1,0:T(8,128)}, u32[]{:S(2)}, u32[]{:S(2)}) collective-permute-start(f32[1024,1024]{1,0:T(8,128)} %fusion.41), channel_id=1, source_target_pairs={{0,1},{1,0},{2,3},{3,2},{4,5},{5,4},{6,7},{7,6},{8,9},{9,8},{10,11... | collective-permute-start | bytes 12582920 | tf_op jit(solution)/shard_map/ppermute | solution.py:1015
  189.9 8.0 %copy-start.2 = (bf16[512,1024]{1,0:T(8,128)(2,1)S(1)}, bf16[512,1024]{1,0:T(8,128)(2,1)}, u32[]{:S(2)}) copy-start(bf16[512,1024]{1,0:T(8,128)(2,1)} %tok_ref.1) | copy-start | bytes 3145732
  198.9 9.8 %copy-start.24 = (bf16[1024,1024]{1,0:T(8,128)(2,1)S(1)}, bf16[1024,1024]{1,0:T(8,128)(2,1)}, u32[]{:S(2)}) copy-start(bf16[1024,1024]{1,0:T(8,128)(2,1)} %get-tuple-element.52) | copy-start | bytes 6291460
  198.9 9.8 %copy-start.27 = (bf16[1024,2048]{1,0:T(8,128)(2,1)S(1)}, bf16[1024,2048]{1,0:T(8,128)(2,1)}, u32[]{:S(2)}) copy-start(bf16[1024,2048]{1,0:T(8,128)(2,1)} %copy-done.26) | copy-start | bytes 12582916
  208.7 6.5 %copy-start.4 = (bf16[1024,1024]{1,0:T(8,128)(2,1)S(1)}, bf16[1024,1024]{1,0:T(8,128)(2,1)}, u32[]{:S(2)}) copy-start(bf16[1024,1024]{1,0:T(8,128)(2,1)} %get-tuple-element.44) | copy-start | bytes 6291460
  222.2 2.1 copy-start
  222.2 3.1 copy-start.10
  225.3 4.3 copy-start.25
  228.3 1.3 copy-start.6
  235.5 7.9 %copy-start.11 = (bf16[2,512,1,8,64]{1,4,3,0,2:T(8,128)(2,1)S(1)}, bf16[2,512,1,8,64]{1,4,3,0,2:T(8,128)(2,1)}, u32[]{:S(2)}) copy-start(bf16[2,512,1,8,64]{1,4,3,0,2:T(8,128)(2,1)} %copy.92) | copy-start | bytes 3145732
  255.0 12.3 %copy-start.8 = (bf16[2,512,1,8,64]{1,4,3,0,2:T(8,128)(2,1)S(1)}, bf16[2,512,1,8,64]{1,4,3,0,2:T(8,128)(2,1)}, u32[]{:S(2)}) copy-start(bf16[2,512,1,8,64]{1,4,3,0,2:T(8,128)(2,1)} %copy.91) | copy-start | bytes 3145732
  267.3 2.6 copy-start.5
  271.8 1.9 copy-start.22
  277.1 1.9 copy-start.12
  280.6 18.2 %collective-permute-start.1 = (f32[512,1024]{1,0:T(8,128)}, f32[512,1024]{1,0:T(8,128)}, u32[]{:S(2)}, u32[]{:S(2)}) collective-permute-start(f32[512,1024]{1,0:T(8,128)} %dynamic-slice_bitcast_fusion), channel_id=1, source_target_pairs={{0,1},{1,0},{2,3},{3,2},{4,5},{5,4},{6,7},{7,6},{8,9},{9,8},{10,11... | collective-permute-start | bytes 6291464 | tf_op jit(solution)/shard_map/ppermute | solution.py:1015
  284.2 5.1 %copy-start.9 = (f32[1024,1024]{1,0:T(8,128)S(1)}, f32[1024,1024]{1,0:T(8,128)}, u32[]{:S(2)}) copy-start(f32[1024,1024]{1,0:T(8,128)} %get-tuple-element.67) | copy-start | bytes 12582916
  287.5 1.6 copy-start.7
  287.5 2.8 copy-start.1
  290.3 1.2 copy-start.15
  290.6 3.1 copy-start.23
  293.8 5.0 %copy-start.3 = (bf16[512,1024]{1,0:T(8,128)(2,1)S(1)}, bf16[512,1024]{1,0:T(8,128)(2,1)}, u32[]{:S(2)}) copy-start(bf16[512,1024]{1,0:T(8,128)(2,1)} %tok_ref.1) | copy-start | bytes 3145732
  293.8 5.0 %copy-start.13 = (f32[2,512,1024]{2,1,0:T(8,128)S(1)}, f32[2,512,1024]{2,1,0:T(8,128)}, u32[]{:S(2)}) copy-start(f32[2,512,1024]{2,1,0:T(8,128)} %copy-done.12) | copy-start | bytes 12582916
  298.8 2.8 copy-start.20
  467.3 5.2 %copy-start.14 = (f32[512,1024]{1,0:T(8,128)S(1)}, f32[512,1024]{1,0:T(8,128)}, u32[]{:S(2)}) copy-start(f32[512,1024]{1,0:T(8,128)} %get-tuple-element.108) | copy-start | bytes 6291460
  471.1 2.7 copy-start.18
  471.1 3.4 copy-start.16

commit v3 on v2

--- a/solution.py
+++ b/solution.py
@@ -596,6 +596,8 @@
 
 
 def span(i, size):
+    if isinstance(i, int):
+        return pl.ds(i * size, size)
     return pl.ds(pl.multiple_of(i * size, size), size)
 
 
@@ -617,7 +619,7 @@
             here = lax.broadcasted_iota(jnp.int32, (128, size), 0) + i * 128
             there = lax.broadcasted_iota(jnp.int32, (128, size), 1)
             fine = ((col == row) & (col >= 0)) | (here == there)
-            mask[s, rows, :] = jnp.where(fine, 0.0, NEG_FILL)
+            mask[s, rows, :] = jnp.where(fine, 0.0, NEG_FILL).astype(BF)
             return carry
 
         lax.fori_loop(0, size // 128, body, 0)
@@ -636,6 +638,7 @@
 
 
 G1, B1, QB, VB, OB, G2, B2, DB = range(8)
+INV_AT = 64
 
 
 def attend_pair(i, triple, mask, attended, lse):
@@ -653,7 +656,7 @@
     kept = lse[s]
     for h in range(2):
         mine = low if h == 0 else ~low
-        scores = mm(jnp.where(mine, q, jnp.zeros_like(q)), k, NT) * HD ** (-0.5) + mask[s]
+        scores = mm(jnp.where(mine, q, jnp.zeros_like(q)), k, NT) * HD ** (-0.5) + mask[s].astype(F32)
         highest = jnp.max(scores, -1, keepdims=True)
         exponent = jnp.exp(scores - highest)
         total = jnp.sum(exponent, -1, keepdims=True)
@@ -666,10 +669,10 @@
 
 def forward_kernel(
     wqkv_ref, wout_ref, win_ref, wdown_ref, tile_ref, tok_ref, cot_ref, col_ref, row_ref,
-    qkv_o, out_o, in_o, down_o, vecs_o, norm1_o, triple_o, att_o, lse_o, xhat_o, inv_o, norm2_o, slope_o, cot_o,
+    qkv_o, out_o, in_o, down_o, vecs_o, norm1_o, triple_o, att_o, lse_o, xhat_o, norm2_o, slope_o, cot_o,
     mask_o, gdown_o, layer_o,
     w_qkv, w_nat, w_out, w_in, w_down, tiles, tile, tile_in, tok, cot, col, row, mask,
-    vecs, hshift, tshift, norm1, triple, att, lse, mid, part, part_in, last_in, norm2, xhat, inv, hidden, slope, gdown,
+    vecs, hshift, tshift, norm1, triple, att, lse, mid, part, part_in, last_in, norm2, xhat, hidden, slope, gdown,
     sent, came, pair_sent, pair_came, local,
 ):
     p = Place()
@@ -760,7 +763,7 @@
     stores.append(load(triple, triple_o))
     lse[...] = jnp.zeros_like(lse)
     pump.loop(8, functools.partial(attend_pair, triple=triple, mask=mask, attended=att, lse=lse), 1)
-    stores += [load(att, att_o), load(lse, lse_o)]
+    stores.append(load(att, att_o))
     g_out.finish()
     half = pair.copy(w_nat.at[pl.ds(8 * (1 - c), 8)], w_out.at[:, mine], 7)
     half.start()
@@ -790,11 +793,13 @@
         mid[rows, :] = v
         normed, inverse = stats(v)
         xhat[rows, :] = normed.astype(BF)
-        inv[rows, :] = jnp.broadcast_to(inverse, (256, 128))
+        lane = lax.broadcasted_iota(jnp.int32, (256, 128), 1)
+        inside = span(lax.rem(i, 2), 256)
+        lse[i // 2, inside, :] = jnp.where(lane < INV_AT, lse[i // 2, inside, :], inverse)
         norm2[rows, :] = (normed * vecs[G2 : G2 + 1, :] + vecs[B2 : B2 + 1, :]).astype(BF)
 
     pump.loop(4, second_norm, 0)
-    stores += [load(xhat, xhat_o), load(inv, inv_o), load(norm2, norm2_o)]
+    stores += [load(xhat, xhat_o), load(lse, lse_o), load(norm2, norm2_o)]
     pump.take(max(len(pump.queue) - 7, 0))
     g_in.finish()
     stores.append(load(w_in, in_o))
@@ -863,16 +868,16 @@
     outs = [
         ((16, 64, dq), BF), ((8, 64, do), BF), ((16, 64, di), BF), ((16,) + w_down.shape, BF),
         ((8, depth), F32), ((tokens, depth), BF), ((tokens, dq), BF), ((tokens, dq // 3), BF), ((2, length, 128), F32),
-        ((tokens, depth), BF), ((tokens, 128), F32), ((tokens, depth), BF), ((tokens, di), BF), ((2, length, depth), BF),
-        ((2, length, length), F32), ((16,) + w_down.shape, BF), ((length, depth), F32),
+        ((tokens, depth), BF), ((tokens, depth), BF), ((tokens, di), BF), ((2, length, depth), BF),
+        ((2, length, length), BF), ((16,) + w_down.shape, BF), ((length, depth), F32),
     ]
     scratch = [
         ((16, 64, dq), BF), ((16, 32, do), BF), ((8, 64, do), BF), ((16, 64, di), BF), ((16,) + w_down.shape, BF),
         ((16, 16, 128), F32), ((16, 128), F32), ((16, 128), F32), ((2, length, depth), BF), ((2, length, depth), BF),
-        ((2, length, 128), jnp.int32), ((2, 8, length), jnp.int32), ((2, length, length), F32),
+        ((2, length, 128), jnp.int32), ((2, 8, length), jnp.int32), ((2, length, length), BF),
         ((8, depth), F32), ((8, di), F32), ((8, dq), F32), ((tokens, depth), BF), ((tokens, dq), BF),
         ((tokens, dq // 3), BF), ((2, length, 128), F32), ((tokens, depth), F32), ((tokens, depth), BF),
-        ((tokens, depth), BF), ((length, depth), BF), ((tokens, depth), BF), ((tokens, depth), BF), ((tokens, 128), F32),
+        ((tokens, depth), BF), ((length, depth), BF), ((tokens, depth), BF), ((tokens, depth), BF),
         ((tokens, di), BF), ((tokens, di), BF), ((16,) + w_down.shape, BF),
     ]
     return pl.pallas_call(
@@ -895,47 +900,93 @@
     )(wqkv2, w_out, win2, w_down, tile, inputs, cotangent, col, row)
 
 
-def scatter_kernel(
-    qkv_ref, out_ref, in_ref, down_ref, vec_ref,
-    qkv_o, out_o, in_o, down_o, vec_o,
+def attend_pair_back(i, triple, mask, lse, gatt, gtriple, sums, c):
+    length = mask.shape[1]
+    half = gatt.shape[1]
+    pairs = half // 128
+    s, pair = i // pairs, lax.rem(i, pairs)
+    rows, blocks = span(s, length), span(s, length // 64)
+
+    def at(third):
+        return pl.ds(pl.multiple_of(third * half + pair * 128, 128), 128)
+
+    q, k, v = (triple[blocks, :, at(t)].reshape(length, 128) for t in range(3))
+    g = gatt[rows, at(0)]
+    lane = lax.broadcasted_iota(jnp.int32, (length, 128), 1)
+    low = lane < HD
+    zero = jnp.zeros_like(q)
+    scale = HD ** (-0.5)
+    parts = []
+    for h in range(2):
+        mine = low if h == 0 else ~low
+        scores = mm(jnp.where(mine, q, zero), k, NT) * scale + mask[s].astype(F32)
+        level = jnp.sum(jnp.where(lane == pair * 2 + h, lse[s], 0.0), -1, keepdims=True)
+        probs = jnp.exp(scores - level)
+        grad_probs = mm(jnp.where(mine, g, zero), v, NT)
+        inner = jnp.sum(probs * grad_probs, -1, keepdims=True)
+        grad_scores = (probs * (grad_probs - inner)).astype(BF)
+        parts.append(
+            (
+                mm(grad_scores, k) * scale,
+                mm(grad_scores, q, TN) * scale,
+                mm(probs.astype(BF), g, TN),
+            )
+        )
+    for t in range(3):
+        joined = jnp.where(low, parts[0][t], parts[1][t]).astype(BF)
+        gtriple[rows, at(t)] = joined
+        if t != 1:
+            row = QB if t == 0 else VB
+            where = pl.ds(pl.multiple_of(half * c + pair * 128, 128), 128)
+            sums[row : row + 1, where] += jnp.sum(joined.astype(F32), 0, keepdims=True)
+
+
+class Later:
+    def __init__(self, wait):
+        self.wait = wait
+
+
+def backward_kernel(
+    qkv_ref, out_ref, in_ref, down_ref, vecs_ref, norm1_ref, triple_ref, att_ref, lse_ref, xhat_ref, norm2_ref,
+    slope_ref, cot_ref, mask_ref, gdown_ref, tok_ref,
+    qkv_o, out_o, in_o, down_o, vec_o, input_o,
     b_qkv, b_out, b_in, b_down, b_vec,
     l_qkv, l_out, l_in, l_down, l_vec,
     f_qkv, f_out, f_in, f_down, f_vec, n_vec,
+    w_qkv, w_out, area, area2, wide, vecs, att, lse, xhat, norm2, cot, mask, part, part_in, gmid, gmixed,
+    gatt, gout, sums,
     sent, came, pair_sent, pair_came, local,
 ):
     p = Place()
     c = p.c
+    length, depth = gmid.shape
+    tokens, units = wide.shape
+    half = depth // 2
     mine = pl.ds(pl.multiple_of(ROWS * c, ROWS), ROWS)
     theirs = pl.ds(pl.multiple_of(ROWS * (1 - c), ROWS), ROWS)
-    loads = [
-        pltpu.make_async_copy(a, b, local.at[i])
-        for i, (a, b) in enumerate(
-            ((down_ref, b_down), (in_ref, b_in), (out_ref.at[:, mine], b_out.at[pl.ds(8 * c, 8)]), (qkv_ref, b_qkv), (vec_ref, b_vec))
-        )
-    ]
-    for load in loads:
-        load.start()
+    slots = iter(range(local.shape[0]))
+
+    def load(src, dst):
+        slot = next(slots)
+        pltpu.make_async_copy(src, dst, local.at[slot]).start()
+        return Later(lambda: pltpu.make_async_copy(src, dst, local.at[slot]).wait())
+
+    in_down = load(gdown_ref, b_down)
+    first = [load(down_ref, area), load(cot_ref, cot), load(slope_ref, wide)]
+    second = [load(norm2_ref, norm2), load(in_ref, area2)]
+    third = [load(xhat_ref, xhat), load(lse_ref, lse), load(vecs_ref, vecs), load(att_ref, att), load(out_ref, w_out)]
+    fourth = [load(mask_ref, mask), load(qkv_ref, w_qkv)]
     p.greet()
-
-    def to_partner(src, dst, slot):
-        return pltpu.make_async_remote_copy(
-            src_ref=src, dst_ref=dst, send_sem=pair_sent.at[slot], recv_sem=pair_came.at[slot],
-            device_id=p.partner(), device_id_type=MESH_ID,
-        )
-
-    half = to_partner(out_ref.at[:, theirs], b_out.at[pl.ds(8 * c, 8)], 0)
-    half.start()
+    pair = Pair(p, pair_sent, pair_came)
     s_down, s_in, s_out, s_qkv, s_vec = (
         Scatter(p, blocks, landed, sent.at[i], came.at[i])
         for i, (blocks, landed) in enumerate(
             ((b_down, l_down), (b_in, l_in), (b_out, l_out), (b_qkv, l_qkv), (b_vec, l_vec))
         )
     )
-    for i, s in enumerate((s_down, s_in, s_out, s_qkv, s_vec)):
-        loads[i].wait()
-        if i == 2:
-            half.wait_recv()
-        s.begin()
+    in_down.wait()
+    s_down.begin()
+    stores = []
 
     def put(ref):
         def write(at, value):
@@ -943,155 +994,260 @@
 
         return write
 
-    finals = {0: f_down, 1: f_in, 2: f_out, 3: f_qkv, 4: f_vec}
-    every = (s_down, s_in, s_out, s_qkv, s_vec)
-    for s in every:
-        for dz in (1, 2, 3, 0):
-            s.across(dz)
-        for dz in (1, 2, 3, 0):
-            s.along(dz)
-    for i, s in enumerate(every):
-        s.total(put(finals[i]))
-    pair = [
-        to_partner(f_qkv.at[theirs], qkv_o.at[c], 1),
-        to_partner(f_in.at[theirs], in_o.at[c], 2),
-        to_partner(f_vec, n_vec, 3),
-    ]
-    for copy in pair:
-        copy.start()
-    stores = [
-        pltpu.make_async_copy(f_down, down_o, local.at[5]),
-        pltpu.make_async_copy(f_out, out_o, local.at[6]),
-        pltpu.make_async_copy(f_qkv.at[mine], qkv_o.at[c], local.at[7]),
-        pltpu.make_async_copy(f_in.at[mine], in_o.at[c], local.at[8]),
-        pltpu.make_async_copy(f_vec, vec_o.at[0], local.at[9]),
-    ]
-    for store in stores:
-        store.start()
-    pair[2].wait_recv()
-    other = pltpu.make_async_copy(n_vec, vec_o.at[1], local.at[10])
-    other.start()
-    for s in every:
+    def end_down():
+        s_down.total(put(f_down))
+        stores.append(load(f_down, down_o))
+
+    def end_in():
+        s_in.total(put(f_in))
+        pair.copy(f_in.at[theirs], in_o.at[c], 1).start()
+        stores.append(load(f_in.at[mine], in_o.at[c]))
+
+    def end_out():
+        s_out.total(put(f_out))
+        stores.append(load(f_out, out_o))
+
+    def end_qkv():
+        s_qkv.total(put(f_qkv))
+        pair.copy(f_qkv.at[theirs], qkv_o.at[c], 2).start()
+        stores.append(load(f_qkv.at[mine], qkv_o.at[c]))
+
+    def end_vec():
+        s_vec.total(put(f_vec))
+        pair.copy(f_vec, n_vec, 3).start()
+        stores.append(load(f_vec, vec_o.at[0]))
+
+    pump = Pump()
+    pump.add(s_down.steps())
+    sums[...] = jnp.zeros_like(sums)
+    b_vec[...] = jnp.zeros_like(b_vec)
+    for copy in first:
+        copy.wait()
+
+    def hidden_grad(i):
+        cols = span(i, 256)
+        w = area[span(i, 2)].reshape(256, depth)
+        grad = mm(cot[...].reshape(tokens, depth), w, NT) * wide[:, cols].astype(F32)
+        low = grad.astype(BF)
+        wide[:, cols] = low
+        total = jnp.sum(low.astype(F32), 0, keepdims=True)
+        b_vec[2 * i, 8:9, :] = total[:, 0:128]
+        b_vec[2 * i + 1, 8:9, :] = total[:, 128:256]
+
+    pump.loop(units // 256, hidden_grad, 1)
+    for copy in second:
+        copy.wait()
+
+    def in_grad(i):
+        cols = span(i, 256)
+        b_in[span(i, 4)] = mm(norm2[:, cols], wide[...], TN).astype(BF).reshape(4, 64, units)
+
+    pump.loop(depth // 256, in_grad, 0)
+    pump.take(len(pump.queue))
+    s_in.begin()
+    pump.add([end_down])
+    pump.add(s_in.steps())
+
+    def send_part(i):
+        rows = span(i, 256)
+        return pair.copy(part.at[rows], part_in.at[rows], 4 + i)
+
+    def norm_grad(i):
+        rows = span(i, 256)
+        part[rows, :] = mm(wide[rows, :], area2[...].reshape(depth, units), NT).astype(BF)
+        send_part(i).start()
+
+    pump.loop(4, norm_grad, 1)
+    norm1_in = load(norm1_ref, area.at[0:8])
+    tok_in = load(tok_ref, area.at[8:12])
+    triple_in = load(triple_ref, area2.at[:, :, 0 : 3 * half])
+    for copy in third:
+        copy.wait()
+
+    def middle_rows(i, ours):
+        s = c if ours else 1 - c
+        inside = span(i, 128)
+        rows = pl.ds(pl.multiple_of(s * length + i * 128, 128), 128)
+        grad = part[rows, :].astype(F32) + part_in[rows, :].astype(F32)
+        normed = xhat[rows, :].astype(F32)
+        scaled = grad * vecs[G2 : G2 + 1, :]
+        top = cot[s, inside, :].astype(F32)
+        middle = top + lse[s, inside, INV_AT : INV_AT + 1] * (
+            scaled
+            - jnp.mean(scaled, -1, keepdims=True)
+            - normed * jnp.mean(scaled * normed, -1, keepdims=True)
+        )
+        low = middle.astype(BF)
+        gmixed[rows, :] = low
+        if ours:
+            gmid[inside, :] = middle
+            sums[G2 : G2 + 1, :] += jnp.sum(grad * normed, 0, keepdims=True)
+            sums[B2 : B2 + 1, :] += jnp.sum(grad, 0, keepdims=True)
+            sums[OB : OB + 1, :] += jnp.sum(low.astype(F32), 0, keepdims=True)
+            sums[DB : DB + 1, :] += jnp.sum(top, 0, keepdims=True)
+
+    for i in range(4):
+        send_part(i).wait_recv()
+    pump.loop(length // 128, functools.partial(middle_rows, ours=True), 0)
+    pump.loop(length // 128, functools.partial(middle_rows, ours=False), 0)
+
+    def out_grad(i):
+        cols = span(i, 256)
+        gout[span(i, 4)] = mm(att[:, cols], gmixed[...], TN).astype(BF).reshape(4, 64, depth)
+
+    pump.loop(half // 256, out_grad, 1)
+    keep = load(gout.at[:, mine], b_out.at[pl.ds(8 * c, 8)])
+    mate = pair.copy(gout.at[:, theirs], b_out.at[pl.ds(8 * c, 8)], 0)
+    mate.start()
+
+    def att_grad(i):
+        rows = span(i, 512)
+        gatt[rows, :] = mm(gmixed[rows, :], w_out[...].reshape(half, depth), NT).astype(BF)
+
+    pump.loop(2, att_grad, 1)
+    keep.wait()
+    mate.wait_recv()
+    s_out.begin()
+    pump.add([end_in])
+    pump.add(s_out.steps())
+    triple_in.wait()
+    for copy in fourth:
+        copy.wait()
+    pump.loop(
+        8,
+        functools.partial(
+            attend_pair_back, triple=area2, mask=mask, lse=lse, gatt=gatt, gtriple=wide, sums=sums, c=c
+        ),
+        2,
+    )
+    norm1_in.wait()
+
+    def qkv_grad(i):
+        cols = span(i, 256)
+        normed = area[0:8, :, cols].reshape(tokens, 256)
+        b_qkv[span(i, 4)] = mm(normed, wide[:, 0 : 3 * half], TN).astype(BF).reshape(4, 64, 3 * half)
+
+    pump.loop(depth // 256, qkv_grad, 0)
+    s_qkv.begin()
+    pump.add([end_out])
+    pump.add(s_qkv.steps())
+    for i in range(4):
+        send_part(i).wait_send()
+
+    def input_grad(i, s):
+        rows = pl.ds(pl.multiple_of(s * length + i * 128, 128), 128)
+        return mm(wide[rows, 0 : 3 * half], w_qkv[...].reshape(depth, 3 * half), NT)
+
+    def first_theirs(i):
+        part[span(i, 128), :] = input_grad(i, 1 - c).astype(BF)
+
+    pump.loop(length // 128, first_theirs, 1)
+    last = pair.copy(part.at[0:length], part_in.at[0:length], 8)
+    last.start()
+    tok_in.wait()
+
+    def first_ours(i):
+        inside = span(i, 128)
+        grad = input_grad(i, c) + part_in[inside, :].astype(F32)
+        normed, inverse = stats(area[8 + i, :, :].astype(F32))
+        scaled = grad * vecs[G1 : G1 + 1, :]
+        gmid[inside, :] = gmid[inside, :] + inverse * (
+            scaled
+            - jnp.mean(scaled, -1, keepdims=True)
+            - normed * jnp.mean(scaled * normed, -1, keepdims=True)
+        )
+        sums[G1 : G1 + 1, :] += jnp.sum(grad * normed, 0, keepdims=True)
+        sums[B1 : B1 + 1, :] += jnp.sum(grad, 0, keepdims=True)
+
+    last.wait_recv()
+    pump.loop(length // 128, first_ours, 1)
+    stores.append(load(gmid, input_o))
+    for w in range(8):
+        for k in range(2):
+            b_vec[2 * w + k, 0:8, :] = sums[:, 128 * w : 128 * (w + 1)]
+    s_vec.begin()
+    rest, pump.queue = pump.queue, []
+    pump.add(rest)
+    pump.add(s_vec.steps())
+    pump.add([end_qkv, end_vec])
+    pump.take(len(pump.queue))
+    pair.copy(f_vec, n_vec, 3).wait_recv()
+    stores.append(load(n_vec, vec_o.at[1]))
+    for s in (s_down, s_in, s_out, s_qkv, s_vec):
         s.drain()
-    half.wait_send()
-    pair[0].wait()
-    pair[1].wait()
-    pair[2].wait_send()
+    mate.wait_send()
+    last.wait_send()
+    pair.copy(f_vec, n_vec, 3).wait_send()
+    pair.copy(f_in.at[theirs], in_o.at[c], 1).wait()
+    pair.copy(f_qkv.at[theirs], qkv_o.at[c], 2).wait()
     for store in stores:
         store.wait()
-    other.wait()
-
-
-def scatter_all(g_qkv, g_out, g_in, g_down, g_vec):
-    bf, f32 = jnp.bfloat16, jnp.float32
-    dq, do, di, dd = g_qkv.shape[2], g_out.shape[2], g_in.shape[2], g_down.shape[2]
-    down = g_down.shape[1]
-    outs = [((2, 32, dq), f32), ((32, do), f32), ((2, 32, di), f32), ((down, dd), f32), ((2, 16, 128), f32)]
-    blocks = [((64, dq), bf), ((32, do), bf), ((64, di), bf), ((down, dd), bf), ((16, 128), f32)]
+
+
+def backward_all(saved, inputs):
+    (
+        qkv, w_out, w_in, w_down, vecs, norm1, triple, att, lse, xhat, norm2, slope, cot, mask, gdown,
+    ) = saved
+    length, depth = inputs.shape
+    tokens = 2 * length
+    dq, do, di = qkv.shape[2], w_out.shape[2], w_in.shape[2]
+    down, dd = w_down.shape[1:]
+    outs = [
+        ((2, 32, dq), F32), ((32, do), F32), ((2, 32, di), F32), ((down, dd), F32), ((2, 16, 128), F32),
+        ((length, depth), F32),
+    ]
+    blocks = [((64, dq), BF), ((32, do), BF), ((64, di), BF), ((down, dd), BF), ((16, 128), F32)]
+    scratch = [((16,) + s, d) for s, d in blocks] + [((15,) + s, d) for s, d in blocks] + [(s, F32) for s, d in blocks]
+    scratch += [
+        ((16, 128), F32), (qkv.shape, BF), (w_out.shape, BF), (w_down.shape, BF), (w_in.shape, BF), (slope.shape, BF),
+        (vecs.shape, F32), (att.shape, BF), (lse.shape, F32), (xhat.shape, BF), (norm2.shape, BF),
+        (cot.shape, BF), (mask.shape, mask.dtype), ((tokens, depth), BF), ((tokens, depth), BF),
+        ((length, depth), F32), ((tokens, depth), BF), ((tokens, depth // 2), BF), (w_out.shape, BF), ((8, depth), F32),
+    ]
+    args = (
+        qkv, w_out, w_in, w_down, vecs, norm1.reshape(8, 128, depth), triple.reshape(16, 64, dq), att, lse, xhat,
+        norm2, slope, cot, mask, gdown, inputs.reshape(4, 128, depth),
+    )
     return pl.pallas_call(
-        scatter_kernel,
+        backward_kernel,
         out_shape=[jax.ShapeDtypeStruct(s, d) for s, d in outs],
-        in_specs=[pl.BlockSpec(memory_space=pl.ANY)] * 5,
-        out_specs=[pl.BlockSpec(memory_space=pl.ANY)] * 5,
-        scratch_shapes=[pltpu.VMEM((16,) + s, d) for s, d in blocks]
-        + [pltpu.VMEM((15,) + s, d) for s, d in blocks]
-        + [pltpu.VMEM(s, f32) for s, d in blocks]
-        + [pltpu.VMEM((16, 128), f32)]
+        in_specs=[pl.BlockSpec(memory_space=pl.ANY)] * len(args),
+        out_specs=[pl.BlockSpec(memory_space=pl.ANY)] * len(outs),
+        scratch_shapes=[pltpu.VMEM(s, d) for s, d in scratch]
         + [
             pltpu.SemaphoreType.DMA((5, 15)),
             pltpu.SemaphoreType.DMA((5, 15)),
-            pltpu.SemaphoreType.DMA((4,)),
-            pltpu.SemaphoreType.DMA((4,)),
-            pltpu.SemaphoreType.DMA((11,)),
+            pltpu.SemaphoreType.DMA((9,)),
+            pltpu.SemaphoreType.DMA((9,)),
+            pltpu.SemaphoreType.DMA((28,)),
         ],
         compiler_params=pltpu.CompilerParams(
-            collective_id=1, has_side_effects=True, vmem_limit_bytes=60 * 1024 * 1024
+            collective_id=1, has_side_effects=True, vmem_limit_bytes=67043328
         ),
-        name="gradients_scatter",
-    )(g_qkv, g_out, g_in, g_down, g_vec)
-
-
-def swap(value):
-    return lax.ppermute(value, "c", [(0, 1), (1, 0)])
-
+        name="backward_scatter",
+    )(*args)
 
 def local_split(
     inputs, segment_ids, cotangent, ln1_gain, ln1_shift, w_qkv, query_bias, value_bias, w_out, out_bias,
     ln2_gain, ln2_shift, w_in, in_bias, w_down, down_bias,
 ):
-    f32, bf = jnp.float32, jnp.bfloat16
     c = lax.axis_index("c")
     narrow = lax.axis_index("x") * 2 + c
-    wide = lax.axis_index("z") * 2 + lax.axis_index("y")
     length, d_model = inputs.shape
     rows = ln1_gain.shape[0]
+    half = d_model // 2
     small = jnp.stack(
         [ln1_gain, ln1_shift, query_bias, value_bias, out_bias, ln2_gain, ln2_shift, down_bias]
-    ).astype(f32)
+    ).astype(F32)
     quarter = jnp.arange(4)[None, :, None] == narrow
     tile = jnp.where(quarter, small[:, None, :], 0.0).reshape(8, 128)
-    tile = jnp.concatenate([tile, in_bias.astype(f32)[None], jnp.zeros((7, 128), f32)])
-    wqkv2 = w_qkv.reshape(rows, 3, 2, d_model // 2).transpose(2, 0, 1, 3).reshape(2, rows, -1)
+    tile = jnp.concatenate([tile, in_bias.astype(F32)[None], jnp.zeros((7, 128), F32)])
+    wqkv2 = w_qkv.reshape(rows, 3, 2, half).transpose(2, 0, 1, 3).reshape(2, rows, -1)
     win2 = w_in.reshape(rows, 16, 2, 128).transpose(2, 0, 1, 3).reshape(2, rows, -1)
     col = jnp.broadcast_to(segment_ids[:, None], (length, 128))
     row = jnp.broadcast_to(segment_ids[None, :], (8, length))
-    half = d_model // 2
-    (
-        qkv_f, out_f, in_f, down_f, vecs, norm_one, triple, attended, lse, x2, r2, norm_two, slope, cot2, mask, grad_down,
-        layer_out,
-    ) = forward_all(wqkv2, w_out, win2, w_down, tile, inputs, cotangent, col, row)
-    g1, g2 = vecs[0], vecs[5]
-    qkv_m = qkv_f.reshape(d_model, -1)
-    out_m = out_f.reshape(-1, d_model)
-    in_m = in_f.reshape(d_model, -1)
-    down_m = down_f.reshape(-1, d_model)
-    cot = cot2.reshape(2 * length, d_model)
-    pick = lambda a, i: lax.dynamic_index_in_dim(a, i, 0, False)
-    x2 = x2.astype(f32)
-    r2 = r2[:, :1]
-    t5 = triple.reshape(2, length, 3, half // HD, HD)
-    q, k, v = t5[:, :, 0], t5[:, :, 1], t5[:, :, 2]
-    scores = jnp.einsum("sqhd,skhd->shqk", q, k, preferred_element_type=f32) * HD ** (-0.5) + mask[:, None]
-    probs = jnp.exp(scores - lse[:, :, : half // HD].transpose(0, 2, 1)[..., None])
-    probs_low = probs.astype(bf)
-    grad_hidden = jnp.einsum("sd,fd->sf", cot, down_m, preferred_element_type=f32)
-    grad_pre = (grad_hidden * slope.astype(f32)).astype(bf)
-    grad_in = jnp.einsum("sd,sf->df", norm_two, grad_pre, preferred_element_type=f32).astype(bf)
-    grad_in_bias = jnp.sum(grad_pre.astype(f32), 0)
-    gn2 = jnp.einsum("sf,df->sd", grad_pre, in_m, preferred_element_type=f32)
-    gn2 = gn2 + swap(gn2)
-    gm = cot.astype(f32) + normalize_back(gn2, x2, r2, g2)
-    grad_mixed = gm.astype(bf)
-    grad_out = jnp.einsum("sd,se->de", attended, grad_mixed, preferred_element_type=f32).astype(bf)
-    grad_att = jnp.einsum("se,de->sd", grad_mixed, out_m, preferred_element_type=f32).astype(bf)
-    ga = grad_att.reshape(2, length, half // HD, HD)
-    gp = jnp.einsum("sqhd,skhd->shqk", ga, v, preferred_element_type=f32)
-    gs = (probs * (gp - jnp.sum(probs * gp, -1, keepdims=True))).astype(bf)
-    gq = jnp.einsum("shqk,skhd->sqhd", gs, k, preferred_element_type=f32) * HD ** (-0.5)
-    gk = jnp.einsum("shqk,sqhd->skhd", gs, q, preferred_element_type=f32) * HD ** (-0.5)
-    gv = jnp.einsum("shqk,sqhd->skhd", probs_low, ga, preferred_element_type=f32)
-    gt = jnp.stack([gq, gk, gv], 2).reshape(2 * length, 3 * half).astype(bf)
-    grad_qkv = jnp.einsum("sd,st->dt", norm_one, gt, preferred_element_type=f32).astype(bf)
-    gqb = jnp.sum(gt[:, :half].astype(f32), 0)
-    gvb = jnp.sum(gt[:, 2 * half :].astype(f32), 0)
-    gn1 = jnp.einsum("st,dt->sd", gt, qkv_m, preferred_element_type=f32).reshape(2, length, d_model)
-    gn1 = pick(gn1, c) + swap(pick(gn1, 1 - c))
-    own = lambda a: pick(a.reshape(2, length, d_model), c)
-    _, x1, r1 = normalize(inputs.astype(f32), g1, g1)
-    grad_input = own(gm) + normalize_back(gn1, x1, r1, g1)
-    put = lambda v: lax.dynamic_update_slice(jnp.zeros((d_model,), f32), v, (c * half,))
-    sums = jnp.stack(
-        [
-            jnp.sum(gn1 * x1, 0), jnp.sum(gn1, 0), put(gqb), put(gvb), jnp.sum(own(grad_mixed).astype(f32), 0),
-            jnp.sum(own(gn2 * x2), 0), jnp.sum(own(gn2), 0), jnp.sum(own(cot).astype(f32), 0),
-        ]
-    )
-    gvec = jnp.repeat(sums.reshape(8, 8, 128).transpose(1, 0, 2), 2, 0)
-    gvec = jnp.concatenate([gvec, grad_in_bias.reshape(16, 1, 128), jnp.zeros((16, 7, 128), f32)], 1)
-    d_qkv, d_out, d_in, d_down, d_vec = scatter_all(
-        grad_qkv.reshape(16, 64, -1), grad_out.reshape(8, 64, -1), grad_in.reshape(16, 64, -1),
-        grad_down.reshape(16, 128, -1), gvec,
-    )
+    *saved, layer_out = forward_all(wqkv2, w_out, win2, w_down, tile, inputs, cotangent, col, row)
+    d_qkv, d_out, d_in, d_down, d_vec, grad_input = backward_all(saved, inputs)
     d_qkv = d_qkv.reshape(2, rows, 3, half).transpose(1, 2, 0, 3).reshape(rows, -1)
     d_in = d_in.reshape(2, rows, 16, 128).transpose(1, 2, 0, 3).reshape(rows, -1)
     eight = (d_vec[0, :8] + d_vec[1, :8]).reshape(8, 4, 32)

time: 485 us -> 323 us (0.67); the launches traced: 476 us -> 322 us
  matrix products: 67.1 us -> 0 us
  local copies, waits for them, and re-layouts: 71.8 us -> 17.4 us
  other arithmetic: 37.7 us -> 1.44 us
  Pallas kernels: 297 us -> 302 us
    dot_general x12 -> x0, matrix products: 67.1 us -> none  [the longest x1 11.6 us: local_split(): gp = jnp.einsum('sqhd,skhd->shqk', ga, v, preferred_element_type=f32)]
    unnamed x64 -> x35, local copies, waits for them, and re-layouts: 24 us -> 5.27 us
    convert_element_type x3 -> x0, other arithmetic: 15.6 us -> none  [the longest x1 12.3 us: local_split(): gs = (probs * (gp - jnp.sum(probs * gp, -1, keepdims=True))).astype(bf)]
    reshape x6 -> x3, local copies, waits for them, and re-layouts: 15.6 us -> 2.18 us  [local_split(): w_qkv.reshape(rows, 3, 2, half).transpose(2, 0, 1, 3).reshape(2, rows, -1)]
    reduce_sum x8 -> x0, other arithmetic: 7.97 us -> none  [the longest x1 2.71 us: local_split(): jnp.sum(gn1 * x1, 0)]
    slice x3 -> x0, local copies, waits for them, and re-layouts: 7.77 us -> none  [the longest x1 5.68 us: local_split(): q, k, v = (t5[:, :, 0], t5[:, :, 1], t5[:, :, 2])]
    mul x1 -> x0, other arithmetic: 7.02 us -> none  [local_split(): gn2 * x2]
    pallas_call x1, Pallas kernels: 153 us -> 158 us  [backward_all(): pl.pallas_call(backward_kernel, out_shape=[jax.ShapeDtypeStruct(s, d) for...]
  transfers between devices with their start and end apart: 2 -> 0, of which waited for: 0 -> 0; matrix products, arithmetic and copies ran while one was open for 13% -> 0% of each run, Pallas kernels for 0% -> 0%
where the time goes in v3:
time: 323 us; the launch traced here: 322 us
  Pallas kernels  302 us (93%)
  local copies, waits for them, and re-layouts  17.4 us (5%)
    pallas_call x1, Pallas kernels, backward_all(): pl.pallas_call(backward_kernel, out_shape=[jax.ShapeDtypeStruct(s, d) for...  158 us
    pallas_call x1, Pallas kernels, forward_all(): pl.pallas_call(forward_kernel, out_shape=[jax.ShapeDtypeStruct(s, d) for...  144 us

profile of v3, /device:TPU:0, one launch (start us, length us, event | category | flops | bytes accessed | tf_op | source)
XLA Modules:
  0.0 322.1 jit_solution(5703123809399095814)
XLA Ops:
  0.6 0.0 copy-start.14
  0.7 0.0 copy-start.6
  0.7 0.0 copy-start.7
  0.7 1.1 reshape.158
  1.9 0.1 copy.46
  2.0 0.9 reshape.159.wqkv_ref
  2.9 1.1 reshape.160
  4.1 0.8 reshape.161.win_ref
  5.0 0.1 broadcast_in_dim.53
  5.1 0.1 broadcast_in_dim.49
  5.2 0.1 broadcast_in_dim.50
  5.3 0.1 pad.2.clone
  5.4 0.7 maximum_maximum_fusion.tile_ref
  6.1 0.8 broadcast_in_dim.58.col_ref
  6.9 0.6 broadcast_in_dim.59.row_ref
  7.5 144.4 %forward_gather.1 = (bf16[16,64,1536]{2,1,0:T(8,128)(2,1)}, bf16[8,64,1024]{2,1,0:T(8,128)(2,1)}, bf16[16,64,2048]{2,1,0:T(8,128)(2,1)}, bf16[16,128,1024]{2,1,0...) custom-call(bf16[2,32,1536]{2,1,0:T(8,128)(2,1)} %reshape.159.wqkv_r, ...), custom_call_target="tpu_custom_call" | custom-call | tf_op jit(solution)/shard_map/forward_gather/pallas_call | solution.py:883
  151.9 158.1 %backward_scatter.1 = (f32[2,32,1536]{2,1,0:T(8,128)}, f32[32,1024]{1,0:T(8,128)}, f32[2,32,2048]{2,1,0:T(8,128)}, f32[128,1024]{1,0:T(8,128)}, f32[2,16,128]{2,1,0:T(8,128)}, /*index=5*/f32[512,1024]{1,0:T(8,128)}) custom-call(bf16[16,64,1536]{2,1,0:T(8,128)(2,1)} %get-tuple-element.38.qkv_ref, bf16[8,64,1024]{2,1,0:T(8,128)(2,1)} %get-tuple-element.39.out_ref, ...), custom_call_target="tpu_custom_call" | custom-call | tf_op jit(solution)/shard_map/backward_scatter/pallas_call | solution.py:1211
  310.0 0.7 slice_add_fusion
  310.7 0.1 add.16
  310.8 0.5 fusion
  311.4 1.3 reshape.165
  312.7 0.3 copy.40
  313.0 1.1 reshape.166
  314.1 0.1 copy.42
  314.2 0.4 copy.41
  314.6 1.2 reshape.168
  315.8 1.2 slice_bitcast_fusion
  317.0 1.3 copy.51
  318.3 1.0 copy-done.1
  319.4 1.3 copy.52
  320.7 0.7 copy.53
  321.4 0.8 copy.54
  (34 shorter events, 0.2 us)
Async XLA Ops:
  0.6 4.3 %copy-start.14 = (bf16[128]{0:T(256)(128)(2,1)S(1)}, bf16[128]{0:T(256)(128)(2,1)}, u32[]{:S(2)}) copy-start(bf16[128]{0:T(256)(128)(2,1)} %param.29) | copy-start | bytes 772
  0.7 4.3 %copy-start.6 = (bf16[32]{0:T(256)(128)(2,1)S(1)}, bf16[32]{0:T(256)(128)(2,1)}, u32[]{:S(2)}) copy-start(bf16[32]{0:T(256)(128)(2,1)} %param.19) | copy-start | bytes 196
  0.7 4.3 %copy-start.7 = (bf16[32]{0:T(256)(128)(2,1)S(1)}, bf16[32]{0:T(256)(128)(2,1)}, u32[]{:S(2)}) copy-start(bf16[32]{0:T(256)(128)(2,1)} %param.20) | copy-start | bytes 196
  0.7 4.3 %copy-start.8 = (bf16[32]{0:T(256)(128)(2,1)S(1)}, bf16[32]{0:T(256)(128)(2,1)}, u32[]{:S(2)}) copy-start(bf16[32]{0:T(256)(128)(2,1)} %param.22) | copy-start | bytes 196
  0.7 4.3 %copy-start.9 = (bf16[32]{0:T(256)(128)(2,1)S(1)}, bf16[32]{0:T(256)(128)(2,1)}, u32[]{:S(2)}) copy-start(bf16[32]{0:T(256)(128)(2,1)} %param.23) | copy-start | bytes 196
  0.7 4.3 %copy-start.10 = (bf16[32]{0:T(256)(128)(2,1)S(1)}, bf16[32]{0:T(256)(128)(2,1)}, u32[]{:S(2)}) copy-start(bf16[32]{0:T(256)(128)(2,1)} %param.25) | copy-start | bytes 196
  0.7 4.3 %copy-start.11 = (bf16[32]{0:T(256)(128)(2,1)S(1)}, bf16[32]{0:T(256)(128)(2,1)}, u32[]{:S(2)}) copy-start(bf16[32]{0:T(256)(128)(2,1)} %param.26) | copy-start | bytes 196
  0.7 4.3 %copy-start.12 = (bf16[32]{0:T(256)(128)(2,1)S(1)}, bf16[32]{0:T(256)(128)(2,1)}, u32[]{:S(2)}) copy-start(bf16[32]{0:T(256)(128)(2,1)} %param.27) | copy-start | bytes 196
  0.7 4.3 %copy-start.13 = (bf16[32]{0:T(256)(128)(2,1)S(1)}, bf16[32]{0:T(256)(128)(2,1)}, u32[]{:S(2)}) copy-start(bf16[32]{0:T(256)(128)(2,1)} %param.31) | copy-start | bytes 196
  0.7 5.3 %copy-start.5 = (s32[512]{0:T(512)S(1)}, s32[512]{0:T(512)}, u32[]{:S(2)}) copy-start(s32[512]{0:T(512)} %param.17) | copy-start | bytes 6148
  310.0 4.1 %copy-start.3 = (f32[2,32,2048]{2,1,0:T(8,128)S(1)}, f32[2,32,2048]{2,1,0:T(8,128)}, u32[]{:S(2)}) copy-start(f32[2,32,2048]{2,1,0:T(8,128)} %get-tuple-element.57) | copy-start | bytes 1572868
  314.1 3.0 copy-start
  317.0 2.3 copy-start.1
  319.4 1.3 copy-start.4
  319.4 2.0 copy-start.2

commit v4 on v3

--- a/solution.py
+++ b/solution.py
@@ -403,6 +403,7 @@
 
 
 Z_AT, X_AT, Y_AT, D_AT = -1, 3, 7, 11
+FAR_FIRST, BY_Y = (3, 2, 1, 0), (3, 1)
 
 
 class Gather:
@@ -429,7 +430,7 @@
         self.copy(block, slot, dict(dx=1)).wait_recv()
 
     def begin(self):
-        for dz in (3, 2, 1):
+        for dz in (1, 2, 3):
             self.send({}, Z_AT + dz, dict(dz=dz))
         self.send({}, X_AT, dict(dx=1))
         self.send({}, Y_AT, dict(dy=1))
@@ -513,22 +514,16 @@
         self.add(at, slots, write)
 
     def begin(self):
-        for dz in (1, 2, 3, 0):
-            if dz < 2:
-                self.send(dict(dz=dz, dy=1, dx=1), D_AT + dz, dict(dy=1))
-                self.send(dict(dz=dz, dy=1), Y_AT + dz, dict(dy=1))
-            else:
-                self.send(dict(dz=dz, dy=1, dx=1), D_AT + dz, dict(dx=1))
-                self.send(dict(dz=dz, dx=1), X_AT + dz, dict(dx=1))
+        for dz in FAR_FIRST:
+            to = dict(dy=1) if dz in BY_Y else dict(dx=1)
+            self.send(dict(dz=dz, dy=1, dx=1), D_AT + dz, to)
+            self.send(dict(dz=dz, **to), (Y_AT if dz in BY_Y else X_AT) + dz, to)
 
     def across(self, dz):
+        to = dict(dx=1) if dz in BY_Y else dict(dy=1)
         self.wait(D_AT + dz)
-        if dz < 2:
-            self.merge(dict(dz=dz, dx=1), (D_AT + dz,))
-            self.send(dict(dz=dz, dx=1), X_AT + dz, dict(dx=1))
-        else:
-            self.merge(dict(dz=dz, dy=1), (D_AT + dz,))
-            self.send(dict(dz=dz, dy=1), Y_AT + dz, dict(dy=1))
+        self.merge(dict(dz=dz, **to), (D_AT + dz,))
+        self.send(dict(dz=dz, **to), (X_AT if dz in BY_Y else Y_AT) + dz, to)
 
     def along(self, dz):
         self.wait(X_AT + dz)
@@ -542,11 +537,11 @@
             self.wait(Z_AT + dz)
         self.add(self.p.index(), (X_AT, Y_AT, Z_AT + 1, Z_AT + 2, Z_AT + 3), write)
 
-    def steps(self):
-        for dz in (1, 2, 3, 0):
-            yield functools.partial(self.across, dz)
-        for dz in (1, 2, 3, 0):
-            yield functools.partial(self.along, dz)
+    def acrosses(self):
+        return [functools.partial(self.across, dz) for dz in FAR_FIRST]
+
+    def alongs(self):
+        return [functools.partial(self.along, dz) for dz in FAR_FIRST]
 
     def drain(self):
         for block, slot, to in self.left:
@@ -670,9 +665,9 @@
 def forward_kernel(
     wqkv_ref, wout_ref, win_ref, wdown_ref, tile_ref, tok_ref, cot_ref, col_ref, row_ref,
     qkv_o, out_o, in_o, down_o, vecs_o, norm1_o, triple_o, att_o, lse_o, xhat_o, norm2_o, slope_o, cot_o,
-    mask_o, gdown_o, layer_o,
+    mask_o, gdown_o, hidden_o, mid_o,
     w_qkv, w_nat, w_out, w_in, w_down, tiles, tile, tile_in, tok, cot, col, row, mask,
-    vecs, hshift, tshift, norm1, triple, att, lse, mid, part, part_in, last_in, norm2, xhat, hidden, slope, gdown,
+    vecs, hshift, tshift, norm1, triple, att, lse, mid, part, part_in, norm2, xhat, hidden, slope, gdown,
     sent, came, pair_sent, pair_came, local,
 ):
     p = Place()
@@ -799,8 +794,8 @@
         norm2[rows, :] = (normed * vecs[G2 : G2 + 1, :] + vecs[B2 : B2 + 1, :]).astype(BF)
 
     pump.loop(4, second_norm, 0)
-    stores += [load(xhat, xhat_o), load(lse, lse_o), load(norm2, norm2_o)]
-    pump.take(max(len(pump.queue) - 7, 0))
+    stores += [load(xhat, xhat_o), load(lse, lse_o), load(norm2, norm2_o), load(mid.at[span(c, length)], mid_o)]
+    pump.take(max(len(pump.queue) - 4, 0))
     g_in.finish()
     stores.append(load(w_in, in_o))
 
@@ -815,8 +810,8 @@
     loads[6].wait()
     swaps[6].wait_recv()
     stores.append(load(cot, cot_o))
-    pump.loop(hidden.shape[1] // 256, expand, 1)
-    stores.append(load(slope, slope_o))
+    pump.loop(hidden.shape[1] // 256, expand, 0)
+    stores += [load(slope, slope_o), load(hidden, hidden_o)]
 
     def down_grad(i):
         cols = span(i, 256)
@@ -830,33 +825,11 @@
     stores.append(load(w_down, down_o))
     for i in range(4):
         send_part(i).wait_send()
-    yours, ours = span(1 - c, length), span(c, length)
-    units = hidden.shape[1]
-
-    def theirs(i):
-        cols = span(i, 256)
-        w = w_down[:, :, cols].reshape(units, 256)
-        part[yours, cols] = mm(hidden[yours, :], w).astype(BF)
-
-    lax.fori_loop(0, depth // 256, lambda i, carry: (theirs(i), carry)[1], 0)
-    last = pair.copy(part.at[yours], last_in, 12)
-    last.start()
-
-    def contract(i):
-        cols = span(i, 256)
-        w = w_down[:, :, cols].reshape(units, 256)
-        mid[ours, cols] = mid[ours, cols] + mm(hidden[ours, :], w) + vecs[DB : DB + 1, cols]
-
-    lax.fori_loop(0, depth // 256, lambda i, carry: (contract(i), carry)[1], 0)
-    last.wait_recv()
-    mid[ours, :] = mid[ours, :] + last_in[...].astype(F32)
-    stores.append(load(mid.at[ours], layer_o))
     for g in (g_vec, g_qkv, g_out, g_in, g_down):
         g.drain()
     for copy in swaps:
         copy.wait_send()
     half.wait_send()
-    last.wait_send()
     for store in stores:
         store.wait()
 
@@ -869,7 +842,8 @@
         ((16, 64, dq), BF), ((8, 64, do), BF), ((16, 64, di), BF), ((16,) + w_down.shape, BF),
         ((8, depth), F32), ((tokens, depth), BF), ((tokens, dq), BF), ((tokens, dq // 3), BF), ((2, length, 128), F32),
         ((tokens, depth), BF), ((tokens, depth), BF), ((tokens, di), BF), ((2, length, depth), BF),
-        ((2, length, length), BF), ((16,) + w_down.shape, BF), ((length, depth), F32),
+        ((2, length, length), BF), ((16,) + w_down.shape, BF), ((tokens, di), BF),
+        ((length, depth), F32),
     ]
     scratch = [
         ((16, 64, dq), BF), ((16, 32, do), BF), ((8, 64, do), BF), ((16, 64, di), BF), ((16,) + w_down.shape, BF),
@@ -877,7 +851,7 @@
         ((2, length, 128), jnp.int32), ((2, 8, length), jnp.int32), ((2, length, length), BF),
         ((8, depth), F32), ((8, di), F32), ((8, dq), F32), ((tokens, depth), BF), ((tokens, dq), BF),
         ((tokens, dq // 3), BF), ((2, length, 128), F32), ((tokens, depth), F32), ((tokens, depth), BF),
-        ((tokens, depth), BF), ((length, depth), BF), ((tokens, depth), BF), ((tokens, depth), BF),
+        ((tokens, depth), BF), ((tokens, depth), BF), ((tokens, depth), BF),
         ((tokens, di), BF), ((tokens, di), BF), ((16,) + w_down.shape, BF),
     ]
     return pl.pallas_call(
@@ -889,8 +863,8 @@
         + [
             pltpu.SemaphoreType.DMA((5, 15)),
             pltpu.SemaphoreType.DMA((5, 15)),
-            pltpu.SemaphoreType.DMA((13,)),
-            pltpu.SemaphoreType.DMA((13,)),
+            pltpu.SemaphoreType.DMA((12,)),
+            pltpu.SemaphoreType.DMA((12,)),
             pltpu.SemaphoreType.DMA((32,)),
         ],
         compiler_params=pltpu.CompilerParams(
@@ -948,8 +922,8 @@
 
 def backward_kernel(
     qkv_ref, out_ref, in_ref, down_ref, vecs_ref, norm1_ref, triple_ref, att_ref, lse_ref, xhat_ref, norm2_ref,
-    slope_ref, cot_ref, mask_ref, gdown_ref, tok_ref,
-    qkv_o, out_o, in_o, down_o, vec_o, input_o,
+    slope_ref, cot_ref, mask_ref, gdown_ref, hidden_ref, mid_ref, tok_ref,
+    qkv_o, out_o, in_o, down_o, vec_o, input_o, layer_o,
     b_qkv, b_out, b_in, b_down, b_vec,
     l_qkv, l_out, l_in, l_down, l_vec,
     f_qkv, f_out, f_in, f_down, f_vec, n_vec,
@@ -972,9 +946,15 @@
         return Later(lambda: pltpu.make_async_copy(src, dst, local.at[slot]).wait())
 
     in_down = load(gdown_ref, b_down)
-    first = [load(down_ref, area), load(cot_ref, cot), load(slope_ref, wide)]
-    second = [load(norm2_ref, norm2), load(in_ref, area2)]
-    third = [load(xhat_ref, xhat), load(lse_ref, lse), load(vecs_ref, vecs), load(att_ref, att), load(out_ref, w_out)]
+    first = [
+        load(down_ref, area),
+        load(hidden_ref.at[:, 0:depth], part),
+        load(hidden_ref.at[:, depth:], gmixed),
+        load(mid_ref, gmid),
+        load(vecs_ref, vecs),
+    ]
+    second = [load(cot_ref, cot), load(slope_ref, wide), load(norm2_ref, norm2), load(in_ref, area2)]
+    third = [load(lse_ref, lse), load(att_ref, att), load(out_ref, w_out)]
     fourth = [load(mask_ref, mask), load(qkv_ref, w_qkv)]
     p.greet()
     pair = Pair(p, pair_sent, pair_came)
@@ -1014,14 +994,34 @@
 
     def end_vec():
         s_vec.total(put(f_vec))
-        pair.copy(f_vec, n_vec, 3).start()
+        pair.copy(f_vec, n_vec, 9).start()
         stores.append(load(f_vec, vec_o.at[0]))
 
     pump = Pump()
-    pump.add(s_down.steps())
     sums[...] = jnp.zeros_like(sums)
     b_vec[...] = jnp.zeros_like(b_vec)
     for copy in first:
+        copy.wait()
+    ours, yours = span(c, length), span(1 - c, length)
+
+    def contract(rows, cols):
+        w = area[:, :, cols].reshape(2, depth, 256)
+        return mm(part[rows, :], w[0]) + mm(gmixed[rows, :], w[1])
+
+    def out_theirs(i):
+        cols = span(i, 256)
+        xhat[length:tokens, cols] = contract(yours, cols).astype(BF)
+
+    pump.loop(depth // 256, out_theirs, 0)
+    rest = pair.copy(xhat.at[length:tokens], xhat.at[0:length], 3)
+    rest.start()
+
+    def out_ours(i):
+        cols = span(i, 256)
+        gmid[:, cols] = gmid[:, cols] + contract(ours, cols) + vecs[DB : DB + 1, cols]
+
+    pump.loop(depth // 256, out_ours, 0)
+    for copy in second:
         copy.wait()
 
     def hidden_grad(i):
@@ -1034,19 +1034,21 @@
         b_vec[2 * i, 8:9, :] = total[:, 0:128]
         b_vec[2 * i + 1, 8:9, :] = total[:, 128:256]
 
-    pump.loop(units // 256, hidden_grad, 1)
-    for copy in second:
-        copy.wait()
+    pump.loop(units // 256, hidden_grad, 0)
 
     def in_grad(i):
         cols = span(i, 256)
         b_in[span(i, 4)] = mm(norm2[:, cols], wide[...], TN).astype(BF).reshape(4, 64, units)
 
     pump.loop(depth // 256, in_grad, 0)
-    pump.take(len(pump.queue))
+    pump.add(s_down.acrosses())
+    pump.take(4)
     s_in.begin()
-    pump.add([end_down])
-    pump.add(s_in.steps())
+    rest.wait_recv()
+    gmid[...] = gmid[...] + xhat[0:length, :].astype(F32)
+    layer = load(gmid, layer_o)
+    rest.wait_send()
+    third.append(load(xhat_ref, xhat))
 
     def send_part(i):
         rows = span(i, 256)
@@ -1057,7 +1059,7 @@
         part[rows, :] = mm(wide[rows, :], area2[...].reshape(depth, units), NT).astype(BF)
         send_part(i).start()
 
-    pump.loop(4, norm_grad, 1)
+    pump.loop(4, norm_grad, 0)
     norm1_in = load(norm1_ref, area.at[0:8])
     tok_in = load(tok_ref, area.at[8:12])
     triple_in = load(triple_ref, area2.at[:, :, 0 : 3 * half])
@@ -1088,6 +1090,7 @@
 
     for i in range(4):
         send_part(i).wait_recv()
+    layer.wait()
     pump.loop(length // 128, functools.partial(middle_rows, ours=True), 0)
     pump.loop(length // 128, functools.partial(middle_rows, ours=False), 0)
 
@@ -1095,7 +1098,7 @@
         cols = span(i, 256)
         gout[span(i, 4)] = mm(att[:, cols], gmixed[...], TN).astype(BF).reshape(4, 64, depth)
 
-    pump.loop(half // 256, out_grad, 1)
+    pump.loop(half // 256, out_grad, 0)
     keep = load(gout.at[:, mine], b_out.at[pl.ds(8 * c, 8)])
     mate = pair.copy(gout.at[:, theirs], b_out.at[pl.ds(8 * c, 8)], 0)
     mate.start()
@@ -1104,12 +1107,13 @@
         rows = span(i, 512)
         gatt[rows, :] = mm(gmixed[rows, :], w_out[...].reshape(half, depth), NT).astype(BF)
 
-    pump.loop(2, att_grad, 1)
+    pump.loop(2, att_grad, 0)
     keep.wait()
     mate.wait_recv()
+    pump.add(s_down.alongs())
+    pump.take(4)
     s_out.begin()
-    pump.add([end_in])
-    pump.add(s_out.steps())
+    pump.add(s_in.acrosses())
     triple_in.wait()
     for copy in fourth:
         copy.wait()
@@ -1118,7 +1122,7 @@
         functools.partial(
             attend_pair_back, triple=area2, mask=mask, lse=lse, gatt=gatt, gtriple=wide, sums=sums, c=c
         ),
-        2,
+        1,
     )
     norm1_in.wait()
 
@@ -1129,8 +1133,8 @@
 
     pump.loop(depth // 256, qkv_grad, 0)
     s_qkv.begin()
-    pump.add([end_out])
-    pump.add(s_qkv.steps())
+    pump.add([end_down])
+    pump.add(s_out.acrosses())
     for i in range(4):
         send_part(i).wait_send()
 
@@ -1141,7 +1145,7 @@
     def first_theirs(i):
         part[span(i, 128), :] = input_grad(i, 1 - c).astype(BF)
 
-    pump.loop(length // 128, first_theirs, 1)
+    pump.loop(length // 128, first_theirs, 0)
     last = pair.copy(part.at[0:length], part_in.at[0:length], 8)
     last.start()
     tok_in.wait()
@@ -1160,24 +1164,25 @@
         sums[B1 : B1 + 1, :] += jnp.sum(grad, 0, keepdims=True)
 
     last.wait_recv()
-    pump.loop(length // 128, first_ours, 1)
+    pump.loop(length // 128, first_ours, 0)
     stores.append(load(gmid, input_o))
     for w in range(8):
         for k in range(2):
             b_vec[2 * w + k, 0:8, :] = sums[:, 128 * w : 128 * (w + 1)]
     s_vec.begin()
-    rest, pump.queue = pump.queue, []
-    pump.add(rest)
-    pump.add(s_vec.steps())
-    pump.add([end_qkv, end_vec])
+    for steps in (
+        s_in.alongs(), s_qkv.acrosses(), s_vec.acrosses(), s_out.alongs(), [end_in, end_out], s_vec.alongs(),
+        s_qkv.alongs(), [end_vec, end_qkv],
+    ):
+        pump.add(steps)
     pump.take(len(pump.queue))
-    pair.copy(f_vec, n_vec, 3).wait_recv()
+    pair.copy(f_vec, n_vec, 9).wait_recv()
     stores.append(load(n_vec, vec_o.at[1]))
     for s in (s_down, s_in, s_out, s_qkv, s_vec):
         s.drain()
     mate.wait_send()
     last.wait_send()
-    pair.copy(f_vec, n_vec, 3).wait_send()
+    pair.copy(f_vec, n_vec, 9).wait_send()
     pair.copy(f_in.at[theirs], in_o.at[c], 1).wait()
     pair.copy(f_qkv.at[theirs], qkv_o.at[c], 2).wait()
     for store in stores:
@@ -1186,7 +1191,7 @@
 
 def backward_all(saved, inputs):
     (
-        qkv, w_out, w_in, w_down, vecs, norm1, triple, att, lse, xhat, norm2, slope, cot, mask, gdown,
+        qkv, w_out, w_in, w_down, vecs, norm1, triple, att, lse, xhat, norm2, slope, cot, mask, gdown, hidden, mid,
     ) = saved
     length, depth = inputs.shape
     tokens = 2 * length
@@ -1194,7 +1199,7 @@
     down, dd = w_down.shape[1:]
     outs = [
         ((2, 32, dq), F32), ((32, do), F32), ((2, 32, di), F32), ((down, dd), F32), ((2, 16, 128), F32),
-        ((length, depth), F32),
+        ((length, depth), F32), ((length, depth), F32),
     ]
     blocks = [((64, dq), BF), ((32, do), BF), ((64, di), BF), ((down, dd), BF), ((16, 128), F32)]
     scratch = [((16,) + s, d) for s, d in blocks] + [((15,) + s, d) for s, d in blocks] + [(s, F32) for s, d in blocks]
@@ -1206,7 +1211,7 @@
     ]
     args = (
         qkv, w_out, w_in, w_down, vecs, norm1.reshape(8, 128, depth), triple.reshape(16, 64, dq), att, lse, xhat,
-        norm2, slope, cot, mask, gdown, inputs.reshape(4, 128, depth),
+        norm2, slope, cot, mask, gdown, hidden, mid, inputs.reshape(4, 128, depth),
     )
     return pl.pallas_call(
         backward_kernel,
@@ -1217,9 +1222,9 @@
         + [
             pltpu.SemaphoreType.DMA((5, 15)),
             pltpu.SemaphoreType.DMA((5, 15)),
-            pltpu.SemaphoreType.DMA((9,)),
-            pltpu.SemaphoreType.DMA((9,)),
-            pltpu.SemaphoreType.DMA((28,)),
+            pltpu.SemaphoreType.DMA((10,)),
+            pltpu.SemaphoreType.DMA((10,)),
+            pltpu.SemaphoreType.DMA((32,)),
         ],
         compiler_params=pltpu.CompilerParams(
             collective_id=1, has_side_effects=True, vmem_limit_bytes=67043328
@@ -1246,8 +1251,8 @@
     win2 = w_in.reshape(rows, 16, 2, 128).transpose(2, 0, 1, 3).reshape(2, rows, -1)
     col = jnp.broadcast_to(segment_ids[:, None], (length, 128))
     row = jnp.broadcast_to(segment_ids[None, :], (8, length))
-    *saved, layer_out = forward_all(wqkv2, w_out, win2, w_down, tile, inputs, cotangent, col, row)
-    d_qkv, d_out, d_in, d_down, d_vec, grad_input = backward_all(saved, inputs)
+    saved = forward_all(wqkv2, w_out, win2, w_down, tile, inputs, cotangent, col, row)
+    d_qkv, d_out, d_in, d_down, d_vec, grad_input, layer_out = backward_all(saved, inputs)
     d_qkv = d_qkv.reshape(2, rows, 3, half).transpose(1, 2, 0, 3).reshape(rows, -1)
     d_in = d_in.reshape(2, rows, 16, 128).transpose(1, 2, 0, 3).reshape(rows, -1)
     eight = (d_vec[0, :8] + d_vec[1, :8]).reshape(8, 4, 32)

time: 323 us -> 281 us (0.87)
  Pallas kernels: 302 us -> 261 us
    pallas_call x1, Pallas kernels: 158 us -> 133 us  [backward_all(): pl.pallas_call(backward_kernel, out_shape=[jax.ShapeDtypeStruct(s, d) for...]
    pallas_call x1, Pallas kernels: 144 us -> 128 us  [forward_all(): pl.pallas_call(forward_kernel, out_shape=[jax.ShapeDtypeStruct(s, d) for...]
where the time goes in v4:
time: 281 us; the launch traced here: 280 us
  Pallas kernels  261 us (93%)
  local copies, waits for them, and re-layouts  17.4 us (6%)
    pallas_call x1, Pallas kernels, backward_all(): pl.pallas_call(backward_kernel, out_shape=[jax.ShapeDtypeStruct(s, d) for...  133 us
    pallas_call x1, Pallas kernels, forward_all(): pl.pallas_call(forward_kernel, out_shape=[jax.ShapeDtypeStruct(s, d) for...  128 us
    unnamed x19, local copies, waits for them, and re-layouts  6.33 us

profile of v4, /device:TPU:0, one launch (start us, length us, event | category | flops | bytes accessed | tf_op | source)
XLA Modules:
  0.0 280.4 jit_solution(9921838845608178303)
XLA Ops:
  0.7 0.1 broadcast_in_dim.49
  0.7 0.1 broadcast_in_dim.50
  0.8 0.8 stack.35
  1.6 0.1 broadcast_in_dim.53
  1.7 0.1 pad.2.clone
  1.8 0.7 bitcast_convert_fusion
  2.5 0.7 maximum_maximum_fusion.tile_ref
  3.1 1.1 reshape.160
  4.3 0.8 reshape.161.win_ref
  5.1 1.1 reshape.158
  6.2 0.1 copy.46
  6.3 0.9 reshape.159.wqkv_ref
  7.3 0.8 broadcast_in_dim.58.col_ref
  8.1 0.6 broadcast_in_dim.59.row_ref
  8.7 127.9 %forward_gather.1 = (bf16[16,64,1536]{2,1,0:T(8,128)(2,1)}, bf16[8,64,1024]{2,1,0:T(8,128)(2,1)}, bf16[16,64,2048]{2,1,0:T(8,128)(2,1)}, bf16[16,128,1024]{2,1,0...) custom-call(bf16[2,32,1536]{2,1,0:T(8,128)(2,1)} %reshape.159.wqkv_r, ...), custom_call_target="tpu_custom_call" | custom-call | tf_op jit(solution)/shard_map/forward_gather/pallas_call | solution.py:857
  136.6 132.9 %backward_scatter.1 = (f32[2,32,1536]{2,1,0:T(8,128)}, f32[32,1024]{1,0:T(8,128)}, f32[2,32,2048]{2,1,0:T(8,128)}, f32[128,1024]{1,0:T(8,128)}, f32[2,16,128]{2,...) custom-call(bf16[16,64,1536]{2,1,0:T(8,128)(2,1)} %get-tuple-element.39.qkv_ref, ...), custom_call_target="tpu_custom_call" | custom-call | tf_op jit(solution)/shard_map/backward_scatter/pallas_call | solution.py:1216
  269.6 1.2 copy.42
  270.8 0.4 copy.41
  271.2 0.0 copy-start.6
  271.2 0.0 copy-start.1
  271.2 1.2 reshape.168
  272.5 0.3 reshape.165
  272.7 0.3 copy.40
  273.1 1.1 reshape.166
  274.1 0.1 add.16
  274.2 0.5 fusion
  274.8 0.5 slice_bitcast_fusion
  275.3 1.3 copy.51
  276.6 1.0 copy-done
  277.6 1.3 copy.52
  279.0 0.7 copy.53
  279.6 0.8 copy.54
  (18 shorter events, 0.1 us)
Async XLA Ops:
  0.6 6.6 %copy-start.5 = (s32[512]{0:T(512)S(1)}, s32[512]{0:T(512)}, u32[]{:S(2)}) copy-start(s32[512]{0:T(512)} %param.17) | copy-start | bytes 6148
  269.6 2.9 %copy-start.3 = (f32[2,32,1536]{2,1,0:T(8,128)S(1)}, f32[2,32,1536]{2,1,0:T(8,128)}, u32[]{:S(2)}) copy-start(f32[2,32,1536]{2,1,0:T(8,128)} %get-tuple-element.59) | copy-start | bytes 1179652
  271.2 2.9 %copy-start.6 = (f32[2,16,128]{2,1,0:T(8,128)S(1)}, f32[2,16,128]{2,1,0:T(8,128)}, u32[]{:S(2)}) copy-start(f32[2,16,128]{2,1,0:T(8,128)} %get-tuple-element.58) | copy-start | bytes 49156
  271.2 4.1 %copy-start.1 = (f32[512,1024]{1,0:T(8,128)S(1)}, f32[512,1024]{1,0:T(8,128)}, u32[]{:S(2)}) copy-start(f32[512,1024]{1,0:T(8,128)} %get-tuple-element.86) | copy-start | bytes 6291460
  275.3 2.3 copy-start
  277.6 1.3 copy-start.4
  277.6 2.0 copy-start.2

commit v5 on v4

--- a/solution.py
+++ b/solution.py
@@ -435,6 +435,12 @@
         self.send({}, X_AT, dict(dx=1))
         self.send({}, Y_AT, dict(dy=1))
 
+    def alongs(self, *dzs):
+        return [functools.partial(self.along, dz) for dz in dzs]
+
+    def acrosses(self, *dzs):
+        return [functools.partial(self.across, dz) for dz in dzs]
+
     def along(self, dz):
         self.wait(dict(dz=dz), Z_AT + dz)
         self.send(dict(dz=dz), X_AT + dz, dict(dx=1))
@@ -457,15 +463,41 @@
         for dz in range(4):
             self.wait(dict(dz=dz, dy=1, dx=1), D_AT + dz)
 
-    def steps(self):
-        for dz in (1, 2, 3):
-            yield functools.partial(self.along, dz)
-        for dz in (0, 1, 2, 3):
-            yield functools.partial(self.across, dz)
-
     def drain(self):
         for block, slot, to in self.left:
             self.copy(block, slot, to).wait_send()
+
+
+PLANE = ({}, dict(dx=1), dict(dy=1), dict(dx=1, dy=1))
+
+
+def line_slot(dz, k):
+    return 4 * dz - 1 + k
+
+
+class PlaneFirstGather(Gather):
+    def line(self, k):
+        for dz in (1, 2, 3):
+            self.send(PLANE[k], line_slot(dz, k), dict(dz=dz))
+
+    def begin(self):
+        self.send({}, 0, dict(dx=1))
+        self.send({}, 1, dict(dy=1))
+        self.line(0)
+
+    def steps(self):
+        def step(k):
+            self.wait(PLANE[k], k - 1)
+            if k == 1:
+                self.send(PLANE[1], 2, dict(dy=1))
+            self.line(k)
+
+        return [functools.partial(step, k) for k in (1, 2, 3)]
+
+    def finish(self):
+        for dz in (1, 2, 3):
+            for k in range(4):
+                self.wait(dict(dz=dz, **PLANE[k]), line_slot(dz, k))
 
 
 class Scatter:
@@ -537,48 +569,64 @@
             self.wait(Z_AT + dz)
         self.add(self.p.index(), (X_AT, Y_AT, Z_AT + 1, Z_AT + 2, Z_AT + 3), write)
 
-    def acrosses(self):
-        return [functools.partial(self.across, dz) for dz in FAR_FIRST]
-
-    def alongs(self):
-        return [functools.partial(self.along, dz) for dz in FAR_FIRST]
+    def acrosses(self, *dzs):
+        return [functools.partial(self.across, dz) for dz in dzs or FAR_FIRST]
+
+    def alongs(self, *dzs):
+        return [functools.partial(self.along, dz) for dz in dzs or FAR_FIRST]
 
     def drain(self):
         for block, slot, to in self.left:
             self.copy(block, slot, to).wait_send()
 
 
-class Pump:
-    def __init__(self):
-        self.queue = []
-
-    def add(self, steps):
-        self.queue.extend(steps)
-
-    def take(self, count):
-        now, self.queue = self.queue[:count], self.queue[count:]
-        for step in now:
+class LineFirstScatter(Scatter):
+    def begin(self):
+        for k in (3, 2, 1, 0):
+            for dz in (3, 2, 1):
+                self.send(dict(dz=dz, **PLANE[k]), line_slot(dz, k), dict(dz=dz))
+
+    def lines(self, k):
+        slots = [line_slot(dz, k) for dz in (1, 2, 3)]
+        for slot in slots:
+            self.wait(slot)
+        if k == 1:
+            self.wait(2)
+            slots.append(2)
+        if k:
+            self.merge(PLANE[k], slots)
+            self.send(PLANE[k], k - 1, dict(dx=1) if k == 1 else dict(dy=1))
+
+    def steps(self):
+        return [functools.partial(self.lines, k) for k in (3, 2, 1)]
+
+    def total(self, write):
+        self.lines(0)
+        self.wait(0)
+        self.wait(1)
+        self.add(self.p.index(), (0, 1, line_slot(1, 0), line_slot(2, 0), line_slot(3, 0)), write)
+
+
+def run(*steps):
+    for step in steps:
+        if isinstance(step, (list, tuple)):
+            run(*step)
+        else:
             step()
 
-    def loop(self, trips, body, per_trip=0):
-        groups = []
-        for i in range(trips):
-            groups.append(self.queue[:per_trip])
-            self.queue = self.queue[per_trip:]
-
-        def trip(i, carry):
-            body(i)
-            for k, group in enumerate(groups):
-                if group:
-
-                    @pl.when(i == k)
-                    def _(group=group):
-                        for step in group:
-                            step()
-
-            return carry
-
-        lax.fori_loop(0, trips, trip, 0)
+
+def loop(trips, body, after=()):
+    def trip(i, carry):
+        body(i)
+        for k, steps in dict(after).items():
+
+            @pl.when(i == k)
+            def _(steps=steps):
+                run(steps)
+
+        return carry
+
+    lax.fori_loop(0, trips, trip, 0)
 
 
 NN = (((1,), (0,)), ((), ()))
@@ -601,6 +649,14 @@
     centred = v - average
     inverse = lax.rsqrt(jnp.mean(centred * centred, -1, keepdims=True) + EPS)
     return centred * inverse, inverse
+
+
+def third_at(pair, third):
+    return pair * 384 + third * 128
+
+
+def third_of(pair, third, core, depth):
+    return third * depth + core * (depth // 2) + pair * 128
 
 
 def build_mask(mask, seg_col, seg_row):
@@ -627,13 +683,21 @@
         hidden_shift[0:1, 128 * j : 128 * (j + 1)] = tiles[j, 8:9, :]
     half = vecs.shape[1] // 2
     first = c == 0
-    triple_shift[0:1, 0:half] = jnp.where(first, vecs[2:3, 0:half], vecs[2:3, half:])
-    triple_shift[0:1, half : 2 * half] = jnp.zeros((1, half), F32)
-    triple_shift[0:1, 2 * half :] = jnp.where(first, vecs[3:4, 0:half], vecs[3:4, half:])
+    for pair in range(half // 128):
+        low, high = 128 * pair, half + 128 * pair
+        for third, row in enumerate((QB, None, VB)):
+            at = third_at(pair, third)
+            if row is None:
+                triple_shift[0:1, at : at + 128] = jnp.zeros((1, 128), F32)
+            else:
+                triple_shift[0:1, at : at + 128] = jnp.where(
+                    first, vecs[row : row + 1, low : low + 128], vecs[row : row + 1, high : high + 128]
+                )
 
 
 G1, B1, QB, VB, OB, G2, B2, DB = range(8)
 INV_AT = 64
+LINE_FROM = 640
 
 
 def attend_pair(i, triple, mask, attended, lse):
@@ -642,9 +706,7 @@
     pairs = half // 128
     s, pair = i // pairs, lax.rem(i, pairs)
     rows = span(s, length)
-    q = triple[rows, pl.ds(pl.multiple_of(pair * 128, 128), 128)]
-    k = triple[rows, pl.ds(pl.multiple_of(half + pair * 128, 128), 128)]
-    v = triple[rows, pl.ds(pl.multiple_of(2 * half + pair * 128, 128), 128)]
+    q, k, v = (triple[rows, pl.ds(pl.multiple_of(third_at(pair, t), 128), 128)] for t in range(3))
     lane = lax.broadcasted_iota(jnp.int32, (length, 128), 1)
     low = lane < HD
     outs = []
@@ -675,18 +737,46 @@
     length = tok.shape[1]
     mine = pl.ds(pl.multiple_of(ROWS * c, ROWS), ROWS)
     slots = iter(range(local.shape[0]))
+    depth, units = norm1.shape[1], hidden.shape[1]
+    pairs = att.shape[1] // 128
 
     def load(src, dst):
         copy = pltpu.make_async_copy(src, dst, local.at[next(slots)])
         copy.start()
         return copy
 
+    def load_parts(parts, whole):
+        slot = local.at[next(slots)]
+        for src, dst in parts:
+            pltpu.make_async_copy(src, dst, slot).start()
+        return pltpu.make_async_copy(whole, whole, slot)
+
+    def qkv_parts(core):
+        return [
+            (
+                wqkv_ref.at[:, pl.ds(pl.multiple_of(third_of(i, t, core, depth), 128), 128)],
+                w_qkv.at[own, mine, pl.ds(third_at(i, t), 128)],
+            )
+            for i in range(pairs)
+            for t in range(3)
+        ]
+
+    def in_parts(core):
+        return [
+            (
+                win_ref.at[:, pl.ds(pl.multiple_of((2 * j + core) * 128, 128), 128)],
+                w_in.at[own, mine, pl.ds(128 * j, 128)],
+            )
+            for j in range(units // 128)
+        ]
+
+    whole_qkv, whole_in = w_qkv.at[own, mine], w_in.at[own, mine]
     loads = [
-        load(wqkv_ref.at[c], w_qkv.at[own, mine]),
+        load(tile_ref, tile),
+        load_parts(qkv_parts(c), whole_qkv),
         load(wout_ref, w_nat.at[own]),
-        load(win_ref.at[c], w_in.at[own, mine]),
+        load_parts(in_parts(c), whole_in),
         load(wdown_ref, w_down.at[own]),
-        load(tile_ref, tile),
         load(tok_ref, tok.at[c]),
         load(cot_ref, cot.at[c]),
         load(col_ref, col.at[c]),
@@ -694,46 +784,42 @@
     ]
     p.greet()
     pair = Pair(p, pair_sent, pair_came)
-    swaps = [
-        pair.copy(tile_ref, tile_in, 0),
-        pair.copy(wqkv_ref.at[1 - c], w_qkv.at[own, mine], 1),
-        pair.copy(win_ref.at[1 - c], w_in.at[own, mine], 2),
-        pair.copy(row_ref, row.at[c], 3),
-        pair.copy(col_ref, col.at[c], 4),
-        pair.copy(tok_ref, tok.at[c], 5),
-        pair.copy(cot_ref, cot.at[c], 6),
-    ]
-    for copy in swaps:
-        copy.start()
-    g_qkv, g_out, g_in, g_down, g_vec = (
+    swaps = [pair.copy(tile_ref, tile_in, 0)]
+    swaps[0].start()
+    for slot, parts, whole in ((1, qkv_parts(1 - c), whole_qkv), (2, in_parts(1 - c), whole_in)):
+        for src, dst in parts:
+            pair.copy(src, dst, slot).start()
+        swaps.append(pair.copy(whole, whole, slot))
+    for slot, src, dst in (
+        (3, row_ref, row.at[c]), (4, col_ref, col.at[c]), (5, tok_ref, tok.at[c]), (6, cot_ref, cot.at[c])
+    ):
+        swaps.append(pair.copy(src, dst, slot))
+        swaps[-1].start()
+    g_vec, g_qkv, g_out, g_in, g_down = (
         Gather(p, blocks, sent.at[i], came.at[i])
-        for i, blocks in enumerate((w_qkv, w_nat, w_in, w_down, tiles))
-    )
+        for i, blocks in enumerate((tiles, w_qkv, w_nat, w_in, w_down.at[:, :, 0:LINE_FROM]))
+    )
+    g_last = PlaneFirstGather(p, w_down.at[:, :, LINE_FROM:], sent.at[5], came.at[5])
     loads[0].wait()
-    swaps[1].wait_recv()
-    g_qkv.begin()
-    loads[4].wait()
     swaps[0].wait_recv()
     tiles[own, 0:8, :] = tile[0:8, :] + tile_in[0:8, :]
     tiles[own, 8:16, :] = tile[8:16, :]
     g_vec.begin()
-    loads[1].wait()
-    g_out.begin()
-    loads[2].wait()
-    swaps[2].wait_recv()
-    g_in.begin()
-    loads[3].wait()
+    for g, load_of, swap_of in ((g_qkv, 1, 1), (g_out, 2, None), (g_in, 3, 2)):
+        loads[load_of].wait()
+        if swap_of is not None:
+            swaps[swap_of].wait_recv()
+        g.begin()
+    run(g_vec.alongs(1, 2, 3), g_qkv.acrosses(0), g_qkv.alongs(1, 2, 3))
+    loads[4].wait()
     g_down.begin()
-    pump = Pump()
-    for g in (g_vec, g_qkv, g_out, g_in, g_down):
-        pump.add(g.steps())
+    g_last.begin()
+    run(g_vec.acrosses(0, 1, 2, 3), g_vec.finish)
     for i in (7, 8, 5):
         loads[i].wait()
     for i in (3, 4, 5):
         swaps[i].wait_recv()
     build_mask(mask, col, row)
-    pump.take(7)
-    g_vec.finish()
     build_vectors(vecs, hshift, tshift, tiles, c)
     tokens = tok.shape[0] * length
 
@@ -743,21 +829,27 @@
         normed, _ = stats(v)
         norm1[rows, :] = (normed * vecs[G1 : G1 + 1, :] + vecs[B1 : B1 + 1, :]).astype(BF)
 
-    pump.loop(tokens // 128, first_norm, 0)
-    pump.take(7)
-    g_qkv.finish()
+    loop(tokens // 128, first_norm)
+    run(g_qkv.acrosses(1, 2, 3), g_out.acrosses(0), g_out.alongs(1, 2, 3), g_in.acrosses(0), g_qkv.finish)
     stores = [load(w_qkv, qkv_o), load(norm1, norm1_o), load(vecs, vecs_o), load(mask, mask_o)]
-    depth = norm1.shape[1]
 
     def project(i):
         cols = span(i, 256)
         w = w_qkv[:, :, cols].reshape(depth, 256)
         triple[:, cols] = (mm(norm1[...], w) + tshift[0:1, cols]).astype(BF)
 
-    pump.loop(triple.shape[1] // 256, project, 1)
+    last = g_last.steps()
+    loop(triple.shape[1] // 256, project, {1: g_in.alongs(1), 3: last[0], 4: last[1], 5: last[2]})
     stores.append(load(triple, triple_o))
     lse[...] = jnp.zeros_like(lse)
-    pump.loop(8, functools.partial(attend_pair, triple=triple, mask=mask, attended=att, lse=lse), 1)
+    loop(
+        8,
+        functools.partial(attend_pair, triple=triple, mask=mask, attended=att, lse=lse),
+        {
+            0: g_out.acrosses(1), 1: g_out.acrosses(2), 2: g_out.acrosses(3), 3: g_in.alongs(2), 5: g_in.alongs(3),
+            7: g_in.acrosses(1),
+        },
+    )
     stores.append(load(att, att_o))
     g_out.finish()
     half = pair.copy(w_nat.at[pl.ds(8 * (1 - c), 8)], w_out.at[:, mine], 7)
@@ -779,7 +871,7 @@
         v = tok[i // 2, span(lax.rem(i, 2), 256), :].astype(F32)
         mid[rows, :] = v + own_part + vecs[OB : OB + 1, :]
 
-    pump.loop(4, mix, 0)
+    loop(4, mix)
 
     def second_norm(i):
         send_part(i).wait_recv()
@@ -793,10 +885,9 @@
         lse[i // 2, inside, :] = jnp.where(lane < INV_AT, lse[i // 2, inside, :], inverse)
         norm2[rows, :] = (normed * vecs[G2 : G2 + 1, :] + vecs[B2 : B2 + 1, :]).astype(BF)
 
-    pump.loop(4, second_norm, 0)
+    loop(4, second_norm)
     stores += [load(xhat, xhat_o), load(lse, lse_o), load(norm2, norm2_o), load(mid.at[span(c, length)], mid_o)]
-    pump.take(max(len(pump.queue) - 4, 0))
-    g_in.finish()
+    run(g_in.acrosses(2, 3), g_down.acrosses(0), g_down.alongs(1), g_in.finish)
     stores.append(load(w_in, in_o))
 
     def expand(i):
@@ -810,7 +901,7 @@
     loads[6].wait()
     swaps[6].wait_recv()
     stores.append(load(cot, cot_o))
-    pump.loop(hidden.shape[1] // 256, expand, 0)
+    loop(units // 256, expand, {2: g_down.alongs(2), 4: g_down.alongs(3)})
     stores += [load(slope, slope_o), load(hidden, hidden_o)]
 
     def down_grad(i):
@@ -818,14 +909,13 @@
         grad = mm(hidden[:, cols], cot[...].reshape(tokens, depth), TN).astype(BF)
         gdown[pl.ds(pl.multiple_of(2 * i, 2), 2)] = grad.reshape(2, 128, depth)
 
-    pump.loop(hidden.shape[1] // 256, down_grad, 1)
+    loop(units // 256, down_grad, {1: g_down.acrosses(1), 4: g_down.acrosses(2), 7: g_down.acrosses(3)})
     stores.append(load(gdown, gdown_o))
-    pump.take(len(pump.queue))
-    g_down.finish()
+    run(g_down.finish, g_last.finish)
     stores.append(load(w_down, down_o))
     for i in range(4):
         send_part(i).wait_send()
-    for g in (g_vec, g_qkv, g_out, g_in, g_down):
+    for g in (g_vec, g_qkv, g_out, g_in, g_down, g_last):
         g.drain()
     for copy in swaps:
         copy.wait_send()
@@ -834,8 +924,8 @@
         store.wait()
 
 
-def forward_all(wqkv2, w_out, win2, w_down, tile, inputs, cotangent, col, row):
-    dq, do, di = wqkv2.shape[2], w_out.shape[1], win2.shape[2]
+def forward_all(w_qkv, w_out, w_in, w_down, tile, inputs, cotangent, col, row):
+    dq, do, di = w_qkv.shape[1] // 2, w_out.shape[1], w_in.shape[1] // 2
     length, depth = inputs.shape
     tokens = 2 * length
     outs = [
@@ -861,8 +951,8 @@
         out_specs=[pl.BlockSpec(memory_space=pl.ANY)] * len(outs),
         scratch_shapes=[pltpu.VMEM(s, d) for s, d in scratch]
         + [
-            pltpu.SemaphoreType.DMA((5, 15)),
-            pltpu.SemaphoreType.DMA((5, 15)),
+            pltpu.SemaphoreType.DMA((6, 15)),
+            pltpu.SemaphoreType.DMA((6, 15)),
             pltpu.SemaphoreType.DMA((12,)),
             pltpu.SemaphoreType.DMA((12,)),
             pltpu.SemaphoreType.DMA((32,)),
@@ -871,21 +961,20 @@
             collective_id=0, has_side_effects=True, vmem_limit_bytes=67043328
         ),
         name="forward_gather",
-    )(wqkv2, w_out, win2, w_down, tile, inputs, cotangent, col, row)
+    )(w_qkv, w_out, w_in, w_down, tile, inputs, cotangent, col, row)
 
 
 def attend_pair_back(i, triple, mask, lse, gatt, gtriple, sums, c):
     length = mask.shape[1]
     half = gatt.shape[1]
-    pairs = half // 128
-    s, pair = i // pairs, lax.rem(i, pairs)
+    pair, s = i // 2, lax.rem(i, 2)
     rows, blocks = span(s, length), span(s, length // 64)
 
     def at(third):
-        return pl.ds(pl.multiple_of(third * half + pair * 128, 128), 128)
+        return pl.ds(pl.multiple_of(third_at(pair, third), 128), 128)
 
     q, k, v = (triple[blocks, :, at(t)].reshape(length, 128) for t in range(3))
-    g = gatt[rows, at(0)]
+    g = gatt[rows, span(pair, 128)]
     lane = lax.broadcasted_iota(jnp.int32, (length, 128), 1)
     low = lane < HD
     zero = jnp.zeros_like(q)
@@ -958,13 +1047,20 @@
     fourth = [load(mask_ref, mask), load(qkv_ref, w_qkv)]
     p.greet()
     pair = Pair(p, pair_sent, pair_came)
-    s_down, s_in, s_out, s_qkv, s_vec = (
-        Scatter(p, blocks, landed, sent.at[i], came.at[i])
-        for i, (blocks, landed) in enumerate(
-            ((b_down, l_down), (b_in, l_in), (b_out, l_out), (b_qkv, l_qkv), (b_vec, l_vec))
-        )
-    )
+    trees = [
+        (b_down.at[:, :, 0:LINE_FROM], l_down.at[:, :, 0:LINE_FROM]),
+        (b_in, l_in),
+        (b_out, l_out),
+        (b_vec, l_vec),
+    ]
+    cuts = [(0, 768), (768, 1152), (1152, 1536)]
+    trees += [(b_qkv.at[:, :, low:high], l_qkv.at[:, :, low:high]) for low, high in cuts]
+    every = [Scatter(p, blocks, landed, sent.at[i], came.at[i]) for i, (blocks, landed) in enumerate(trees)]
+    s_down, s_in, s_out, s_vec, *s_qkv = every
+    s_line = LineFirstScatter(p, b_down.at[:, :, LINE_FROM:], l_down.at[:, :, LINE_FROM:], sent.at[7], came.at[7])
+    every.append(s_line)
     in_down.wait()
+    s_line.begin()
     s_down.begin()
     stores = []
 
@@ -975,29 +1071,47 @@
         return write
 
     def end_down():
-        s_down.total(put(f_down))
+        s_down.total(put(f_down.at[:, 0:LINE_FROM]))
+        s_line.total(put(f_down.at[:, LINE_FROM:]))
         stores.append(load(f_down, down_o))
+
+    def parts_out(ref, out, places, slot):
+        here = next(slots)
+        for at, place in places:
+            to = out.at[:, pl.ds(pl.multiple_of(place, 128), 128)]
+            pltpu.make_async_copy(ref.at[mine, pl.ds(at, 128)], to, local.at[here]).start()
+            pair.copy(ref.at[theirs, pl.ds(at, 128)], to, slot).start()
+        size = 128 * len(places)
+
+        def wait():
+            low = places[0][0]
+            some = ref.at[mine, pl.ds(low, size)]
+            pltpu.make_async_copy(some, some, local.at[here]).wait()
+            pair.copy(some, some, slot).wait()
+
+        stores.append(Later(wait))
 
     def end_in():
         s_in.total(put(f_in))
-        pair.copy(f_in.at[theirs], in_o.at[c], 1).start()
-        stores.append(load(f_in.at[mine], in_o.at[c]))
+        parts_out(f_in, in_o, [(128 * j, (2 * j + c) * 128) for j in range(units // 128)], 1)
 
     def end_out():
         s_out.total(put(f_out))
         stores.append(load(f_out, out_o))
 
-    def end_qkv():
-        s_qkv.total(put(f_qkv))
-        pair.copy(f_qkv.at[theirs], qkv_o.at[c], 2).start()
-        stores.append(load(f_qkv.at[mine], qkv_o.at[c]))
+    def end_qkv(n):
+        low, high = cuts[n]
+        s_qkv[n].total(put(f_qkv.at[:, low:high]))
+        places = [
+            (third_at(i, t), third_of(i, t, c, depth)) for i in range(low // 384, high // 384) for t in range(3)
+        ]
+        parts_out(f_qkv, qkv_o, places, 10 + n)
 
     def end_vec():
         s_vec.total(put(f_vec))
         pair.copy(f_vec, n_vec, 9).start()
         stores.append(load(f_vec, vec_o.at[0]))
 
-    pump = Pump()
     sums[...] = jnp.zeros_like(sums)
     b_vec[...] = jnp.zeros_like(b_vec)
     for copy in first:
@@ -1012,7 +1126,7 @@
         cols = span(i, 256)
         xhat[length:tokens, cols] = contract(yours, cols).astype(BF)
 
-    pump.loop(depth // 256, out_theirs, 0)
+    loop(depth // 256, out_theirs)
     rest = pair.copy(xhat.at[length:tokens], xhat.at[0:length], 3)
     rest.start()
 
@@ -1020,7 +1134,7 @@
         cols = span(i, 256)
         gmid[:, cols] = gmid[:, cols] + contract(ours, cols) + vecs[DB : DB + 1, cols]
 
-    pump.loop(depth // 256, out_ours, 0)
+    loop(depth // 256, out_ours)
     for copy in second:
         copy.wait()
 
@@ -1034,16 +1148,15 @@
         b_vec[2 * i, 8:9, :] = total[:, 0:128]
         b_vec[2 * i + 1, 8:9, :] = total[:, 128:256]
 
-    pump.loop(units // 256, hidden_grad, 0)
+    loop(units // 256, hidden_grad)
 
     def in_grad(i):
         cols = span(i, 256)
         b_in[span(i, 4)] = mm(norm2[:, cols], wide[...], TN).astype(BF).reshape(4, 64, units)
 
-    pump.loop(depth // 256, in_grad, 0)
-    pump.add(s_down.acrosses())
-    pump.take(4)
-    s_in.begin()
+    loop(depth // 256, in_grad)
+    line = s_line.steps()
+    run(s_down.acrosses(), s_in.begin, line[0])
     rest.wait_recv()
     gmid[...] = gmid[...] + xhat[0:length, :].astype(F32)
     layer = load(gmid, layer_o)
@@ -1059,7 +1172,8 @@
         part[rows, :] = mm(wide[rows, :], area2[...].reshape(depth, units), NT).astype(BF)
         send_part(i).start()
 
-    pump.loop(4, norm_grad, 0)
+    loop(4, norm_grad)
+    run(s_down.alongs(), line[1])
     norm1_in = load(norm1_ref, area.at[0:8])
     tok_in = load(tok_ref, area.at[8:12])
     triple_in = load(triple_ref, area2.at[:, :, 0 : 3 * half])
@@ -1091,14 +1205,14 @@
     for i in range(4):
         send_part(i).wait_recv()
     layer.wait()
-    pump.loop(length // 128, functools.partial(middle_rows, ours=True), 0)
-    pump.loop(length // 128, functools.partial(middle_rows, ours=False), 0)
+    loop(length // 128, functools.partial(middle_rows, ours=True))
+    loop(length // 128, functools.partial(middle_rows, ours=False))
 
     def out_grad(i):
         cols = span(i, 256)
         gout[span(i, 4)] = mm(att[:, cols], gmixed[...], TN).astype(BF).reshape(4, 64, depth)
 
-    pump.loop(half // 256, out_grad, 0)
+    loop(half // 256, out_grad)
     keep = load(gout.at[:, mine], b_out.at[pl.ds(8 * c, 8)])
     mate = pair.copy(gout.at[:, theirs], b_out.at[pl.ds(8 * c, 8)], 0)
     mate.start()
@@ -1107,34 +1221,29 @@
         rows = span(i, 512)
         gatt[rows, :] = mm(gmixed[rows, :], w_out[...].reshape(half, depth), NT).astype(BF)
 
-    pump.loop(2, att_grad, 0)
+    loop(2, att_grad)
     keep.wait()
     mate.wait_recv()
-    pump.add(s_down.alongs())
-    pump.take(4)
-    s_out.begin()
-    pump.add(s_in.acrosses())
+    run(s_in.acrosses(3, 2), s_out.begin, line[2])
     triple_in.wait()
     for copy in fourth:
         copy.wait()
-    pump.loop(
-        8,
-        functools.partial(
-            attend_pair_back, triple=area2, mask=mask, lse=lse, gatt=gatt, gtriple=wide, sums=sums, c=c
-        ),
-        1,
+    attend_back = functools.partial(
+        attend_pair_back, triple=area2, mask=mask, lse=lse, gatt=gatt, gtriple=wide, sums=sums, c=c
     )
     norm1_in.wait()
 
-    def qkv_grad(i):
+    def qkv_grad(i, cut):
         cols = span(i, 256)
         normed = area[0:8, :, cols].reshape(tokens, 256)
-        b_qkv[span(i, 4)] = mm(normed, wide[:, 0 : 3 * half], TN).astype(BF).reshape(4, 64, 3 * half)
-
-    pump.loop(depth // 256, qkv_grad, 0)
-    s_qkv.begin()
-    pump.add([end_down])
-    pump.add(s_out.acrosses())
+        grad = mm(normed, wide[:, 768 * cut : 768 * (cut + 1)], TN).astype(BF)
+        b_qkv[span(i, 4), :, 768 * cut : 768 * (cut + 1)] = grad.reshape(4, 64, 768)
+
+    loop(4, attend_back, {0: s_in.acrosses(1), 1: s_in.acrosses(0)})
+    loop(depth // 256, functools.partial(qkv_grad, cut=0))
+    run(s_qkv[0].begin)
+    loop(4, lambda i: attend_back(i + 4), {0: s_in.alongs(3), 1: s_in.alongs(2), 2: s_in.alongs(1), 3: s_in.alongs(0)})
+    run(s_out.acrosses())
     for i in range(4):
         send_part(i).wait_send()
 
@@ -1145,9 +1254,11 @@
     def first_theirs(i):
         part[span(i, 128), :] = input_grad(i, 1 - c).astype(BF)
 
-    pump.loop(length // 128, first_theirs, 0)
+    loop(length // 128, first_theirs)
     last = pair.copy(part.at[0:length], part_in.at[0:length], 8)
     last.start()
+    loop(depth // 256, functools.partial(qkv_grad, cut=1))
+    run(s_qkv[1].begin)
     tok_in.wait()
 
     def first_ours(i):
@@ -1164,27 +1275,24 @@
         sums[B1 : B1 + 1, :] += jnp.sum(grad, 0, keepdims=True)
 
     last.wait_recv()
-    pump.loop(length // 128, first_ours, 0)
+    loop(length // 128, first_ours)
     stores.append(load(gmid, input_o))
     for w in range(8):
         for k in range(2):
             b_vec[2 * w + k, 0:8, :] = sums[:, 128 * w : 128 * (w + 1)]
-    s_vec.begin()
-    for steps in (
-        s_in.alongs(), s_qkv.acrosses(), s_vec.acrosses(), s_out.alongs(), [end_in, end_out], s_vec.alongs(),
-        s_qkv.alongs(), [end_vec, end_qkv],
-    ):
-        pump.add(steps)
-    pump.take(len(pump.queue))
+    run(
+        s_vec.begin, s_qkv[2].begin, s_qkv[0].acrosses(), end_down, s_out.alongs(), end_in, s_qkv[0].alongs(),
+        s_qkv[1].acrosses(), s_vec.acrosses(), s_qkv[2].acrosses(), end_out, s_qkv[1].alongs(), s_vec.alongs(),
+        s_qkv[2].alongs(), functools.partial(end_qkv, 0), functools.partial(end_qkv, 1), end_vec,
+        functools.partial(end_qkv, 2),
+    )
     pair.copy(f_vec, n_vec, 9).wait_recv()
     stores.append(load(n_vec, vec_o.at[1]))
-    for s in (s_down, s_in, s_out, s_qkv, s_vec):
+    for s in every:
         s.drain()
     mate.wait_send()
     last.wait_send()
     pair.copy(f_vec, n_vec, 9).wait_send()
-    pair.copy(f_in.at[theirs], in_o.at[c], 1).wait()
-    pair.copy(f_qkv.at[theirs], qkv_o.at[c], 2).wait()
     for store in stores:
         store.wait()
 
@@ -1198,7 +1306,7 @@
     dq, do, di = qkv.shape[2], w_out.shape[2], w_in.shape[2]
     down, dd = w_down.shape[1:]
     outs = [
-        ((2, 32, dq), F32), ((32, do), F32), ((2, 32, di), F32), ((down, dd), F32), ((2, 16, 128), F32),
+        ((32, 2 * dq), F32), ((32, do), F32), ((32, 2 * di), F32), ((down, dd), F32), ((2, 16, 128), F32),
         ((length, depth), F32), ((length, depth), F32),
     ]
     blocks = [((64, dq), BF), ((32, do), BF), ((64, di), BF), ((down, dd), BF), ((16, 128), F32)]
@@ -1220,10 +1328,10 @@
         out_specs=[pl.BlockSpec(memory_space=pl.ANY)] * len(outs),
         scratch_shapes=[pltpu.VMEM(s, d) for s, d in scratch]
         + [
-            pltpu.SemaphoreType.DMA((5, 15)),
-            pltpu.SemaphoreType.DMA((5, 15)),
-            pltpu.SemaphoreType.DMA((10,)),
-            pltpu.SemaphoreType.DMA((10,)),
+            pltpu.SemaphoreType.DMA((8, 15)),
+            pltpu.SemaphoreType.DMA((8, 15)),
+            pltpu.SemaphoreType.DMA((13,)),
+            pltpu.SemaphoreType.DMA((13,)),
             pltpu.SemaphoreType.DMA((32,)),
         ],
         compiler_params=pltpu.CompilerParams(
@@ -1239,22 +1347,16 @@
     c = lax.axis_index("c")
     narrow = lax.axis_index("x") * 2 + c
     length, d_model = inputs.shape
-    rows = ln1_gain.shape[0]
-    half = d_model // 2
     small = jnp.stack(
         [ln1_gain, ln1_shift, query_bias, value_bias, out_bias, ln2_gain, ln2_shift, down_bias]
     ).astype(F32)
     quarter = jnp.arange(4)[None, :, None] == narrow
     tile = jnp.where(quarter, small[:, None, :], 0.0).reshape(8, 128)
     tile = jnp.concatenate([tile, in_bias.astype(F32)[None], jnp.zeros((7, 128), F32)])
-    wqkv2 = w_qkv.reshape(rows, 3, 2, half).transpose(2, 0, 1, 3).reshape(2, rows, -1)
-    win2 = w_in.reshape(rows, 16, 2, 128).transpose(2, 0, 1, 3).reshape(2, rows, -1)
     col = jnp.broadcast_to(segment_ids[:, None], (length, 128))
     row = jnp.broadcast_to(segment_ids[None, :], (8, length))
-    saved = forward_all(wqkv2, w_out, win2, w_down, tile, inputs, cotangent, col, row)
+    saved = forward_all(w_qkv, w_out, w_in, w_down, tile, inputs, cotangent, col, row)
     d_qkv, d_out, d_in, d_down, d_vec, grad_input, layer_out = backward_all(saved, inputs)
-    d_qkv = d_qkv.reshape(2, rows, 3, half).transpose(1, 2, 0, 3).reshape(rows, -1)
-    d_in = d_in.reshape(2, rows, 16, 128).transpose(1, 2, 0, 3).reshape(rows, -1)
     eight = (d_vec[0, :8] + d_vec[1, :8]).reshape(8, 4, 32)
     eight = lax.dynamic_index_in_dim(eight, narrow, 1, False)
     return (

time: 281 us -> 267 us (0.950)
  Pallas kernels: 261 us -> 250 us
  local copies, waits for them, and re-layouts: 17.4 us -> 13.4 us
    pallas_call x1, Pallas kernels: 133 us -> 124 us  [backward_all(): pl.pallas_call(backward_kernel, out_shape=[jax.ShapeDtypeStruct(s, d) for...]
    reshape x9 -> x0, local copies, waits for them, and re-layouts: 6.67 us -> none  [the longest x3 2.12 us: local_split(): w_qkv.reshape(rows, 3, 2, half).transpose(2, 0, 1, 3).reshape(2, rows, -1)]
    unnamed x19 -> x16, local copies, waits for them, and re-layouts: 6.33 us -> 7.63 us
where the time goes in v5:
time: 267 us; the launch traced here: 266 us
  Pallas kernels  250 us (94%)
  local copies, waits for them, and re-layouts  13.4 us (5%)
    pallas_call x1, Pallas kernels, forward_all(): pl.pallas_call(forward_kernel, out_shape=[jax.ShapeDtypeStruct(s, d) for...  126 us
    pallas_call x1, Pallas kernels, backward_all(): pl.pallas_call(backward_kernel, out_shape=[jax.ShapeDtypeStruct(s, d) for...  124 us
    unnamed x16, local copies, waits for them, and re-layouts  7.63 us

profile of v5, /device:TPU:0, one launch (start us, length us, event | category | flops | bytes accessed | tf_op | source)
XLA Modules:
  0.0 266.2 jit_solution(18316782167709423519)
XLA Ops:
  0.7 0.1 broadcast_in_dim.49
  0.7 0.1 broadcast_in_dim.50
  0.8 0.8 stack.35
  1.6 0.1 broadcast_in_dim.53
  1.7 0.1 pad.2.clone
  1.8 0.7 bitcast_convert_fusion
  2.5 0.7 maximum_maximum_fusion.tile_ref
  3.1 1.5 broadcast_in_dim.58.col_ref
  4.6 1.3 broadcast_in_dim.59.row_ref
  5.9 126.4 %forward_gather.1 = (bf16[16,64,1536]{2,1,0:T(8,128)(2,1)}, bf16[8,64,1024]{2,1,0:T(8,128)(2,1)}, bf16[16,64,2048]{2,1,0:T(8,128)(2,1)}, bf16[16,128,1024]{2,1,0...) custom-call(bf16[32,3072]{1,0:T(8,128)(2,1)} %wqkv_ref.1, ...), custom_call_target="tpu_custom_call" | custom-call | tf_op jit(solution)/shard_map/forward_gather/pallas_call | solution.py:947
  132.4 123.6 %backward_scatter.1 = (f32[32,3072]{1,0:T(8,128)}, f32[32,1024]{1,0:T(8,128)}, f32[32,4096]{1,0:T(8,128)}, f32[128,1024]{1,0:T(8,128)}, f32[2,16,128]{2,1,0:T(8,...) custom-call(bf16[16,64,1536]{2,1,0:T(8,128)(2,1)} %get-tuple-element.39.qkv_ref, ...), custom_call_target="tpu_custom_call" | custom-call | tf_op jit(solution)/shard_map/backward_scatter/pallas_call | solution.py:1324
  256.0 0.7 slice_add_fusion
  256.7 0.1 add.16
  256.8 0.5 fusion
  257.4 1.2 slice_bitcast_fusion
  258.5 0.0 copy-start
  258.5 3.3 %copy.37 = f32[512,1024]{1,0:T(8,128)} copy(f32[512,1024]{1,0:T(8,128)} %get-tuple-element.86) | data formatting | bytes 4194304
  261.9 0.0 copy-done
  261.9 0.0 copy-start.3
  261.9 0.0 copy-start.4
  261.9 0.0 copy-start.2
  261.9 1.3 copy.38
  263.2 0.0 copy-done.3
  263.2 0.0 copy-start.1
  263.2 0.7 copy.39
  263.9 0.0 copy-done.4
  263.9 0.7 copy.40
  264.6 0.0 copy-done.2
  264.6 0.8 copy.41
  265.4 0.0 copy-done.1
  265.4 0.8 copy.42
  (4 shorter events, 0.0 us)
Async XLA Ops:
  258.5 3.3 %copy-start = (f32[512,1024]{1,0:T(8,128)S(1)}, f32[512,1024]{1,0:T(8,128)}, u32[]{:S(2)}) copy-start(f32[512,1024]{1,0:T(8,128)} %get-tuple-element.87) | copy-start | bytes 6291460
  261.9 1.3 copy-start.3
  261.9 2.1 copy-start.4
  261.9 2.7 %copy-start.2 = (f32[32,4096]{1,0:T(8,128)S(1)}, f32[32,4096]{1,0:T(8,128)}, u32[]{:S(2)}) copy-start(f32[32,4096]{1,0:T(8,128)} %get-tuple-element.97) | copy-start | bytes 1572868
  263.2 2.2 copy-start.1
